TPU v7x, 32 devices: a whole 2x2x4 slice. The times are simulated.
32 devices in a mesh: fsdp: 4 (over x, core), ctx: 2 (over y), tp: 4 (over z).
Axes of the slice: x: 2, y: 2, z: 4, core: 2. Of those that a mesh axis runs over, the one named last changes fastest.
Arguments:
- tokens: bfloat16 [4, 1024, 768], P('fsdp', 'ctx'), may hold values from -6 to 6
- parents: int32 [4, 2], P('fsdp'), may hold values from 0 to 0, as said below
- routes: int32 [4, 1024, 2], P('fsdp', 'ctx'), may hold values from 0 to 7, all different within a row; in each aligned block of 512 rows (0 to 511, 512 to 1023, ..., all dimensions but the last counted through in order) at most 192 rows name the same one
- gates: float32 [4, 1024, 2], P('fsdp', 'ctx'), may hold values from 0.2 to 1
- attn_gain: bfloat16 [2, 768], P(None, 'fsdp'), may hold values from 0.5 to 1.5
- ffn_gain: bfloat16 [2, 768], P(None, 'fsdp'), may hold values from 0.5 to 1.5
- qkv_weight: bfloat16 [2, 768, 3, 768], P(None, 'fsdp', None, 'tp'), may hold values from -0.21875 to 0.21875
- out_weight: bfloat16 [2, 768, 768], P(None, 'tp', 'fsdp'), may hold values from -0.875 to 0.875
- shared_in: bfloat16 [2, 768, 2, 2048], P(None, 'fsdp', None, 'tp'), may hold values from -0.21875 to 0.21875
- shared_out: bfloat16 [2, 2048, 768], P(None, 'tp', 'fsdp'), may hold values from -0.125 to 0.125
- expert_in: bfloat16 [2, 8, 768, 2, 2048], P(None, None, 'fsdp', None, 'tp'), may hold values from -0.21875 to 0.21875
- expert_out: bfloat16 [2, 8, 2048, 768], P(None, None, 'tp', 'fsdp'), may hold values from -0.125 to 0.125
- cotangent: bfloat16 [4, 1024, 768], P('fsdp', 'ctx'), may hold values from -6 to 6
Outputs:
- result: bfloat16 [4, 1024, 768], P('fsdp', 'ctx')
- tokens_grad: float32 [4, 1024, 768], P('fsdp', 'ctx')
- attn_gain_grad: float32 [2, 768], P(None, 'fsdp')
- ffn_gain_grad: float32 [2, 768], P(None, 'fsdp')
- qkv_grad: float32 [2, 768, 3, 768], P(None, 'fsdp', None, 'tp')
- out_grad: float32 [2, 768, 768], P(None, 'tp', 'fsdp')
- shared_in_grad: float32 [2, 768, 2, 2048], P(None, 'fsdp', None, 'tp')
- shared_out_grad: float32 [2, 2048, 768], P(None, 'tp', 'fsdp')
- expert_in_grad: float32 [2, 8, 768, 2, 2048], P(None, None, 'fsdp', None, 'tp')
- expert_out_grad: float32 [2, 8, 2048, 768], P(None, None, 'tp', 'fsdp')
Inputs may be any that keep to these rules, and one draw needn't show every extreme that they name: parents[g, 0] = 0 marks the root segment; for every segment b >= 1, parents[g, b] < b; the last segment's parent is segment 2 - 2. `routes`: each token names 2 distinct experts; among the 512 rows of one device no expert is named more than 192 times.
All inputs are finite; a program needn't handle non-finite values.
Results may differ from a plain program's by a relative error of at most 0.039.
Values may be sent and summed in bfloat16 or wider, within the bound.
No kernel may reach another device: no remote copies, remote signals or barrier semaphores. Data moves between devices by JAX's collectives and lax.ppermute only.
A program may use at most 320 MiB of HBM per device.

v0:
```python
import jax
import jax.numpy as jnp
from jax import lax
from jax.sharding import PartitionSpec as P

HEAD_DIM = 64


EPS = 1e-06
SCALE = 0.125
MASKED = -1000000000.0


def silu_parts(gate):
    sigmoid = jax.nn.sigmoid(gate)
    return (gate * sigmoid, sigmoid * (1.0 + gate * (1.0 - sigmoid)))


def norm_forward(values, gain):
    inverse = lax.rsqrt(jnp.mean(values * values, axis=-1, keepdims=True) + EPS)
    scaled = values * inverse
    return (scaled * gain, scaled, inverse)


def norm_backward(d_normed, scaled, inverse, gain):
    d_scaled = d_normed * gain
    d_values = inverse * (d_scaled - scaled * jnp.mean(d_scaled * scaled, axis=-1, keepdims=True))
    return (d_values, jnp.sum(d_normed * scaled, axis=0))


def ancestry(parent_row):
    count = parent_row.shape[0]
    block_ids = jnp.arange(count, dtype=jnp.int32)
    step_map = ((parent_row[:, None] == block_ids[None, :]) & (block_ids[:, None] > 0)).astype(
        jnp.float32
    )
    identity = jnp.eye(count, dtype=jnp.float32)

    def climb(index, state):
        reach_now, on_path = state
        reach_now = jnp.dot(reach_now, step_map, precision=lax.Precision.HIGHEST)
        return (reach_now, on_path + reach_now)

    return lax.fori_loop(0, count, climb, (identity, identity))[1]


def allowed_keys(anc_row, start, block, tree_len):
    key_pos = jnp.arange(tree_len, dtype=jnp.int32)
    query_pos = start + jnp.arange(block, dtype=jnp.int32)
    on_path = jnp.repeat(anc_row, block)[None, :] > 0.5
    return on_path & (key_pos[None, :] <= query_pos[:, None])


def slot_maps(route_rows, gate_rows, experts, capacity):
    flat_routes = route_rows.reshape(-1)
    one_hot = (flat_routes[:, None] == jnp.arange(experts, dtype=jnp.int32)[None, :]).astype(
        jnp.int32
    )
    earlier = jnp.cumsum(one_hot, axis=0) - one_hot
    placed = flat_routes * capacity + jnp.sum(earlier * one_hot, axis=1)
    owners = jnp.arange(flat_routes.shape[0], dtype=jnp.int32) // route_rows.shape[1]
    slot_owner = jnp.zeros((experts * capacity,), jnp.int32).at[placed].set(owners)
    slot_gate = jnp.zeros((experts * capacity,), jnp.float32).at[placed].set(gate_rows.reshape(-1))
    slot_live = jnp.zeros((experts * capacity,), jnp.bool_).at[placed].set(True)
    return (placed.reshape(route_rows.shape), slot_owner, slot_gate, slot_live)


def fetch(gain_a, gain_b, qkv_w, out_w, sh_in, sh_out, ex_in, ex_out):
    return (
        lax.all_gather(gain_a, "fsdp", axis=0, tiled=True),
        lax.all_gather(gain_b, "fsdp", axis=0, tiled=True),
        lax.all_gather(qkv_w, "fsdp", axis=0, tiled=True),
        lax.all_gather(out_w, "fsdp", axis=1, tiled=True),
        lax.all_gather(sh_in, "fsdp", axis=0, tiled=True),
        lax.all_gather(sh_out, "fsdp", axis=1, tiled=True),
        lax.all_gather(ex_in, "fsdp", axis=1, tiled=True),
        lax.all_gather(ex_out, "fsdp", axis=2, tiled=True),
    )


def fetch_again(gain_a, gain_b, qkv_w, out_w, sh_in, sh_out, ex_in, ex_out):
    return (
        lax.all_gather(gain_a, "fsdp", axis=0, tiled=True),
        lax.all_gather(gain_b, "fsdp", axis=0, tiled=True),
        lax.all_gather(qkv_w, "fsdp", axis=0, tiled=True),
        lax.all_gather(out_w, "fsdp", axis=1, tiled=True),
        lax.all_gather(sh_in, "fsdp", axis=0, tiled=True),
        lax.all_gather(sh_out, "fsdp", axis=1, tiled=True),
        lax.all_gather(ex_in, "fsdp", axis=1, tiled=True),
        lax.all_gather(ex_out, "fsdp", axis=2, tiled=True),
    )


def head_total(values):
    return lax.psum(values.astype(jnp.bfloat16), "tp").astype(jnp.float32)


def settle(g_gain_a, g_gain_b, g_qkv, g_out, g_shin, g_shout, g_exin, g_exout):
    shares = (
        lax.psum_scatter(
            g_gain_a.astype(jnp.bfloat16), "fsdp", scatter_dimension=0, tiled=True
        ).astype(jnp.float32),
        lax.psum_scatter(
            g_gain_b.astype(jnp.bfloat16), "fsdp", scatter_dimension=0, tiled=True
        ).astype(jnp.float32),
        lax.psum_scatter(
            g_qkv.astype(jnp.bfloat16), "fsdp", scatter_dimension=0, tiled=True
        ).astype(jnp.float32),
        lax.psum_scatter(
            g_out.astype(jnp.bfloat16), "fsdp", scatter_dimension=1, tiled=True
        ).astype(jnp.float32),
        lax.psum_scatter(
            g_shin.astype(jnp.bfloat16), "fsdp", scatter_dimension=0, tiled=True
        ).astype(jnp.float32),
        lax.psum_scatter(
            g_shout.astype(jnp.bfloat16), "fsdp", scatter_dimension=1, tiled=True
        ).astype(jnp.float32),
        lax.psum_scatter(
            g_exin.astype(jnp.bfloat16), "fsdp", scatter_dimension=1, tiled=True
        ).astype(jnp.float32),
        lax.psum_scatter(
            g_exout.astype(jnp.bfloat16), "fsdp", scatter_dimension=2, tiled=True
        ).astype(jnp.float32),
    )
    return (
        lax.psum(shares[0].astype(jnp.bfloat16), "ctx").astype(jnp.float32),
        lax.psum(shares[1].astype(jnp.bfloat16), "ctx").astype(jnp.float32),
        lax.psum(shares[2].astype(jnp.bfloat16), "ctx").astype(jnp.float32),
        lax.psum(shares[3].astype(jnp.bfloat16), "ctx").astype(jnp.float32),
        lax.psum(shares[4].astype(jnp.bfloat16), "ctx").astype(jnp.float32),
        lax.psum(shares[5].astype(jnp.bfloat16), "ctx").astype(jnp.float32),
        lax.psum(shares[6].astype(jnp.bfloat16), "ctx").astype(jnp.float32),
        lax.psum(shares[7].astype(jnp.bfloat16), "ctx").astype(jnp.float32),
    )


def shards(
    tokens,
    parents,
    routes,
    gates,
    attn_gain,
    ffn_gain,
    qkv_weight,
    out_weight,
    shared_in,
    shared_out,
    expert_in,
    expert_out,
    cotangent,
):
    f32 = jnp.float32
    bf16 = jnp.bfloat16
    rows_here = tokens.shape[1]
    width = tokens.shape[2]
    layers = qkv_weight.shape[0]
    experts = expert_in.shape[1]
    capacity = 3 * rows_here // 8
    tree_len = rows_here * lax.axis_size("ctx")
    ancestors = ancestry(parents[0])
    block = tree_len // ancestors.shape[0]
    local_blocks = rows_here // block
    anc_rows = lax.dynamic_slice_in_dim(
        ancestors, lax.axis_index("ctx") * local_blocks, local_blocks, 0
    )
    starts = lax.axis_index("ctx") * rows_here + jnp.arange(local_blocks, dtype=jnp.int32) * block
    slot_index, slot_owner, slot_gate, slot_live = slot_maps(routes[0], gates[0], experts, capacity)
    gate_rows = gates[0]
    stream = tokens[0].astype(f32)
    kept = []
    saved = []
    for layer_id in range(layers):
        weights = fetch(
            attn_gain[layer_id],
            ffn_gain[layer_id],
            qkv_weight[layer_id],
            out_weight[layer_id],
            shared_in[layer_id],
            shared_out[layer_id],
            expert_in[layer_id],
            expert_out[layer_id],
        )
        kept.append(None)
        normed, scaled_a, inverse_a = norm_forward(stream, weights[0].astype(f32))
        normed_b = normed.astype(bf16)
        qkv = jnp.einsum("td,dcf->tcf", normed_b, weights[2], preferred_element_type=f32).astype(
            bf16
        )
        heads_here = qkv.shape[2] // HEAD_DIM
        keys_all, values_all = (
            lax.all_gather(qkv[:, 1], "ctx", axis=0, tiled=True),
            lax.all_gather(qkv[:, 2], "ctx", axis=0, tiled=True),
        )
        keys_all = keys_all.reshape(tree_len, heads_here, HEAD_DIM)
        values_all = values_all.reshape(tree_len, heads_here, HEAD_DIM)
        queries = qkv[:, 0].reshape(local_blocks, block, heads_here, HEAD_DIM)

        def attend(inputs):
            query_block, anc_row, start = inputs
            allowed = allowed_keys(anc_row, start, block, tree_len)
            scores = (
                jnp.einsum("qhd,khd->hqk", query_block, keys_all, preferred_element_type=f32)
                * SCALE
            )
            scores = jnp.where(allowed[None], scores, MASKED)
            peak = jnp.max(scores, axis=-1, keepdims=True)
            expo = jnp.exp(scores - peak)
            denom = jnp.sum(expo, axis=-1, keepdims=True)
            probs = (expo / denom).astype(bf16)
            attended = jnp.einsum("hqk,khd->qhd", probs, values_all, preferred_element_type=f32)
            return (attended, (peak + jnp.log(denom))[:, :, 0])

        attended, log_norm = lax.map(attend, (queries, anc_rows, starts))
        heads_out = attended.reshape(rows_here, heads_here * HEAD_DIM).astype(bf16)
        mixed = stream + head_total(jnp.dot(heads_out, weights[3], preferred_element_type=f32))
        ffn_normed, scaled_b, inverse_b = norm_forward(mixed, weights[1].astype(f32))
        ffn_in = ffn_normed.astype(bf16)
        gate_up = jnp.einsum("td,dcf->tcf", ffn_in, weights[4], preferred_element_type=f32)
        shared_hidden = (jax.nn.silu(gate_up[:, 0]) * gate_up[:, 1]).astype(bf16)
        branch_part = jnp.dot(shared_hidden, weights[5], preferred_element_type=f32)
        slot_rows = jnp.where(slot_live[:, None], ffn_in[slot_owner], jnp.zeros((), bf16)).reshape(
            experts, capacity, width
        )
        expert_gu = jnp.einsum("ecd,edkf->eckf", slot_rows, weights[6], preferred_element_type=f32)
        expert_hidden = (jax.nn.silu(expert_gu[:, :, 0]) * expert_gu[:, :, 1]).astype(bf16)
        expert_rows = jnp.einsum(
            "ecf,efd->ecd", expert_hidden, weights[7], preferred_element_type=f32
        ).reshape(experts * capacity, width)
        branch_part = branch_part + jnp.sum(expert_rows[slot_index] * gate_rows[:, :, None], axis=1)
        saved.append(
            (
                scaled_a,
                inverse_a,
                normed_b,
                qkv,
                keys_all,
                values_all,
                log_norm,
                heads_out,
                scaled_b,
                inverse_b,
                ffn_in,
                gate_up,
                shared_hidden,
                slot_rows,
                expert_gu,
                expert_hidden,
            )
        )
        stream = mixed + head_total(branch_part)
    d_stream = cotangent[0].astype(f32)
    settled = [None] * layers
    for layer_id in reversed(range(layers)):
        (
            scaled_a,
            inverse_a,
            normed_b,
            qkv,
            keys_all,
            values_all,
            log_norm,
            heads_out,
            scaled_b,
            inverse_b,
            ffn_in,
            gate_up,
            shared_hidden,
            slot_rows,
            expert_gu,
            expert_hidden,
        ) = saved[layer_id]
        weights = fetch_again(
            attn_gain[layer_id],
            ffn_gain[layer_id],
            qkv_weight[layer_id],
            out_weight[layer_id],
            shared_in[layer_id],
            shared_out[layer_id],
            expert_in[layer_id],
            expert_out[layer_id],
        )
        gain_a = weights[0].astype(f32)
        gain_b = weights[1].astype(f32)
        d_branch = d_stream.astype(bf16)
        g_shout = jnp.einsum("tf,td->fd", shared_hidden, d_branch, preferred_element_type=f32)
        d_shared = jnp.einsum("td,fd->tf", d_branch, weights[5], preferred_element_type=f32)
        active, slope = silu_parts(gate_up[:, 0])
        d_sgu = jnp.stack([d_shared * gate_up[:, 1] * slope, d_shared * active], axis=1).astype(
            bf16
        )
        g_shin = jnp.einsum("td,tcf->dcf", ffn_in, d_sgu, preferred_element_type=f32)
        d_ffn = jnp.einsum("tcf,dcf->td", d_sgu, weights[4], preferred_element_type=f32)
        d_rows = (
            (slot_gate[:, None] * d_stream[slot_owner])
            .astype(bf16)
            .reshape(experts, capacity, width)
        )
        g_exout = jnp.einsum("ecf,ecd->efd", expert_hidden, d_rows, preferred_element_type=f32)
        d_expert = jnp.einsum("ecd,efd->ecf", d_rows, weights[7], preferred_element_type=f32)
        active_e, slope_e = silu_parts(expert_gu[:, :, 0])
        d_egu = jnp.stack(
            [d_expert * expert_gu[:, :, 1] * slope_e, d_expert * active_e], axis=2
        ).astype(bf16)
        g_exin = jnp.einsum("ecd,eckf->edkf", slot_rows, d_egu, preferred_element_type=f32)
        d_slots = jnp.einsum(
            "eckf,edkf->ecd", d_egu, weights[6], preferred_element_type=f32
        ).reshape(experts * capacity, width)
        d_ffn = d_ffn + jnp.sum(d_slots[slot_index], axis=1)
        d_mixed, g_gain_b = norm_backward(head_total(d_ffn), scaled_b, inverse_b, gain_b)
        d_mixed = d_mixed + d_stream
        d_attn = d_mixed.astype(bf16)
        g_out = jnp.einsum("tf,td->fd", heads_out, d_attn, preferred_element_type=f32)
        heads_here = qkv.shape[2] // HEAD_DIM
        d_heads = jnp.einsum("td,fd->tf", d_attn, weights[3], preferred_element_type=f32).astype(
            bf16
        )
        d_heads = d_heads.reshape(local_blocks, block, heads_here, HEAD_DIM)
        queries = qkv[:, 0].reshape(local_blocks, block, heads_here, HEAD_DIM)

        def back_block(carry, inputs):
            d_keys_acc, d_values_acc = carry
            query_block, d_out_block, norm_block, anc_row, start = inputs
            allowed = allowed_keys(anc_row, start, block, tree_len)
            scores = (
                jnp.einsum("qhd,khd->hqk", query_block, keys_all, preferred_element_type=f32)
                * SCALE
            )
            scores = jnp.where(allowed[None], scores, MASKED)
            probs = jnp.exp(scores - norm_block[:, :, None])
            d_prob = jnp.einsum("qhd,khd->hqk", d_out_block, values_all, preferred_element_type=f32)
            weighted = jnp.sum(probs * d_prob, axis=-1, keepdims=True)
            d_scores = (probs * (d_prob - weighted)).astype(bf16)
            d_query = (
                jnp.einsum("hqk,khd->qhd", d_scores, keys_all, preferred_element_type=f32) * SCALE
            )
            d_keys_acc = (
                d_keys_acc
                + jnp.einsum("hqk,qhd->khd", d_scores, query_block, preferred_element_type=f32)
                * SCALE
            )
            d_values_acc = d_values_acc + jnp.einsum(
                "hqk,qhd->khd", probs.astype(bf16), d_out_block, preferred_element_type=f32
            )
            return ((d_keys_acc, d_values_acc), d_query)

        zero_grad = jnp.zeros((tree_len, heads_here, HEAD_DIM), f32)
        (d_keys_all, d_values_all), d_queries = lax.scan(
            back_block, (zero_grad, zero_grad), (queries, d_heads, log_norm, anc_rows, starts)
        )
        d_keys, d_values = (
            lax.psum_scatter(
                d_keys_all.astype(jnp.bfloat16), "ctx", scatter_dimension=0, tiled=True
            ).astype(jnp.float32),
            lax.psum_scatter(
                d_values_all.astype(jnp.bfloat16), "ctx", scatter_dimension=0, tiled=True
            ).astype(jnp.float32),
        )
        d_qkv = jnp.stack(
            [
                d_queries.reshape(rows_here, heads_here * HEAD_DIM),
                d_keys.reshape(rows_here, heads_here * HEAD_DIM),
                d_values.reshape(rows_here, heads_here * HEAD_DIM),
            ],
            axis=1,
        ).astype(bf16)
        g_qkv = jnp.einsum("td,tcf->dcf", normed_b, d_qkv, preferred_element_type=f32)
        d_normed = head_total(
            jnp.einsum("tcf,dcf->td", d_qkv, weights[2], preferred_element_type=f32)
        )
        d_input, g_gain_a = norm_backward(d_normed, scaled_a, inverse_a, gain_a)
        d_stream = d_input + d_mixed
        settled[layer_id] = settle(
            g_gain_a, g_gain_b, g_qkv, g_out, g_shin, g_shout, g_exin, g_exout
        )
    stacked = [
        jnp.stack([settled[layer_id][member] for layer_id in range(layers)]) for member in range(8)
    ]
    return (
        stream.astype(bf16)[None],
        d_stream[None],
        stacked[0],
        stacked[1],
        stacked[2],
        stacked[3],
        stacked[4],
        stacked[5],
        stacked[6],
        stacked[7],
    )


def solution(mesh):
    return jax.shard_map(
        shards,
        mesh=mesh,
        in_specs=(
            P("fsdp", "ctx", None),
            P("fsdp", None),
            P("fsdp", "ctx", None),
            P("fsdp", "ctx", None),
            P(None, "fsdp"),
            P(None, "fsdp"),
            P(None, "fsdp", None, "tp"),
            P(None, "tp", "fsdp"),
            P(None, "fsdp", None, "tp"),
            P(None, "tp", "fsdp"),
            P(None, None, "fsdp", None, "tp"),
            P(None, None, "tp", "fsdp"),
            P("fsdp", "ctx", None),
        ),
        out_specs=(
            P("fsdp", "ctx", None),
            P("fsdp", "ctx", None),
            P(None, "fsdp"),
            P(None, "fsdp"),
            P(None, "fsdp", None, "tp"),
            P(None, "tp", "fsdp"),
            P(None, "fsdp", None, "tp"),
            P(None, "tp", "fsdp"),
            P(None, None, "fsdp", None, "tp"),
            P(None, None, "tp", "fsdp"),
        ),
        check_vma=False,
    )
```

profile of v0, /device:TPU:0, one launch (start us, length us, event | category | flops | bytes accessed | tf_op | source)
XLA Modules:
  0.0 1695.1 jit_solution(10182549878249450047)
XLA Ops:
  10.2 14.5 all-gather.1
  128.2 16.1 all-gather.31.cloned.1.call-done
  153.4 74.9 %all-gather.29.cloned.1.call-done = bf16[1,8,768,2,512]{4,2,3,1,0:T(8,128)(2,1)} async-done(((bf16[1,8,192,2,512]{4,2,3,1,0:T(8,128)(2,1)}), bf16[1,8,768,2,512]{4,2,3,1,0:T(8,128)(2,1)}) %all-gather.29.cloned.1.call-update) | async-done | bytes 12582928 | tf_op jit(solution)/shard_map/all_gather | solution.py:76
  256.4 16.2 multiply_reduce_fusion.3
  276.8 14.2 all-gather.11
  360.1 14.1 all-gather.17
  392.9 38.4 %all-gather.35.cloned.1.call-done = bf16[1,8,768,2,512]{4,2,3,1,0:T(8,128)(2,1)} async-done(((bf16[1,8,192,2,512]{4,2,3,1,0:T(8,128)(2,1)}), bf16[1,8,768,2,512]{4,2,3,1,0:T(8,128)(2,1)}) %all-gather.35.cloned.1.call-update) | async-done | bytes 12582928 | tf_op jit(solution)/shard_map/all_gather | solution.py:76
  488.6 42.5 %all-reduce.28.cloned.1.call-done = bf16[512,768]{1,0:T(8,128)(2,1)} async-done(((bf16[512,768]{1,0:T(8,128)(2,1)}), bf16[512,768]{1,0:T(8,128)(2,1)}) %all-reduce.28.cloned.1.call-update) | async-done | bytes 786448 | tf_op jit(solution)/shard_map/psum | solution.py:95
  559.3 15.9 reduce-scatter.21.cloned.1.call-done
  578.7 43.5 %all-reduce.30.cloned.1.call-done = bf16[512,768]{1,0:T(8,128)(2,1)} async-done(((bf16[512,768]{1,0:T(8,128)(2,1)}), bf16[512,768]{1,0:T(8,128)(2,1)}) %all-reduce.30.cloned.1.call-update) | async-done | bytes 786448 | tf_op jit(solution)/shard_map/psum | solution.py:95
  681.4 43.1 %all-reduce.32.cloned.1.call-done = bf16[512,768]{1,0:T(8,128)(2,1)} async-done(((bf16[512,768]{1,0:T(8,128)(2,1)}), bf16[512,768]{1,0:T(8,128)(2,1)}) %all-reduce.32.cloned.1.call-update) | async-done | bytes 786448 | tf_op jit(solution)/shard_map/psum | solution.py:95
  833.1 16.3 multiply_reduce_fusion.2
  856.1 14.8 reduce-scatter.35.cloned.1.call-done
  871.0 28.7 %reduce-scatter.31.cloned.1.call-done = bf16[192,3,192]{2,0,1:T(8,128)(2,1)} async-done(((bf16[768,3,192]{2,0,1:T(8,128)(2,1)}), bf16[192,3,192]{2,0,1:T(8,128)(2,1)}) %reduce-scatter.31.cloned.1.call-update) | async-done | bytes 221200 | tf_op jit(solution)/shard_map/reduce_scatter | solution.py:106
  899.7 25.9 %reduce-scatter.37.cloned.1.call-done = bf16[512,192]{0,1:T(8,128)(2,1)} async-done(((bf16[512,768]{0,1:T(8,128)(2,1)}), bf16[512,192]{0,1:T(8,128)(2,1)}) %reduce-scatter.37.cloned.1.call-update) | async-done | bytes 196624 | tf_op jit(solution)/shard_map/reduce_scatter | solution.py:115
  925.5 31.2 %reduce-scatter.33.cloned.1.call-done = bf16[192,2,512]{2,0,1:T(8,128)(2,1)} async-done(((bf16[768,2,512]{2,0,1:T(8,128)(2,1)}), bf16[192,2,512]{2,0,1:T(8,128)(2,1)}) %reduce-scatter.33.cloned.1.call-update) | async-done | bytes 393232 | tf_op jit(solution)/shard_map/reduce_scatter | solution.py:112
  956.7 28.3 %reduce-scatter.29.cloned.1.call-done = bf16[192,3,192]{2,0,1:T(8,128)(2,1)} async-done(((bf16[768,3,192]{2,0,1:T(8,128)(2,1)}), bf16[192,3,192]{2,0,1:T(8,128)(2,1)}) %reduce-scatter.29.cloned.1.call-update) | async-done | bytes 221200 | tf_op jit(solution)/shard_map/reduce_scatter | solution.py:106
  985.1 61.5 %reduce-scatter.47.cloned.1.call-done = bf16[8,512,192]{1,2,0:T(8,128)(2,1)} async-done(((bf16[8,512,768]{1,2,0:T(8,128)(2,1)}), bf16[8,512,192]{1,2,0:T(8,128)(2,1)}) %reduce-scatter.47.cloned.1.call-update) | async-done | bytes 1572880 | tf_op jit(solution)/shard_map/reduce_scatter | solution.py:121
  1046.6 60.9 %reduce-scatter.45.cloned.1.call-done = bf16[8,512,192]{1,2,0:T(8,128)(2,1)} async-done(((bf16[8,512,768]{1,2,0:T(8,128)(2,1)}), bf16[8,512,192]{1,2,0:T(8,128)(2,1)}) %reduce-scatter.45.cloned.1.call-update) | async-done | bytes 1572880 | tf_op jit(solution)/shard_map/reduce_scatter | solution.py:121
  1107.5 102.3 %reduce-scatter.43.cloned.1.call-done = bf16[8,192,2,512]{3,1,2,0:T(8,128)(2,1)} async-done(((bf16[8,768,2,512]{3,1,2,0:T(8,128)(2,1)}), bf16[8,192,2,512]{3,1,2,0:T(8,128)(2,1)}) %reduce-scatter.43.cloned.1.call-update) | async-done | bytes 3145744 | tf_op jit(solution)/shard_map/reduce_scatter | solution.py:118
  1209.8 101.7 %reduce-scatter.41.cloned.1.call-done = bf16[8,192,2,512]{3,1,2,0:T(8,128)(2,1)} async-done(((bf16[8,768,2,512]{3,1,2,0:T(8,128)(2,1)}), bf16[8,192,2,512]{3,1,2,0:T(8,128)(2,1)}) %reduce-scatter.41.cloned.1.call-update) | async-done | bytes 3145744 | tf_op jit(solution)/shard_map/reduce_scatter | solution.py:118
  1312.2 71.8 %all-reduce.34.cloned.1.call-done = (bf16[512,768]{1,0:T(8,128)(2,1)}, bf16[512,768]{1,0:T(8,128)(2,1)}) async-done(((bf16[512,768]{1,0:T(8,128)(2,1)}, bf16[512,768]{1,0:T(8,128)(2,1)}), (bf16[512,768]{1,0:T(8,128)(2,1)}, bf16[512,768]{1,0:T(8,128)(2,1)})) %all-reduce.34.cloned.1.call-update) | async-done | bytes 1572880 | tf_op jit(solution)/shard_map/psum | solution.py:95
  1401.6 254.4 %all-reduce.36.cloned.1.call-done = (bf16[1,192,3,192]{3,1,2,0:T(8,128)(2,1)}, bf16[1,192,3,192]{3,1,2,0:T(8,128)(2,1)}, bf16[1,192,192]{2,1,0:T(8,128)(2,1)}, b...) async-done(((bf16[1,192,3,192]{3,1,2,0:T(8,128)(2,1)}, ...) | async-done | bytes 11206672 | tf_op jit(solution)/shard_map/psum | solution.py:128
  1662.5 18.6 %copy.128 = f32[2,8,192,2,512]{4,3,2,1,0:T(2,128)} copy(f32[2,8,192,2,512]{4,2,3,1,0:T(8,128)S(1)} %maximum_convert_fusion) | data formatting | bytes 25165824
  (524 shorter events, 526.4 us)
Async XLA Ops:
  8.0 106.6 %all-reduce.22.cloned.1.call-start = ((), (), s32[]{:S(2)}) async-start(), calls=%async_computation.16 | async-start | bytes 1572864 | tf_op jit(solution)/shard_map/psum | solution.py:95
  76.3 152.0 %all-gather.29.cloned.1.call-start = ((), (), s32[]{:S(2)}) async-start(), calls=%async_computation.37 | async-start | bytes 15728640 | tf_op jit(solution)/shard_map/all_gather | solution.py:76
  86.9 231.1 %all-reduce.24.cloned.1.call-start = ((), (), s32[]{:S(2)}) async-start(), calls=%async_computation.17 | async-start | bytes 1572864 | tf_op jit(solution)/shard_map/psum | solution.py:95
  274.2 100.1 %all-gather.37.cloned.1.call-start = ((), (), s32[]{:S(2)}) async-start(), calls=%async_computation.41 | async-start | bytes 7864320 | tf_op jit(solution)/shard_map/all_gather | solution.py:77
  276.5 108.0 %all-reduce.26.cloned.1.call-start = ((), (), s32[]{:S(2)}) async-start(), calls=%async_computation.18 | async-start | bytes 1572864 | tf_op jit(solution)/shard_map/psum | solution.py:95
  341.5 89.8 %all-gather.35.cloned.1.call-start = ((), (), s32[]{:S(2)}) async-start(), calls=%async_computation.40 | async-start | bytes 15728640 | tf_op jit(solution)/shard_map/all_gather | solution.py:76
  345.9 133.9 %all-gather.33.cloned.1.call-start = ((), (), s32[]{:S(2)}) async-start(), calls=%async_computation.39 | async-start | bytes 1966080 | tf_op jit(solution)/shard_map/all_gather | solution.py:74
  347.6 183.4 %all-reduce.28.cloned.1.call-start = ((), (), s32[]{:S(2)}) async-start(), calls=%async_computation.19 | async-start | bytes 1572864 | tf_op jit(solution)/shard_map/psum | solution.py:95
  578.5 146.0 %all-reduce.32.cloned.1.call-start = ((), (), s32[]{:S(2)}) async-start(), calls=%async_computation.23 | async-start | bytes 1572864 | tf_op jit(solution)/shard_map/psum | solution.py:95
  681.4 92.1 %reduce-scatter.27.cloned.1.call-start = ((), (), s32[]{:S(2)}) async-start(), calls=%async_computation.25 | async-start | bytes 589824 | tf_op jit(solution)/shard_map/reduce_scatter | solution.py:354
  747.8 105.1 %reduce-scatter.51.cloned.1.call-start = ((), (), s32[]{:S(2)}) async-start(), calls=%async_computation.43 | async-start | bytes 491520
  750.7 103.8 %reduce-scatter.49.cloned.1.call-start = ((), (), s32[]{:S(2)}) async-start(), calls=%async_computation.42 | async-start | bytes 491520
  753.5 102.6 %reduce-scatter.39.cloned.1.call-start = ((), (), s32[]{:S(2)}) async-start(), calls=%async_computation.31 | async-start | bytes 983040 | tf_op jit(solution)/shard_map/reduce_scatter | solution.py:115
  757.0 113.9 %reduce-scatter.35.cloned.1.call-start = ((), (), s32[]{:S(2)}) async-start(), calls=%async_computation.29 | async-start | bytes 1966080 | tf_op jit(solution)/shard_map/reduce_scatter | solution.py:112
  760.5 139.2 %reduce-scatter.31.cloned.1.call-start = ((), (), s32[]{:S(2)}) async-start(), calls=%async_computation.27 | async-start | bytes 1474560 | tf_op jit(solution)/shard_map/reduce_scatter | solution.py:106
  764.2 161.3 %reduce-scatter.37.cloned.1.call-start = ((), (), s32[]{:S(2)}) async-start(), calls=%async_computation.30 | async-start | bytes 983040 | tf_op jit(solution)/shard_map/reduce_scatter | solution.py:115
  767.0 189.8 %reduce-scatter.33.cloned.1.call-start = ((), (), s32[]{:S(2)}) async-start(), calls=%async_computation.28 | async-start | bytes 1966080 | tf_op jit(solution)/shard_map/reduce_scatter | solution.py:112
  770.4 214.6 %reduce-scatter.29.cloned.1.call-start = ((), (), s32[]{:S(2)}) async-start(), calls=%async_computation.26 | async-start | bytes 1474560 | tf_op jit(solution)/shard_map/reduce_scatter | solution.py:106
  776.7 269.9 %reduce-scatter.47.cloned.1.call-start = ((), (), s32[]{:S(2)}) async-start(), calls=%async_computation.35 | async-start | bytes 7864320 | tf_op jit(solution)/shard_map/reduce_scatter | solution.py:121
  784.1 323.5 %reduce-scatter.45.cloned.1.call-start = ((), (), s32[]{:S(2)}) async-start(), calls=%async_computation.34 | async-start | bytes 7864320 | tf_op jit(solution)/shard_map/reduce_scatter | solution.py:121
  792.6 417.2 %reduce-scatter.43.cloned.1.call-start = ((), (), s32[]{:S(2)}) async-start(), calls=%async_computation.33 | async-start | bytes 15728640 | tf_op jit(solution)/shard_map/reduce_scatter | solution.py:118
  802.3 509.1 %reduce-scatter.41.cloned.1.call-start = ((), (), s32[]{:S(2)}) async-start(), calls=%async_computation.32 | async-start | bytes 15728640 | tf_op jit(solution)/shard_map/reduce_scatter | solution.py:118
  812.0 572.0 %all-reduce.34.cloned.1.call-start = ((), (), s32[]{:S(2)}) async-start(), calls=%async_computation.44 | async-start | bytes 3145728 | tf_op jit(solution)/shard_map/psum | solution.py:95
  852.8 803.3 %all-reduce.36.cloned.1.call-start = ((), (), s32[]{:S(2)}) async-start(), calls=%async_computation.45 | async-start | bytes 22806528 | tf_op jit(solution)/shard_map/psum | solution.py:128
  (129 other events, 1936.7 us)
Sparse Core Ops, SparseCore 0:
  69.0 44.4 all-reduce.21
  274.3 43.6 all-reduce.23
  341.7 42.7 all-reduce.25
  487.4 43.6 all-reduce.27
  546.8 12.4 reduce-scatter.22
  562.0 13.1 reduce-scatter.20
  578.6 43.6 all-reduce.29
  681.5 42.9 all-reduce.31
  739.3 12.4 reduce-scatter.26
  754.6 13.1 reduce-scatter.24
  770.2 20.8 reduce-scatter.50
  793.5 20.8 reduce-scatter.48
  816.9 23.2 reduce-scatter.38
  842.7 28.1 reduce-scatter.34
  873.9 25.6 reduce-scatter.30
  902.2 23.2 reduce-scatter.36
  928.5 28.1 reduce-scatter.32
  959.3 25.6 reduce-scatter.28
  988.2 58.3 reduce-scatter.46
  1049.1 58.3 reduce-scatter.44
  1110.7 99.0 reduce-scatter.42
  1212.4 99.0 reduce-scatter.40
  1314.5 69.4 all-reduce.33
  1388.1 267.9 all-reduce.35
Sparse Core Ops, SparseCore 1:
  71.5 20.3 all-gather.26
  93.8 50.4 all-gather.30
  146.3 81.9 all-gather.28
  277.1 51.2 all-gather.36
  345.9 85.3 all-gather.34
  433.5 19.5 all-gather.32
where the time goes:
time: 1710 us; the launch traced here: 1700 us
  waiting for transfers between devices  1070 us (63%)
  local copies, waits for them, and re-layouts  198 us (12%)
  matrix products  185 us (11%)
  blocking collectives  123 us (7%)
  other arithmetic  101 us (6%)
  between operations  19.3 us (1%)
    psum x1, waiting for transfers between devices, settle(): lax.psum(shares[2].astype(jnp.bfloat16), 'ctx').astype(jnp.float32)  254 us
    psum x7, waiting for transfers between devices, head_total(): return lax.psum(values.astype(jnp.bfloat16), 'tp').astype(jnp.float32)  211 us
    reduce_scatter x2, waiting for transfers between devices, settle(): lax.psum_scatter(g_exin.astype(jnp.bfloat16), 'fsdp', scatter_dimension=1...  204 us
    reduce_scatter x2, waiting for transfers between devices, settle(): lax.psum_scatter(g_exout.astype(jnp.bfloat16), 'fsdp', scatter_dimension=...  122 us
    all_gather x2, waiting for transfers between devices, fetch(): lax.all_gather(ex_in, 'fsdp', axis=1, tiled=True)  113 us
    unnamed x278, local copies, waits for them, and re-layouts  65.9 us
    reduce_scatter x2, waiting for transfers between devices, settle(): lax.psum_scatter(g_qkv.astype(jnp.bfloat16), 'fsdp', scatter_dimension=0,...  57 us
    reduce_scatter x2, waiting for transfers between devices, settle(): lax.psum_scatter(g_shin.astype(jnp.bfloat16), 'fsdp', scatter_dimension=0...  46 us
  transfers between devices with their start and end apart: 30, of which 21 were waited for; matrix products, arithmetic and copies ran while one was open for 16% of the time, Pallas kernels for 0%

commit v1 on v0

v1 whole, which is shorter than its diff:
```python
import functools

import jax
import jax.numpy as jnp
from jax import lax
from jax.experimental import pallas as pl
from jax.experimental.pallas import tpu as pltpu
from jax.sharding import PartitionSpec as P

HEAD_DIM = 64
EPS = 1e-06
SCALE = 0.125
MASKED = -1000000000.0
F32 = jnp.float32
BF16 = jnp.bfloat16
VMEM_LIMIT = 56 << 20

NN = (((1,), (0,)), ((), ()))
NT = (((1,), (1,)), ((), ()))
TN = (((0,), (0,)), ((), ()))


def mm(a, b, dims=NN):
    return lax.dot_general(a, b, dims, preferred_element_type=F32)


def swap(values, axis, mask):
    count = lax.axis_size(axis)
    return lax.ppermute(values, axis, [(k, k ^ mask) for k in range(count)])


def gather_blocks(values):
    far = swap(values, "fsdp", 2)
    return [values, swap(values, "fsdp", 1), far, swap(far, "fsdp", 1)]


def swap_blocks(values, axis, block):
    take = lambda r: lax.slice_in_dim(values, r * block, (r + 1) * block, axis=axis)
    return jnp.concatenate([take(1), take(0), take(3), take(2)], axis=axis)


def to_relative(values, block):
    me = lax.axis_index("fsdp")
    cut = lambda v, lo, hi: lax.slice_in_dim(v, lo * block, hi * block, axis=v.ndim - 1)
    far = jnp.concatenate([cut(values, 2, 4), cut(values, 0, 2)], axis=-1)
    values = jnp.where((me & 2) > 0, far, values)
    return jnp.where((me & 1) > 0, swap_blocks(values, values.ndim - 1, block), values)


def tp_sum(part):
    part = part.astype(BF16)
    count = lax.axis_size("tp")
    half = part.shape[0] // 2
    bit = lax.axis_index("tp") & 1
    keep = lax.dynamic_slice_in_dim(part, bit * half, half, 0)
    give = lax.dynamic_slice_in_dim(part, (1 - bit) * half, half, 0)
    total = keep.astype(F32) + swap(give, "tp", 1).astype(F32)
    step = 2
    while step < count:
        sent = total.astype(BF16)
        total = sent.astype(F32) + swap(sent, "tp", step).astype(F32)
        step *= 2
    mine = total.astype(BF16)
    other = swap(mine, "tp", 1)
    first = jnp.where(bit == 0, mine, other)
    last = jnp.where(bit == 0, other, mine)
    return jnp.concatenate([first, last], axis=0).astype(F32)


def ctx_sum(part):
    count = lax.axis_size("ctx")
    total = part
    step = 1
    while step < count:
        sent = total.astype(BF16)
        total = sent.astype(F32) + swap(sent, "ctx", step).astype(F32)
        step *= 2
    return total.astype(F32)


def ctx_scatter(whole):
    count = lax.axis_size("ctx")
    parts = whole.reshape((count, whole.shape[0] // count) + whole.shape[1:])
    parts = lax.all_to_all(parts, "ctx", 0, 0, tiled=True)
    return jnp.sum(parts.astype(F32), axis=0)


def settle_plain(grad, axis):
    block = grad.shape[axis] // 4
    cut = lambda v, lo, hi: lax.slice_in_dim(v, lo * block, hi * block, axis=axis)
    grad = grad.astype(BF16)
    near = cut(grad, 0, 2).astype(F32) + swap(cut(grad, 2, 4), "fsdp", 2).astype(F32)
    near = near.astype(BF16)
    own = cut(near, 0, 1).astype(F32) + swap(cut(near, 1, 2), "fsdp", 1).astype(F32)
    return ctx_sum(own.astype(BF16))


def settle_experts(near, far, axis):
    block = near.shape[axis] // 2
    cut = lambda v, lo, hi: lax.slice_in_dim(v, lo * block, hi * block, axis=axis)
    got = swap(far, "fsdp", 2)
    own = (cut(near, 0, 1).astype(F32) + cut(got, 0, 1).astype(F32)).astype(BF16)
    give = (cut(near, 1, 2).astype(F32) + cut(got, 1, 2).astype(F32)).astype(BF16)
    other = swap(give, "fsdp", 1)
    own, other = ctx_sum(own), ctx_sum(other)
    core = lax.axis_index("fsdp") & 1
    first = jnp.where(core == 0, own, other)
    last = jnp.where(core == 0, other, own)
    return jnp.concatenate([first, last], axis=0)


def allowed_of(base_ref, path_ref, rows, tree_len):
    query_pos = (
        base_ref[0]
        + pl.program_id(0) * rows
        + lax.broadcasted_iota(jnp.int32, (rows, tree_len), 0)
    )
    key_pos = lax.broadcasted_iota(jnp.int32, (rows, tree_len), 1)
    return (key_pos <= query_pos) & (path_ref[...] > 0.5)


def softmax_of(query, key, allowed):
    scores = jnp.where(allowed, mm(query, key, NT) * SCALE, MASKED)
    expo = jnp.exp(scores - jnp.max(scores, axis=-1, keepdims=True))
    return expo * (1.0 / jnp.sum(expo, axis=-1, keepdims=True))


def attend_kernel(base_ref, path_ref, q_ref, k_ref, v_ref, out_ref):
    rows, width = q_ref.shape
    allowed = allowed_of(base_ref, path_ref, rows, k_ref.shape[0])
    outs = []
    for head in range(width // HEAD_DIM):
        cols = slice(head * HEAD_DIM, (head + 1) * HEAD_DIM)
        probs = softmax_of(q_ref[:, cols], k_ref[:, cols], allowed).astype(BF16)
        outs.append(mm(probs, v_ref[:, cols]))
    out_ref[...] = jnp.concatenate(outs, axis=1).astype(BF16)


def attend_back_kernel(
    base_ref, path_ref, q_ref, k_ref, v_ref, do_ref, dq_ref, dk_ref, dv_ref, dk_acc, dv_acc
):
    rows, width = q_ref.shape
    allowed = allowed_of(base_ref, path_ref, rows, k_ref.shape[0])

    @pl.when(pl.program_id(0) == 0)
    def _():
        dk_acc[...] = jnp.zeros_like(dk_acc)
        dv_acc[...] = jnp.zeros_like(dv_acc)

    dqs, dks, dvs = [], [], []
    for head in range(width // HEAD_DIM):
        cols = slice(head * HEAD_DIM, (head + 1) * HEAD_DIM)
        query, key, value, d_out = q_ref[:, cols], k_ref[:, cols], v_ref[:, cols], do_ref[:, cols]
        probs = softmax_of(query, key, allowed)
        d_prob = mm(d_out, value, NT)
        weighted = jnp.sum(probs * d_prob, axis=-1, keepdims=True)
        d_scores = (probs * (d_prob - weighted)).astype(BF16)
        dqs.append(mm(d_scores, key) * SCALE)
        dks.append(mm(d_scores, query, TN))
        dvs.append(mm(probs.astype(BF16), d_out, TN))
    dq_ref[...] = jnp.concatenate(dqs, axis=1).astype(BF16)
    dk_acc[...] += jnp.concatenate(dks, axis=1)
    dv_acc[...] += jnp.concatenate(dvs, axis=1)

    @pl.when(pl.program_id(0) == pl.num_programs(0) - 1)
    def _():
        dk_ref[...] = (dk_acc[...] * SCALE).astype(BF16)
        dv_ref[...] = dv_acc[...].astype(BF16)


def attention_call(kernel, base, path, arrays, outs, scratch, flops):
    rows, width = arrays[0].shape
    tree_len = arrays[1].shape[0]
    tile = rows // 2
    tiled = pl.BlockSpec((tile, width), lambda t, *_: (t, 0))
    whole = pl.BlockSpec((tree_len, width), lambda t, *_: (0, 0))
    spec_of = lambda a: tiled if a.shape[0] == rows and a is not arrays[1] and a is not arrays[2] else whole
    return pl.pallas_call(
        kernel,
        out_shape=[jax.ShapeDtypeStruct((n, width), BF16) for n in outs],
        grid_spec=pltpu.PrefetchScalarGridSpec(
            num_scalar_prefetch=1,
            grid=(rows // tile,),
            in_specs=[pl.BlockSpec((1, tree_len), lambda t, *_: (0, 0))]
            + [spec_of(a) for a in arrays],
            out_specs=[tiled if at == 0 else whole for at in range(len(outs))],
            scratch_shapes=scratch,
        ),
        compiler_params=pltpu.CompilerParams(
            dimension_semantics=("arbitrary",), vmem_limit_bytes=VMEM_LIMIT
        ),
        cost_estimate=pl.CostEstimate(
            flops=flops * rows * tree_len * width,
            transcendentals=rows * tree_len * width // HEAD_DIM,
            bytes_accessed=2 * width * (2 * rows + 4 * tree_len),
        ),
    )(base, path, *arrays)


def one_hot_rows(pos_row, slots):
    hit = lax.broadcasted_iota(jnp.int32, (slots, pos_row.shape[1]), 0) == pos_row
    return jnp.where(hit, 1.0, 0.0).astype(BF16)


def one_hot_cols(pos_col, slots):
    hit = lax.broadcasted_iota(jnp.int32, (pos_col.shape[0], slots), 1) == pos_col
    return jnp.where(hit, 1.0, 0.0).astype(BF16)


def joined(refs, at):
    return jnp.concatenate([ref[at] for ref in refs], axis=0)


def expert_kernel(core_ref, tok_ref, row_ref, col_ref, mix_ref, *refs):
    ins, outs = refs[:4], refs[4:8]
    own_ref, sib_ref, x_ref, gate_ref, up_ref, acc = refs[8:]
    slots = x_ref.shape[1]

    @pl.when(pl.program_id(0) == 0)
    def _():
        acc[...] = jnp.zeros_like(acc)

    chosen = mm(one_hot_rows(row_ref[0], slots), tok_ref[...]).astype(BF16)
    x_ref[0] = chosen
    gate = mm(chosen, joined(ins, (0, 0)))
    up = mm(chosen, joined(ins, (0, 1)))
    gate_ref[0] = gate
    up_ref[0] = up
    hidden = (gate / (1.0 + jnp.exp(-gate)) * up).astype(BF16)
    rows = mm(hidden, joined(outs, 0), NT).astype(BF16)
    acc[...] += mix_ref[0] * mm(one_hot_cols(col_ref[0], slots), rows)

    @pl.when(pl.program_id(0) == pl.num_programs(0) - 1)
    def _():
        half = own_ref.shape[0]
        own_ref[...] = acc[:half, :]
        sib_ref[...] = acc[half:, :].astype(BF16)


def expert_back_kernel(core_ref, d_ref, row_ref, col_ref, mix_ref, x_ref, gate_ref, up_ref, *refs):
    ins, outs = refs[:4], refs[4:8]
    own_ref, sib_ref, gin_near, gin_far, gout_near, gout_far, acc = refs[8:]
    slots = x_ref.shape[1]

    @pl.when(pl.program_id(0) == 0)
    def _():
        acc[...] = jnp.zeros_like(acc)

    hit = lax.broadcasted_iota(jnp.int32, (slots, row_ref.shape[2]), 0) == row_ref[0]
    weight = jnp.sum(jnp.where(hit, mix_ref[0], 0.0), axis=1, keepdims=True)
    d_rows = (mm(jnp.where(hit, 1.0, 0.0).astype(BF16), d_ref[...]) * weight).astype(BF16)
    d_hidden = mm(d_rows, joined(outs, 0))
    gate, up = gate_ref[0], up_ref[0]
    sigmoid = 1.0 / (1.0 + jnp.exp(-gate))
    active = gate * sigmoid
    hidden = (active * up).astype(BF16)
    d_gate = (d_hidden * up * (sigmoid * (1.0 + gate * (1.0 - sigmoid)))).astype(BF16)
    d_up = (d_hidden * active).astype(BF16)
    half = gin_near.shape[2]
    chosen = x_ref[0]
    g_out = mm(d_rows, hidden, TN).astype(BF16)
    gout_near[0] = g_out[:half]
    gout_far[0] = g_out[half:]
    for at, d_part in enumerate((d_gate, d_up)):
        g_in = mm(chosen, d_part, TN).astype(BF16)
        gin_near[0, at] = g_in[:half]
        gin_far[0, at] = g_in[half:]
    d_x = mm(d_gate, joined(ins, (0, 0)), NT) + mm(d_up, joined(ins, (0, 1)), NT)
    acc[...] += mm(one_hot_cols(col_ref[0], slots), d_x.astype(BF16))

    @pl.when(pl.program_id(0) == pl.num_programs(0) - 1)
    def _():
        count = own_ref.shape[0]
        own_ref[...] = acc[:count, :]
        sib_ref[...] = acc[count:, :].astype(BF16)


def experts_call(kernel, core, tok, row, col, mix, kept, w_in, w_out, new, flops):
    count = row.shape[0]
    tokens, width = tok.shape
    _, _, block, hid = w_in[0].shape
    lead = lambda a: pl.BlockSpec((1,) + a.shape[1:], lambda e, c: (e,) + (0,) * (len(a.shape) - 1))
    whole = lambda s: pl.BlockSpec(s, lambda e, c: (0,) * len(s))
    mine = lambda a: pl.BlockSpec(
        (1,) + a.shape[1:], lambda e, c: (c[0] * count + e,) + (0,) * (a.ndim - 1)
    )
    half = (tokens // 2, width)
    shapes = [jax.ShapeDtypeStruct(half, F32), jax.ShapeDtypeStruct(half, BF16)] + new
    moved = 2 * count * 12 * block * hid + sum(
        s.size * s.dtype.itemsize for s in list(kept) + shapes + [tok]
    )
    return pl.pallas_call(
        kernel,
        out_shape=shapes,
        grid_spec=pltpu.PrefetchScalarGridSpec(
            num_scalar_prefetch=1,
            grid=(count,),
            in_specs=[whole(tok.shape), lead(row), lead(col), lead(mix)]
            + [lead(a) for a in kept]
            + [mine(a) for a in list(w_in) + list(w_out)],
            out_specs=[whole(half), whole(half)] + [lead(s) for s in new],
            scratch_shapes=[pltpu.VMEM((tokens, width), F32)],
        ),
        compiler_params=pltpu.CompilerParams(
            dimension_semantics=("arbitrary",), vmem_limit_bytes=VMEM_LIMIT
        ),
        cost_estimate=pl.CostEstimate(
            flops=flops, transcendentals=count * 384 * hid, bytes_accessed=moved
        ),
    )(core, tok, row, col, mix, *kept, *w_in, *w_out)


def norm_forward(values, gain):
    inverse = lax.rsqrt(jnp.mean(values * values, axis=-1, keepdims=True) + EPS)
    scaled = values * inverse
    return (scaled * gain, inverse)


def norm_backward(d_normed, scaled, inverse, gain):
    d_scaled = d_normed * gain
    d_values = inverse * (d_scaled - scaled * jnp.mean(d_scaled * scaled, axis=-1, keepdims=True))
    return (d_values, jnp.sum(d_normed * scaled, axis=0))


def ancestry(parent_row):
    count = parent_row.shape[0]
    block_ids = jnp.arange(count, dtype=jnp.int32)
    step_map = ((parent_row[:, None] == block_ids[None, :]) & (block_ids[:, None] > 0)).astype(F32)
    reach = on_path = jnp.eye(count, dtype=F32)
    for _ in range(count):
        reach = jnp.dot(reach, step_map, precision=lax.Precision.HIGHEST)
        on_path = on_path + reach
    return on_path


def shards(
    tokens,
    parents,
    routes,
    gates,
    attn_gain,
    ffn_gain,
    qkv_weight,
    out_weight,
    shared_in,
    shared_out,
    expert_in,
    expert_out,
    cotangent,
):
    rows_here, width = tokens.shape[1], tokens.shape[2]
    layers, experts = expert_in.shape[0], expert_in.shape[1]
    block = qkv_weight.shape[1]
    heads_width = qkv_weight.shape[3]
    hid = expert_in.shape[4]
    tree_len = rows_here * lax.axis_size("ctx")
    me = lax.axis_index("fsdp")
    core = me & 1
    per_core = experts // 2
    capacity = 2 * (3 * rows_here // 8)

    qkv_t = qkv_weight.transpose(0, 2, 1, 3)
    out_t = out_weight.transpose(0, 2, 1)
    sin_t = shared_in.transpose(0, 2, 1, 3)
    sout_t = shared_out.transpose(0, 2, 1)
    ein_t = expert_in.transpose(0, 1, 3, 2, 4)
    eout_t = expert_out.transpose(0, 1, 3, 2)

    gains = jnp.concatenate(
        gather_blocks(jnp.concatenate([attn_gain, ffn_gain], axis=0)), axis=1
    ).astype(F32)
    weights = []
    for at in range(layers):
        weights.append(
            dict(
                qkv=jnp.concatenate(gather_blocks(qkv_t[at]), axis=1),
                out=jnp.concatenate(gather_blocks(out_t[at]), axis=0),
                sin=jnp.concatenate(gather_blocks(sin_t[at]), axis=1),
                sout=jnp.concatenate(gather_blocks(sout_t[at]), axis=0),
                eout=gather_blocks(eout_t[at]),
                ein=gather_blocks(ein_t[at]),
            )
        )

    ancestors = ancestry(parents[0])
    segment = tree_len // ancestors.shape[0]
    start = lax.axis_index("ctx") * rows_here
    anc_row = lax.dynamic_slice_in_dim(ancestors, start // segment, 1, 0)
    path = jnp.repeat(anc_row, segment, axis=1)
    base = jnp.reshape(start, (1,)).astype(jnp.int32)

    chosen = routes[0][:, :, None] == jnp.arange(experts, dtype=jnp.int32)[None, None, :]
    mixing = jnp.sum(jnp.where(chosen, gates[0][:, :, None], 0.0), axis=1)
    mixing = jnp.concatenate([mixing, swap(mixing, "fsdp", 1)], axis=0)
    mixing = lax.dynamic_slice_in_dim(mixing, core * per_core, per_core, 1)
    named = mixing > 0.0
    pair = mixing.shape[0]
    earlier = (jnp.arange(pair)[:, None] > jnp.arange(pair)[None, :]).astype(BF16)
    slot = mm(earlier, named.astype(BF16)).astype(jnp.int32)
    slot = jnp.where(named, slot, -1).T
    mixing = mixing.T
    slot_row, slot_col = slot[:, None, :], slot[:, :, None]
    mix_row, mix_col = mixing[:, None, :], mixing[:, :, None]
    core_id = jnp.reshape(core, (1,)).astype(jnp.int32)

    with_sibling = lambda v: jnp.concatenate(
        [v, swap_blocks(swap(v, "fsdp", 1), 1, block)], axis=0
    )
    from_sibling = lambda v: swap_blocks(swap(v, "fsdp", 1), 1, block).astype(F32)
    sds = jax.ShapeDtypeStruct
    flops = 2 * per_core * capacity * width * hid

    stream = to_relative(tokens[0], block).astype(F32)
    saved = []
    for at in range(layers):
        w = weights[at]
        normed, inverse_a = norm_forward(stream, gains[at][None])
        normed = normed.astype(BF16)
        query, key, value = (mm(normed, w["qkv"][part]).astype(BF16) for part in range(3))
        both = lax.all_gather(jnp.concatenate([key, value], axis=1), "ctx", axis=0, tiled=True)
        keys, values = both[:, :heads_width], both[:, heads_width:]
        (heads_out,) = attention_call(
            attend_kernel, base, path, (query, keys, values), (rows_here,), [], 4
        )
        mixed = stream + tp_sum(mm(heads_out, w["out"], NT))
        ffn_in, inverse_b = norm_forward(mixed, gains[layers + at][None])
        ffn_in = ffn_in.astype(BF16)
        pair_in = with_sibling(ffn_in)
        gate = mm(ffn_in, w["sin"][0])
        up = mm(ffn_in, w["sin"][1])
        shared_hidden = (gate * jax.nn.sigmoid(gate) * up).astype(BF16)
        branch = mm(shared_hidden, w["sout"], NT)
        own, sib, x, e_gate, e_up = experts_call(
            expert_kernel,
            core_id,
            pair_in,
            slot_row,
            slot_col,
            mix_col,
            (),
            w["ein"],
            w["eout"],
            [
                sds((per_core, capacity, width), BF16),
                sds((per_core, capacity, hid), F32),
                sds((per_core, capacity, hid), F32),
            ],
            5 * flops,
        )
        branch = branch + own + from_sibling(sib)
        saved.append(
            (stream, inverse_a, normed, query, keys, values, heads_out, mixed, inverse_b, ffn_in)
            + (gate, up, shared_hidden, x, e_gate, e_up)
        )
        stream = mixed + tp_sum(branch)
    result = to_relative(stream.astype(BF16), block)

    d_stream = to_relative(cotangent[0], block).astype(F32)
    grads = [None] * layers
    for at in reversed(range(layers)):
        w = weights[at]
        (stream, inverse_a, normed, query, keys, values, heads_out, mixed, inverse_b, ffn_in) = (
            saved[at][:10]
        )
        gate, up, shared_hidden, x, e_gate, e_up = saved[at][10:]
        d_branch = d_stream.astype(BF16)
        pair_d = with_sibling(d_branch)
        d_shared = mm(d_branch, w["sout"])
        sigmoid = jax.nn.sigmoid(gate)
        active = gate * sigmoid
        d_gate = (d_shared * up * (sigmoid * (1.0 + gate * (1.0 - sigmoid)))).astype(BF16)
        d_up = (d_shared * active).astype(BF16)
        d_ffn = mm(d_gate, w["sin"][0], NT) + mm(d_up, w["sin"][1], NT)
        own, sib, gin_near, gin_far, gout_near, gout_far = experts_call(
            expert_back_kernel,
            core_id,
            pair_d,
            slot_row,
            slot_col,
            mix_row,
            (x, e_gate, e_up),
            w["ein"],
            w["eout"],
            [sds((per_core, 2, 2 * block, hid), BF16)] * 2
            + [sds((per_core, 2 * block, hid), BF16)] * 2,
            8 * flops,
        )
        d_ffn = tp_sum(d_ffn + own + from_sibling(sib))
        g_sout = mm(d_branch, shared_hidden, TN)
        g_sin = jnp.stack([mm(ffn_in, d_gate, TN), mm(ffn_in, d_up, TN)])
        d_mixed, g_gain_b = norm_backward(
            d_ffn, mixed * inverse_b, inverse_b, gains[layers + at][None]
        )
        d_mixed = d_mixed + d_stream
        d_attn = d_mixed.astype(BF16)
        g_out = mm(d_attn, heads_out, TN)
        d_heads = mm(d_attn, w["out"]).astype(BF16)
        d_query, d_keys, d_values = attention_call(
            attend_back_kernel,
            base,
            path,
            (query, keys, values, d_heads),
            (rows_here, tree_len, tree_len),
            [pltpu.VMEM((tree_len, heads_width), F32)] * 2,
            10,
        )
        d_both = ctx_scatter(jnp.concatenate([d_keys, d_values], axis=1)).astype(BF16)
        d_parts = (d_query, d_both[:, :heads_width], d_both[:, heads_width:])
        d_normed = tp_sum(sum(mm(d, w["qkv"][part], NT) for part, d in enumerate(d_parts)))
        g_qkv = jnp.stack([mm(normed, d, TN) for d in d_parts])
        d_input, g_gain_a = norm_backward(
            d_normed, stream * inverse_a, inverse_a, gains[at][None]
        )
        d_stream = d_input + d_mixed
        grads[at] = (
            g_gain_a,
            g_gain_b,
            settle_plain(g_qkv, 1),
            settle_plain(g_out, 0),
            settle_plain(g_sin, 1),
            settle_plain(g_sout, 0),
            settle_experts(gin_near, gin_far, 2),
            settle_experts(gout_near, gout_far, 1),
        )
    member = lambda number: jnp.stack([grads[at][number] for at in range(layers)])
    gain_grads = settle_plain(jnp.concatenate([member(0), member(1)], axis=0), 1)
    return (
        result[None],
        to_relative(d_stream, block)[None],
        gain_grads[:layers],
        gain_grads[layers:],
        member(2).transpose(0, 2, 1, 3),
        member(3).transpose(0, 2, 1),
        member(4).transpose(0, 2, 1, 3),
        member(5).transpose(0, 2, 1),
        member(6).transpose(0, 1, 3, 2, 4),
        member(7).transpose(0, 1, 3, 2),
    )


def solution(mesh):
    return jax.shard_map(
        shards,
        mesh=mesh,
        in_specs=(
            P("fsdp", "ctx", None),
            P("fsdp", None),
            P("fsdp", "ctx", None),
            P("fsdp", "ctx", None),
            P(None, "fsdp"),
            P(None, "fsdp"),
            P(None, "fsdp", None, "tp"),
            P(None, "tp", "fsdp"),
            P(None, "fsdp", None, "tp"),
            P(None, "tp", "fsdp"),
            P(None, None, "fsdp", None, "tp"),
            P(None, None, "tp", "fsdp"),
            P("fsdp", "ctx", None),
        ),
        out_specs=(
            P("fsdp", "ctx", None),
            P("fsdp", "ctx", None),
            P(None, "fsdp"),
            P(None, "fsdp"),
            P(None, "fsdp", None, "tp"),
            P(None, "tp", "fsdp"),
            P(None, "fsdp", None, "tp"),
            P(None, "tp", "fsdp"),
            P(None, None, "fsdp", None, "tp"),
            P(None, None, "tp", "fsdp"),
        ),
        check_vma=False,
    )
```

time: 1710 us -> 942 us (0.55)
  waiting for transfers between devices: 1070 us -> 422 us
  matrix products: 185 us -> 49.2 us
  Pallas kernels: 0 us -> 116 us
  local copies, waits for them, and re-layouts: 198 us -> 87.7 us
  starting transfers between devices: 2.54 us -> 112 us
  blocking collectives: 123 us -> 22.6 us
  other arithmetic: 101 us -> 123 us
    reduce_scatter x14 -> x0, waiting for transfers between devices: 472 us -> none  [the longest x2 204 us: settle(): lax.psum_scatter(g_exin.astype(jnp.bfloat16), 'fsdp', scatter_dimension=1...]
    psum x8 -> x0, waiting for transfers between devices: 465 us -> none  [the longest x1 254 us: settle(): lax.psum(shares[2].astype(jnp.bfloat16), 'ctx').astype(jnp.float32)]
    ppermute x0 -> x115, waiting for transfers between devices: none -> 422 us  [swap(): return lax.ppermute(values, axis, [(k, k ^ mask) for k in range(count)])]
    dot_general x48 -> x45, matrix products: 183 us -> 49.2 us  [the longest x43 48.8 us: mm(): return lax.dot_general(a, b, dims, preferred_element_type=F32)]
    all_gather x6 -> x0, waiting for transfers between devices: 129 us -> none  [the longest x2 113 us: fetch(): lax.all_gather(ex_in, 'fsdp', axis=1, tiled=True)]
    pallas_call x0 -> x8, Pallas kernels: none -> 116 us  [the longest x4 81.7 us: experts_call(): pl.pallas_call(kernel, out_shape=shapes, grid_spec=pltpu.PrefetchScalarGr...]
    ppermute x0 -> x115, starting transfers between devices: none -> 103 us  [swap(): return lax.ppermute(values, axis, [(k, k ^ mask) for k in range(count)])]
    all_gather x10 -> x2, blocking collectives: 104 us -> 22.6 us  [shards(): lax.all_gather(jnp.concatenate([key, value], axis=1), 'ctx', axis=0, tile...]
  transfers between devices with their start and end apart: 30 -> 117, of which waited for: 21 -> 41; matrix products, arithmetic and copies ran while one was open for 16% -> 22% of each run, Pallas kernels for 0% -> 12%
where the time goes in v1:
time: 942 us; the launch traced here: 936 us
  waiting for transfers between devices  422 us (45%)
  other arithmetic  123 us (13%)
  Pallas kernels  116 us (12%)
  starting transfers between devices  112 us (12%)
  local copies, waits for them, and re-layouts  87.7 us (9%)
  matrix products  49.2 us (5%)
  blocking collectives  22.6 us (2%)
    ppermute x115, waiting for transfers between devices, swap(): return lax.ppermute(values, axis, [(k, k ^ mask) for k in range(count)])  422 us
    ppermute x115, starting transfers between devices, swap(): return lax.ppermute(values, axis, [(k, k ^ mask) for k in range(count)])  103 us
    pallas_call x4, Pallas kernels, experts_call(): pl.pallas_call(kernel, out_shape=shapes, grid_spec=pltpu.PrefetchScalarGr...  81.7 us
    dot_general x43, matrix products, mm(): return lax.dot_general(a, b, dims, preferred_element_type=F32)  48.8 us
    unnamed x345, local copies, waits for them, and re-layouts  45.6 us
    pallas_call x4, Pallas kernels, attention_call(): pl.pallas_call(kernel, out_shape=[jax.ShapeDtypeStruct((n, width), BF16)...  34.5 us
    all_gather x2, blocking collectives, shards(): lax.all_gather(jnp.concatenate([key, value], axis=1), 'ctx', axis=0, tile...  22.6 us
  transfers between devices with their start and end apart: 117, of which 41 were waited for; matrix products, arithmetic and copies ran while one was open for 22% of the time, Pallas kernels for 12%

profile of v1, /device:TPU:0, one launch (start us, length us, event | category | flops | bytes accessed | tf_op | source)
XLA Modules:
  0.0 935.7 jit_solution(15238845463708068931)
XLA Ops:
  26.7 60.9 %collective-permute-done.7 = bf16[192,192]{0,1:T(8,128)(2,1)} collective-permute-done((bf16[192,192]{0,1:T(8,128)(2,1)}, bf16[192,192]{0,1:T(8,128)(2,1)}, u32[]{:S(2)}, u32[]{:S(2)}) %collective-permute-start.7) | collective-permute-done | bytes 73760 | tf_op jit(solution)/shard_map/ppermute | solution.py:29
  90.4 12.4 %all_gather.6 = bf16[1024,384]{1,0:T(8,128)(2,1)S(1)} all-gather(bf16[512,384]{1,0:T(8,128)(2,1)S(1)} %pad_maximum_fusion.19), channel_id=1, replica_groups=mesh['fsdp'=4,'ctx'=2,'tp'=4] {'ctx'}, dimensions={0}, use_global_device_ids=true | all-gather | bytes 1179648 | tf_op jit(solution)/shard_map/all_gather | solution.py:420
  127.7 16.1 %collective-permute-done.10 = bf16[256,768]{1,0:T(8,128)(2,1)S(1)} collective-permute-done((bf16[256,768]{1,0:T(8,128)(2,1)S(1)}, bf16[256,768]{1,0:T(8,128)(2,1)S(1)}, u32[]{:S(2)}, u32[]{:S(2)}) %collective-permute-start.10) | collective-permute-done | bytes 393248 | tf_op jit(solution)/shard_map/ppermute | solution.py:29
  181.2 17.2 %shard_map.205 = (f32[512,768]{1,0:T(8,128)}, bf16[512,768]{1,0:T(8,128)(2,1)}, bf16[4,384,768]{2,1,0:T(8,128)(2,1)}, f32[4,384,512]{2,1,0:T(8,128)}, f32[4,384,512]{2,1,0:T(8,128)}) custom-call(s32[1]{0:T(128)} %bitcast.27.core_ref, bf16[1024,768]{1,0:T(8,128)(2,1)} %maximum_maximum_fusion.tok_ref, s32[4,1,1024]{2,1,0:T(1,128)} %copy.100.row_ref, ...), custom_call_target="tpu_custom_call" | custom-call | flops 6039797760 | bytes 22020096 | tf_op jit(solution)/shard_map/pallas_call | solution.py:292
  206.8 9.7 %collective-permute-done.27 = bf16[256,768]{1,0:T(8,128)(2,1)S(1)} collective-permute-done((bf16[256,768]{1,0:T(8,128)(2,1)S(1)}, bf16[256,768]{1,0:T(8,128)(2,1)S(1)}, u32[]{:S(2)}, u32[]{:S(2)}) %collective-permute-start.27) | collective-permute-done | bytes 393248 | tf_op jit(solution)/shard_map/ppermute | solution.py:29
  256.4 10.2 %all_gather.7 = bf16[1024,384]{1,0:T(8,128)(2,1)S(1)} all-gather(bf16[512,384]{1,0:T(8,128)(2,1)S(1)} %pad_maximum_fusion.20), channel_id=1, replica_groups=mesh['fsdp'=4,'ctx'=2,'tp'=4] {'ctx'}, dimensions={0}, use_global_device_ids=true | all-gather | bytes 1179648 | tf_op jit(solution)/shard_map/all_gather | solution.py:420
  294.4 23.5 %collective-permute-done.40 = bf16[2,192,512]{2,1,0:T(8,128)(2,1)} collective-permute-done((bf16[2,192,512]{2,1,0:T(8,128)(2,1)}, bf16[2,192,512]{2,1,0:T(8,128)(2,1)}, u32[]{:S(2)}, u32[]{:S(2)}) %collective-permute-start.40) | collective-permute-done | bytes 393248 | tf_op jit(solution)/shard_map/ppermute | solution.py:29
  343.3 18.4 %collective-permute-done.50.refs_6_ = bf16[8,192,512]{2,1,0:T(8,128)(2,1)S(1)} collective-permute-done((bf16[8,192,512]{2,1,0:T(8,128)(2,1)S(1)}, bf16[8,192,512]{2,1,0:T(8,128)(2,1)S(1)}, u32[]{:S(2)}, u32[]{:S(2)}) %collective-permute-start.50) | collective-permute-done | bytes 1572896 | tf_op jit(solution)/shard_map/ppermute | solution.py:29
  379.2 17.2 %shard_map.207 = (f32[512,768]{1,0:T(8,128)}, bf16[512,768]{1,0:T(8,128)(2,1)}, bf16[4,384,768]{2,1,0:T(8,128)(2,1)}, f32[4,384,512]{2,1,0:T(8,128)}, f32[4,384,512]{2,1,0:T(8,128)}) custom-call(s32[1]{0:T(128)} %bitcast.27.core_ref, bf16[1024,768]{1,0:T(8,128)(2,1)} %maximum_maximum_fusion.1.tok_ref, s32[4,1,1024]{2,1,0:T(1,128)} %copy.100.row_ref, ...), custom_call_target="tpu_custom_call" | custom-call | flops 6039797760 | bytes 22020096 | tf_op jit(solution)/shard_map/pallas_call | solution.py:292
  396.5 23.7 %shard_map.208 = (f32[512,768]{1,0:T(8,128)}, bf16[512,768]{1,0:T(8,128)(2,1)}, bf16[4,2,384,512]{3,2,1,0:T(8,128)(2,1)}, bf16[4,2,384,512]{3,2,1,0:T(8,128)(2,1...) custom-call(s32[1]{0:T(128)} %bitcast.27.core_ref, bf16[1024,768]{1,0:T(8,128)(2,1)} %maximum_maximum_fusion.2.d_ref, ...), custom_call_target="tpu_custom_call" | custom-call | flops 9663676416 | bytes 31457280 | tf_op jit(solution)/shard_map/pallas_call | solution.py:292
  446.2 10.7 %collective-permute-done.53 = bf16[256,768]{1,0:T(8,128)(2,1)S(1)} collective-permute-done((bf16[256,768]{1,0:T(8,128)(2,1)S(1)}, bf16[256,768]{1,0:T(8,128)(2,1)S(1)}, u32[]{:S(2)}, u32[]{:S(2)}) %collective-permute-start.53) | collective-permute-done | bytes 393248 | tf_op jit(solution)/shard_map/ppermute | solution.py:29
  457.1 12.8 %collective-permute-done.59 = bf16[256,768]{1,0:T(8,128)(2,1)S(1)} collective-permute-done((bf16[256,768]{1,0:T(8,128)(2,1)S(1)}, bf16[256,768]{1,0:T(8,128)(2,1)S(1)}, u32[]{:S(2)}, u32[]{:S(2)}) %collective-permute-start.59) | collective-permute-done | bytes 393248 | tf_op jit(solution)/shard_map/ppermute | solution.py:29
  502.1 10.4 %shard_map.209 = (bf16[512,192]{1,0:T(8,128)(2,1)}, bf16[1024,192]{1,0:T(8,128)(2,1)}, bf16[1024,192]{1,0:T(8,128)(2,1)}) custom-call(s32[1]{0:T(128)} %bitcast.1.base_ref, f32[1,1024]{1,0:T(1,128)} %bitcast.331, bf16[512,192]{1,0:T(8,128)(2,1)} %convolution_convert_fusion.16.q_ref, bf16[1024,192]{1,0:T(8,128)(2,1)} %get-tuple-element.221.k_ref, ...), custom_call_target="tpu_custom_call" | custom-call | flops 1006632960 | bytes 1966080 | tf_op jit(solution)/shard_map/pallas_call | solution.py:178
  557.9 12.1 %collective-permute-done.62 = bf16[256,768]{1,0:T(8,128)(2,1)S(1)} collective-permute-done((bf16[256,768]{1,0:T(8,128)(2,1)S(1)}, bf16[256,768]{1,0:T(8,128)(2,1)S(1)}, u32[]{:S(2)}, u32[]{:S(2)}) %collective-permute-start.62) | collective-permute-done | bytes 393248 | tf_op jit(solution)/shard_map/ppermute | solution.py:29
  601.5 25.1 %collective-permute-done.78 = bf16[3,384,192]{1,2,0:T(8,128)(2,1)S(1)} collective-permute-done((bf16[3,384,192]{1,2,0:T(8,128)(2,1)S(1)}, bf16[3,384,192]{1,2,0:T(8,128)(2,1)S(1)}, u32[]{:S(2)}, u32[]{:S(2)}) %collective-permute-start.78) | collective-permute-done | bytes 442400 | tf_op jit(solution)/shard_map/ppermute | solution.py:29
  632.6 23.6 %shard_map.210 = (f32[512,768]{1,0:T(8,128)}, bf16[512,768]{1,0:T(8,128)(2,1)}, bf16[4,2,384,512]{3,2,1,0:T(8,128)(2,1)}, bf16[4,2,384,512]{3,2,1,0:T(8,128)(2,1...) custom-call(s32[1]{0:T(128)} %bitcast.27.core_ref, bf16[1024,768]{1,0:T(8,128)(2,1)} %maximum_maximum_fusion.3.d_ref, ...), custom_call_target="tpu_custom_call" | custom-call | flops 9663676416 | bytes 31457280 | tf_op jit(solution)/shard_map/pallas_call | solution.py:292
  670.3 38.8 %collective-permute-done.89 = bf16[2,192,512]{2,1,0:T(8,128)(2,1)S(1)} collective-permute-done((bf16[2,192,512]{2,1,0:T(8,128)(2,1)S(1)}, bf16[2,192,512]{2,1,0:T(8,128)(2,1)S(1)}, u32[]{:S(2)}, u32[]{:S(2)}) %collective-permute-start.89) | collective-permute-done | bytes 393248 | tf_op jit(solution)/shard_map/ppermute | solution.py:29
  718.4 12.4 %collective-permute-done.67 = bf16[256,768]{1,0:T(8,128)(2,1)S(1)} collective-permute-done((bf16[256,768]{1,0:T(8,128)(2,1)S(1)}, bf16[256,768]{1,0:T(8,128)(2,1)S(1)}, u32[]{:S(2)}, u32[]{:S(2)}) %collective-permute-start.67) | collective-permute-done | bytes 393248 | tf_op jit(solution)/shard_map/ppermute | solution.py:29
  751.1 10.6 %shard_map.211 = (bf16[512,192]{1,0:T(8,128)(2,1)}, bf16[1024,192]{1,0:T(8,128)(2,1)}, bf16[1024,192]{1,0:T(8,128)(2,1)}) custom-call(s32[1]{0:T(128)} %bitcast.1.base_ref, f32[1,1024]{1,0:T(1,128)} %bitcast.332, bf16[512,192]{1,0:T(8,128)(2,1)} %convolution_convert_fusion.17.q_ref, bf16[1024,192]{1,0:T(8,128)(2,1)} %get-tuple-element.235.k_ref, ...), custom_call_target="tpu_custom_call" | custom-call | flops 1006632960 | bytes 1966080 | tf_op jit(solution)/shard_map/pallas_call | solution.py:178
  771.2 10.5 %collective-permute-done.81 = bf16[384,192]{0,1:T(8,128)(2,1)} collective-permute-done((bf16[384,192]{0,1:T(8,128)(2,1)}, bf16[384,192]{0,1:T(8,128)(2,1)}, u32[]{:S(2)}, u32[]{:S(2)}) %collective-permute-start.81) | collective-permute-done | bytes 147488 | tf_op jit(solution)/shard_map/ppermute | solution.py:29
  813.6 11.9 %collective-permute-done.70 = bf16[256,768]{1,0:T(8,128)(2,1)S(1)} collective-permute-done((bf16[256,768]{1,0:T(8,128)(2,1)S(1)}, bf16[256,768]{1,0:T(8,128)(2,1)S(1)}, u32[]{:S(2)}, u32[]{:S(2)}) %collective-permute-start.70) | collective-permute-done | bytes 393248 | tf_op jit(solution)/shard_map/ppermute | solution.py:29
  855.2 40.2 %collective-permute-done.74 = bf16[4,192]{1,0:T(4,128)(2,1)S(1)} collective-permute-done((bf16[4,192]{1,0:T(4,128)(2,1)S(1)}, bf16[4,192]{1,0:T(4,128)(2,1)S(1)}, u32[]{:S(2)}, u32[]{:S(2)}) %collective-permute-start.74) | collective-permute-done | bytes 1568 | tf_op jit(solution)/shard_map/ppermute | solution.py:29
  903.9 9.3 maximum_bitcast_fusion
  913.2 22.1 %copy.117 = f32[2,8,192,2,512]{4,3,2,1,0:T(2,128)} copy(f32[2,8,192,2,512]{4,2,3,1,0:T(8,128)} %maximum_bitcast_fusion) | data formatting | bytes 25165824
  (799 shorter events, 471.9 us)
Async XLA Ops:
  5.5 82.1 %collective-permute-start.3 = (bf16[3,192,192]{2,1,0:T(8,128)(2,1)}, bf16[3,192,192]{2,1,0:T(8,128)(2,1)}, u32[]{:S(2)}, u32[]{:S(2)}) collective-permute-start(bf16[3,192,192]{2,1,0:T(8,128)(2,1)} %get-tuple-element.249), channel_id=1, source_target_pairs={{0,8},{8,0},{16,24},{24,16},{1,9},{9,1},{17,25},{25,17},{2,10},{10... | collective-permute-start | bytes 663560 | tf_op jit(solution)/shard_map/ppermute | solution.py:29
  14.9 112.3 %collective-permute-start.21 = (bf16[8,2,192,512]{3,2,1,0:T(8,128)(2,1)}, bf16[8,2,192,512]{3,2,1,0:T(8,128)(2,1)}, u32[]{:S(2)}, u32[]{:S(2)}) collective-permute-start(bf16[8,2,192,512]{3,2,1,0:T(8,128)(2,1)} %get-tuple-element.135.refs_0_), channel_id=1, source_target_pairs={{0,16},{8,24},{16,0},{24,8},{1,17},{9,25},{17,1},{25,9},{2,18},{10... | collective-permute-start | bytes 9437192 | tf_op jit(solution)/shard_map/ppermute | solution.py:29
  24.4 63.2 %collective-permute-start.7 = (bf16[192,192]{0,1:T(8,128)(2,1)}, bf16[192,192]{0,1:T(8,128)(2,1)}, u32[]{:S(2)}, u32[]{:S(2)}) collective-permute-start(bf16[192,192]{0,1:T(8,128)(2,1)} %get-tuple-element.253), channel_id=1, source_target_pairs={{0,16},{8,24},{16,0},{24,8},{1,17},{9,25},{17,1},{25,9},{2,18},{10... | collective-permute-start | bytes 221192 | tf_op jit(solution)/shard_map/ppermute | solution.py:29
  24.8 87.0 %collective-permute-start.6 = (bf16[192,192]{0,1:T(8,128)(2,1)}, bf16[192,192]{0,1:T(8,128)(2,1)}, u32[]{:S(2)}, u32[]{:S(2)}) collective-permute-start(bf16[192,192]{0,1:T(8,128)(2,1)} %get-tuple-element.253), channel_id=1, source_target_pairs={{0,8},{8,0},{16,24},{24,16},{1,9},{9,1},{17,25},{25,17},{2,10},{10... | collective-permute-start | bytes 221192 | tf_op jit(solution)/shard_map/ppermute | solution.py:29
  25.0 62.6 %collective-permute-start.5 = (bf16[3,192,192]{2,1,0:T(8,128)(2,1)}, bf16[3,192,192]{2,1,0:T(8,128)(2,1)S(1)}, u32[]{:S(2)}, u32[]{:S(2)}) collective-permute-start(bf16[3,192,192]{2,1,0:T(8,128)(2,1)} %collective-permute-done.4), channel_id=1, source_target_pairs={{0,8},{8,0},{16,24},{24,16},{1,9},{9,1},{17,25},{25,17},{2,10},{10... | collective-permute-start | bytes 663560 | tf_op jit(solution)/shard_map/ppermute | solution.py:29
  127.2 53.6 %collective-permute-start.20 = (bf16[8,2,192,512]{3,2,1,0:T(8,128)(2,1)}, bf16[8,2,192,512]{3,2,1,0:T(8,128)(2,1)}, u32[]{:S(2)}, u32[]{:S(2)}) collective-permute-start(bf16[8,2,192,512]{3,2,1,0:T(8,128)(2,1)} %get-tuple-element.135.refs_0_), channel_id=1, source_target_pairs={{0,8},{8,0},{16,24},{24,16},{1,9},{9,1},{17,25},{25,17},{2,10},{10... | collective-permute-start | bytes 9437192 | tf_op jit(solution)/shard_map/ppermute | solution.py:29
  127.2 54.0 %collective-permute-start.22 = (bf16[8,2,192,512]{3,2,1,0:T(8,128)(2,1)}, bf16[8,2,192,512]{3,2,1,0:T(8,128)(2,1)}, u32[]{:S(2)}, u32[]{:S(2)}) collective-permute-start(bf16[8,2,192,512]{3,2,1,0:T(8,128)(2,1)} %collective-permute-done.21.refs_2_), channel_id=1, source_target_pairs={{0,8},{8,0},{16,24},{24,16},{1,9},{9,1},{17,25},{25,17},{2,10},{10... | collective-permute-start | bytes 9437192 | tf_op jit(solution)/shard_map/ppermute | solution.py:29
  222.1 54.7 %collective-permute-start.33 = (bf16[192,192]{0,1:T(8,128)(2,1)}, bf16[192,192]{0,1:T(8,128)(2,1)}, u32[]{:S(2)}, u32[]{:S(2)}) collective-permute-start(bf16[192,192]{0,1:T(8,128)(2,1)} %get-tuple-element.252), channel_id=1, source_target_pairs={{0,8},{8,0},{16,24},{24,16},{1,9},{9,1},{17,25},{25,17},{2,10},{10... | collective-permute-start | bytes 221192 | tf_op jit(solution)/shard_map/ppermute | solution.py:29
  239.4 85.8 %collective-permute-start.47 = (bf16[8,2,192,512]{3,2,1,0:T(8,128)(2,1)}, bf16[8,2,192,512]{3,2,1,0:T(8,128)(2,1)}, u32[]{:S(2)}, u32[]{:S(2)}) collective-permute-start(bf16[8,2,192,512]{3,2,1,0:T(8,128)(2,1)} %get-tuple-element.134.refs_0_), channel_id=1, source_target_pairs={{0,16},{8,24},{16,0},{24,8},{1,17},{9,25},{17,1},{25,9},{2,18},{10... | collective-permute-start | bytes 9437192 | tf_op jit(solution)/shard_map/ppermute | solution.py:29
  322.5 55.5 %collective-permute-start.46 = (bf16[8,2,192,512]{3,2,1,0:T(8,128)(2,1)}, bf16[8,2,192,512]{3,2,1,0:T(8,128)(2,1)}, u32[]{:S(2)}, u32[]{:S(2)}) collective-permute-start(bf16[8,2,192,512]{3,2,1,0:T(8,128)(2,1)} %get-tuple-element.134.refs_0_), channel_id=1, source_target_pairs={{0,8},{8,0},{16,24},{24,16},{1,9},{9,1},{17,25},{25,17},{2,10},{10... | collective-permute-start | bytes 9437192 | tf_op jit(solution)/shard_map/ppermute | solution.py:29
  376.5 48.4 %collective-permute-start.98 = (bf16[192,512]{1,0:T(8,128)(2,1)}, bf16[192,512]{1,0:T(8,128)(2,1)}, u32[]{:S(2)}, u32[]{:S(2)}) collective-permute-start(bf16[192,512]{1,0:T(8,128)(2,1)} %add_convert_fusion.42), channel_id=1, source_target_pairs={{0,4},{4,0},{1,5},{5,1},{2,6},{6,2},{3,7},{7,3},{8,12},{12,8},{9,1... | collective-permute-start | bytes 589832 | tf_op jit(solution)/shard_map/ppermute | solution.py:29
  423.4 50.1 %collective-permute-start.111 = (bf16[4,384,512]{2,1,0:T(8,128)(2,1)S(1)}, bf16[4,384,512]{2,1,0:T(8,128)(2,1)S(1)}, u32[]{:S(2)}, u32[]{:S(2)}) collective-permute-start(bf16[4,384,512]{2,1,0:T(8,128)(2,1)S(1)} %copy-done.143), channel_id=1, source_target_pairs={{0,16},{8,24},{16,0},{24,8},{1,17},{9,25},{17,1},{25,9},{2,18},{10... | collective-permute-start | bytes 4718600 | tf_op jit(solution)/shard_map/ppermute | solution.py:29
  424.9 146.0 %collective-permute-start.103 = (bf16[4,2,384,512]{3,2,1,0:T(8,128)(2,1)}, bf16[4,2,384,512]{3,2,1,0:T(8,128)(2,1)}, u32[]{:S(2)}, u32[]{:S(2)}) collective-permute-start(bf16[4,2,384,512]{3,2,1,0:T(8,128)(2,1)} %get-tuple-element.61), channel_id=1, source_target_pairs={{0,16},{8,24},{16,0},{24,8},{1,17},{9,25},{17,1},{25,9},{2,18},{10... | collective-permute-start | bytes 9437192 | tf_op jit(solution)/shard_map/ppermute | solution.py:29
  475.1 80.9 %collective-permute-start.113 = (bf16[4,192,512]{2,1,0:T(8,128)(2,1)}, bf16[4,192,512]{2,1,0:T(8,128)(2,1)}, u32[]{:S(2)}, u32[]{:S(2)}) collective-permute-start(bf16[4,192,512]{2,1,0:T(8,128)(2,1)} %get-tuple-element.142), channel_id=1, source_target_pairs={{0,8},{8,0},{16,24},{24,16},{1,9},{9,1},{17,25},{25,17},{2,10},{10... | collective-permute-start | bytes 2359304 | tf_op jit(solution)/shard_map/ppermute | solution.py:29
  475.1 101.1 %collective-permute-start.112 = (bf16[4,192,512]{2,1,0:T(8,128)(2,1)}, bf16[4,192,512]{2,1,0:T(8,128)(2,1)}, u32[]{:S(2)}, u32[]{:S(2)}) collective-permute-start(bf16[4,192,512]{2,1,0:T(8,128)(2,1)} %get-tuple-element.143), channel_id=1, source_target_pairs={{0,4},{4,0},{1,5},{5,1},{2,6},{6,2},{3,7},{7,3},{8,12},{12,8},{9,1... | collective-permute-start | bytes 2359304 | tf_op jit(solution)/shard_map/ppermute | solution.py:29
  575.0 86.4 %collective-permute-start.105 = (bf16[4,2,192,512]{3,2,1,0:T(8,128)(2,1)}, bf16[4,2,192,512]{3,2,1,0:T(8,128)(2,1)}, u32[]{:S(2)}, u32[]{:S(2)}) collective-permute-start(bf16[4,2,192,512]{3,2,1,0:T(8,128)(2,1)} %get-tuple-element.132), channel_id=1, source_target_pairs={{0,8},{8,0},{16,24},{24,16},{1,9},{9,1},{17,25},{25,17},{2,10},{10... | collective-permute-start | bytes 4718600 | tf_op jit(solution)/shard_map/ppermute | solution.py:29
  575.0 157.2 %collective-permute-start.104 = (bf16[4,2,192,512]{3,2,1,0:T(8,128)(2,1)S(1)}, bf16[4,2,192,512]{3,2,1,0:T(8,128)(2,1)}, u32[]{:S(2)}, u32[]{:S(2)}) collective-permute-start(bf16[4,2,192,512]{3,2,1,0:T(8,128)(2,1)S(1)} %get-tuple-element.133), channel_id=1, source_target_pairs={{0,4},{4,0},{1,5},{5,1},{2,6},{6,2},{3,7},{7,3},{8,12},{12,8},{9,1... | collective-permute-start | bytes 4718600 | tf_op jit(solution)/shard_map/ppermute | solution.py:29
  661.4 55.4 %collective-permute-start.107 = (bf16[4,384,512]{2,1,0:T(8,128)(2,1)S(1)}, bf16[4,384,512]{2,1,0:T(8,128)(2,1)S(1)}, u32[]{:S(2)}, u32[]{:S(2)}) collective-permute-start(bf16[4,384,512]{2,1,0:T(8,128)(2,1)S(1)} %copy-done.144), channel_id=1, source_target_pairs={{0,16},{8,24},{16,0},{24,8},{1,17},{9,25},{17,1},{25,9},{2,18},{10... | collective-permute-start | bytes 4718600 | tf_op jit(solution)/shard_map/ppermute | solution.py:29
  662.9 69.5 %collective-permute-start.106 = (bf16[4,2,192,512]{3,2,1,0:T(8,128)(2,1)}, bf16[4,2,192,512]{3,2,1,0:T(8,128)(2,1)S(1)}, u32[]{:S(2)}, u32[]{:S(2)}) collective-permute-start(bf16[4,2,192,512]{3,2,1,0:T(8,128)(2,1)} %collective-permute-done.105), channel_id=1, source_target_pairs={{0,4},{4,0},{1,5},{5,1},{2,6},{6,2},{3,7},{7,3},{8,12},{12,8},{9,1... | collective-permute-start | bytes 4718600 | tf_op jit(solution)/shard_map/ppermute | solution.py:29
  709.1 99.9 %collective-permute-start.99 = (bf16[4,2,384,512]{3,2,1,0:T(8,128)(2,1)}, bf16[4,2,384,512]{3,2,1,0:T(8,128)(2,1)}, u32[]{:S(2)}, u32[]{:S(2)}) collective-permute-start(bf16[4,2,384,512]{3,2,1,0:T(8,128)(2,1)} %get-tuple-element.59), channel_id=1, source_target_pairs={{0,16},{8,24},{16,0},{24,8},{1,17},{9,25},{17,1},{25,9},{2,18},{10... | collective-permute-start | bytes 9437192 | tf_op jit(solution)/shard_map/ppermute | solution.py:29
  718.4 78.2 %collective-permute-start.109 = (bf16[4,192,512]{2,1,0:T(8,128)(2,1)}, bf16[4,192,512]{2,1,0:T(8,128)(2,1)}, u32[]{:S(2)}, u32[]{:S(2)}) collective-permute-start(bf16[4,192,512]{2,1,0:T(8,128)(2,1)} %get-tuple-element.138), channel_id=1, source_target_pairs={{0,8},{8,0},{16,24},{24,16},{1,9},{9,1},{17,25},{25,17},{2,10},{10... | collective-permute-start | bytes 2359304 | tf_op jit(solution)/shard_map/ppermute | solution.py:29
  730.8 96.3 %collective-permute-start.108 = (bf16[4,192,512]{2,1,0:T(8,128)(2,1)}, bf16[4,192,512]{2,1,0:T(8,128)(2,1)}, u32[]{:S(2)}, u32[]{:S(2)}) collective-permute-start(bf16[4,192,512]{2,1,0:T(8,128)(2,1)} %get-tuple-element.139), channel_id=1, source_target_pairs={{0,4},{4,0},{1,5},{5,1},{2,6},{6,2},{3,7},{7,3},{8,12},{12,8},{9,1... | collective-permute-start | bytes 2359304 | tf_op jit(solution)/shard_map/ppermute | solution.py:29
  825.5 70.5 %collective-permute-start.100 = (bf16[4,2,192,512]{3,2,1,0:T(8,128)(2,1)}, bf16[4,2,192,512]{3,2,1,0:T(8,128)(2,1)}, u32[]{:S(2)}, u32[]{:S(2)}) collective-permute-start(bf16[4,2,192,512]{3,2,1,0:T(8,128)(2,1)} %get-tuple-element.129), channel_id=1, source_target_pairs={{0,4},{4,0},{1,5},{5,1},{2,6},{6,2},{3,7},{7,3},{8,12},{12,8},{9,1... | collective-permute-start | bytes 4718600 | tf_op jit(solution)/shard_map/ppermute | solution.py:29
  846.0 50.0 %collective-permute-start.102 = (bf16[4,2,192,512]{3,2,1,0:T(8,128)(2,1)}, bf16[4,2,192,512]{3,2,1,0:T(8,128)(2,1)S(1)}, u32[]{:S(2)}, u32[]{:S(2)}) collective-permute-start(bf16[4,2,192,512]{3,2,1,0:T(8,128)(2,1)} %collective-permute-done.101), channel_id=1, source_target_pairs={{0,4},{4,0},{1,5},{5,1},{2,6},{6,2},{3,7},{7,3},{8,12},{12,8},{9,1... | collective-permute-start | bytes 4718600 | tf_op jit(solution)/shard_map/ppermute | solution.py:29
  (262 other events, 3303.6 us)

commit v2 on v1

v2 whole, which is shorter than its diff:
```python
import functools

import jax
import jax.numpy as jnp
from jax import lax
from jax.experimental import pallas as pl
from jax.experimental.pallas import tpu as pltpu
from jax.sharding import PartitionSpec as P

HEAD_DIM = 64
EPS = 1e-06
SCALE = 0.125
MASKED = -1000000000.0
F32 = jnp.float32
BF16 = jnp.bfloat16
MIB = 1 << 20
LIGHT = 1000
KEYS, QUERY, OUT, GAINS, PACK = 0, 384, 640, 832, 896

NN = (((1,), (0,)), ((), ()))
NT = (((1,), (1,)), ((), ()))
TN = (((0,), (0,)), ((), ()))


def mm(a, b, dims=NN):
    return lax.dot_general(a, b, dims, preferred_element_type=F32)


def sds(shape, dtype):
    return jax.ShapeDtypeStruct(tuple(shape), dtype)


def swap(values, axis, mask):
    count = lax.axis_size(axis)
    return lax.ppermute(values, axis, [(k, k ^ mask) for k in range(count)])


def after(value, dep):
    return lax.optimization_barrier((value, dep))[0]


def add(a, b):
    return (a.astype(F32) + b.astype(F32)).astype(BF16)


def gather_blocks(values):
    far = swap(values, "fsdp", 2)
    return [values, swap(values, "fsdp", 1), far, swap(far, "fsdp", 1)]


def tp_sum(halves, between):
    count = lax.axis_size("tp")
    chunks = len(halves) // 2
    totals = [add(k, swap(g, "tp", 1)) for k, g in zip(halves[:chunks], halves[chunks:])]
    totals = between(*totals)
    step = 2
    while step < count:
        totals = [add(total, swap(total, "tp", step)) for total in totals]
        step *= 2
    return list(totals) + [swap(total, "tp", 1) for total in totals]


def ctx_last(part):
    count = lax.axis_size("ctx")
    step = 1
    while step * 2 < count:
        part = add(part, swap(part, "ctx", step))
        step *= 2
    return part, swap(part, "ctx", step)


def call(kernel, scal, grid, ins, outs, scratch=(), flops=0, exps=0, alias=None, limit=32):
    def spec(item):
        shape, block, index = item[0].shape, item[1], item[2]
        if block == "any":
            return pl.BlockSpec(memory_space=pl.ANY)
        if block is None:
            return pl.BlockSpec(shape, lambda *_: (0,) * len(shape))
        return pl.BlockSpec(block, index)

    size = lambda a: a.size * a.dtype.itemsize
    moved = sum(size(i[0]) for i in list(ins) + list(outs) if i[1] != "any" and len(i) < 4)
    moved += sum(i[3] for i in list(ins) + list(outs) if len(i) > 3)
    return pl.pallas_call(
        kernel,
        out_shape=[o[0] for o in outs],
        grid_spec=pltpu.PrefetchScalarGridSpec(
            num_scalar_prefetch=1,
            grid=grid,
            in_specs=[spec(i) for i in ins],
            out_specs=[spec(o) for o in outs],
            scratch_shapes=list(scratch),
        ),
        compiler_params=pltpu.CompilerParams(
            dimension_semantics=("arbitrary",) * len(grid), vmem_limit_bytes=limit * MIB
        ),
        cost_estimate=pl.CostEstimate(flops=flops // LIGHT, transcendentals=0, bytes_accessed=moved // LIGHT),
        input_output_aliases=alias or {},
    )(scal, *[i[0] for i in ins])


def whole(a):
    return (a, None, None)


def tiled(a):
    return (a, (a.shape[0] // 2,) + a.shape[1:], lambda t, *_: (t,) + (0,) * (len(a.shape) - 1))


def joined(refs, *at):
    return jnp.concatenate([ref[at] if at else ref[...] for ref in refs], axis=0)


def gain_row(pack_refs, which):
    cols = jnp.concatenate([ref[:, GAINS - 64 : PACK] for ref in pack_refs], axis=0)
    at = lax.broadcasted_iota(jnp.int32, (8, 128), 1)
    pick = jnp.where(at == 64 + which, 1.0, 0.0).astype(BF16)
    return mm(pick, cols, NT)[:1]


def swap_pairs(values, block):
    two = 2 * block
    return jnp.concatenate(
        [pltpu.roll(values[:, at : at + two], block, 1) for at in (0, two)], axis=1
    )


def relative(values, me, block):
    two = 2 * block
    far = jnp.concatenate([values[:, two:], values[:, :two]], axis=1)
    values = jnp.where((me & 2) > 0, far, values)
    return jnp.where((me & 1) > 0, swap_pairs(values, block), values)


def arrived(bit, refs):
    chunks = len(refs) // 2
    mine, other = joined(refs[:chunks]), joined(refs[chunks:])
    return jnp.where(pl.program_id(0) == bit, mine, other).astype(F32)


def put_halves(tile, bit, values, refs):
    chunks = len(refs) // 2
    rows = values.shape[0] // chunks
    values = values.astype(BF16)

    @pl.when(tile == bit)
    def _():
        for at in range(chunks):
            refs[at][...] = values[at * rows : (at + 1) * rows]

    @pl.when(tile != bit)
    def _():
        for at in range(chunks):
            refs[chunks + at][...] = values[at * rows : (at + 1) * rows]


def half_shapes(rows, width, chunks):
    return [whole(sds((rows // 2 // chunks, width), BF16)) for _ in range(2 * chunks)]


def normed_of(values, gain):
    inverse = lax.rsqrt(jnp.mean(values * values, axis=-1, keepdims=True) + EPS)
    scaled = values * inverse
    return scaled, inverse, scaled * gain


def norm_back(d_normed, values, gain):
    scaled, inverse, _ = normed_of(values, gain)
    d_scaled = d_normed * gain
    mean = jnp.mean(d_scaled * scaled, axis=-1, keepdims=True)
    return inverse * (d_scaled - scaled * mean), jnp.sum(d_normed * scaled, axis=0, keepdims=True)


def order_kernel(scal, tok_ref, cot_ref, tok_out, cot_out, *, block):
    for src, dst in ((tok_ref, tok_out), (cot_ref, cot_out)):
        dst[...] = relative(src[...].astype(F32), scal[0], block).astype(BF16)


def project(stream, packs, normed_ref, q_ref, kv_ref):
    _, _, normed = normed_of(stream, gain_row(packs, 0))
    normed = normed.astype(BF16)
    normed_ref[...] = normed
    weight = joined(packs)
    kv_ref[...] = mm(normed, weight[:, KEYS:QUERY]).astype(BF16)
    q_ref[...] = mm(normed, weight[:, QUERY : QUERY + q_ref.shape[1]]).astype(BF16)


def first_kernel(scal, tok_ref, *refs):
    project(tok_ref[...].astype(F32), refs[:4], *refs[4:])


def next_kernel(scal, mixed_ref, *refs, parts):
    stream = mixed_ref[...] + arrived(scal[1], refs[:parts])
    packs, (stream_ref, *outs) = refs[parts : parts + 4], refs[parts + 4 :]
    stream_ref[...] = stream
    project(stream, packs, *outs)


def last_kernel(scal, mixed_ref, *refs, block):
    result = mixed_ref[...] + arrived(scal[1], refs[:-1])
    refs[-1][...] = relative(result, scal[0], block).astype(BF16)


def allowed_of(scal, path_ref, rows, tree_len):
    first = scal[3] + pl.program_id(0) * rows
    query_pos = first + lax.broadcasted_iota(jnp.int32, (rows, tree_len), 0)
    key_pos = lax.broadcasted_iota(jnp.int32, (rows, tree_len), 1)
    return (key_pos <= query_pos) & (path_ref[...] > 0.5)


def softmax_of(query, key, allowed):
    scores = jnp.where(allowed, mm(query, key, NT) * SCALE, MASKED)
    expo = jnp.exp(scores - jnp.max(scores, axis=-1, keepdims=True))
    return expo * (1.0 / jnp.sum(expo, axis=-1, keepdims=True))


def head_cols(width):
    return [slice(at, at + HEAD_DIM) for at in range(0, width, HEAD_DIM)]


def attend_kernel(scal, path_ref, q_ref, kv_ref, *refs):
    packs, heads_ref, halves = refs[:4], refs[4], refs[5:]
    rows, width = q_ref.shape
    allowed = allowed_of(scal, path_ref, rows, kv_ref.shape[0])
    outs = []
    for cols in head_cols(width):
        vals = slice(width + cols.start, width + cols.stop)
        probs = softmax_of(q_ref[:, cols], kv_ref[:, cols], allowed).astype(BF16)
        outs.append(mm(probs, kv_ref[:, vals]))
    heads = jnp.concatenate(outs, axis=1).astype(BF16)
    heads_ref[...] = heads
    weight = jnp.concatenate([ref[:, OUT : OUT + width] for ref in packs], axis=0)
    put_halves(pl.program_id(0), scal[1], mm(heads, weight, NT), halves)


def attend_back_kernel(scal, path_ref, q_ref, kv_ref, d_ref, heads_ref, *refs):
    packs, (dq_ref, gout_ref), (dkv_refs, scratch) = refs[:4], refs[4:6], (refs[6:-2], refs[-2:])
    dkv_acc, gout_acc = scratch
    rows, width = q_ref.shape
    tile = pl.program_id(0)
    allowed = allowed_of(scal, path_ref, rows, kv_ref.shape[0])

    @pl.when(tile == 0)
    def _():
        dkv_acc[...] = jnp.zeros_like(dkv_acc)
        gout_acc[...] = jnp.zeros_like(gout_acc)

    weight = jnp.concatenate([ref[:, OUT : OUT + width] for ref in packs], axis=0)
    d_heads = mm(d_ref[...], weight).astype(BF16)
    gout_acc[...] += mm(d_ref[...], heads_ref[...], TN)
    dqs, dks, dvs = [], [], []
    for cols in head_cols(width):
        vals = slice(width + cols.start, width + cols.stop)
        query, key, value, d_out = q_ref[:, cols], kv_ref[:, cols], kv_ref[:, vals], d_heads[:, cols]
        probs = softmax_of(query, key, allowed)
        d_prob = mm(d_out, value, NT)
        weighted = jnp.sum(probs * d_prob, axis=-1, keepdims=True)
        d_scores = (probs * (d_prob - weighted)).astype(BF16)
        dqs.append(mm(d_scores, key) * SCALE)
        dks.append(mm(d_scores, query, TN) * SCALE)
        dvs.append(mm(probs.astype(BF16), d_out, TN))
    dq_ref[...] = jnp.concatenate(dqs, axis=1).astype(BF16)
    dkv_acc[...] += jnp.concatenate(dks + dvs, axis=1)

    @pl.when(tile == pl.num_programs(0) - 1)
    def _():
        gout_ref[...] = gout_acc[...].astype(BF16)
        if len(dkv_refs) == 1:
            dkv_refs[0][...] = dkv_acc[...].astype(BF16)
        else:
            half = dkv_refs[0].shape[0]
            for at in range(2):
                part = dkv_acc[at * half : (at + 1) * half, :].astype(BF16)
                mine = scal[3] == at * half

                @pl.when(mine)
                def _():
                    dkv_refs[0][...] = part

                @pl.when(jnp.logical_not(mine))
                def _():
                    dkv_refs[1][...] = part


def project_back_kernel(scal, dq_ref, own_ref, got_ref, normed_ref, gout_ref, *refs, chunks):
    packs, halves, grads = refs[:4], refs[4 : 4 + 2 * chunks], refs[4 + 2 * chunks :]
    d_kv = (own_ref[...].astype(F32) + got_ref[...].astype(F32)).astype(BF16)
    d_q, normed = dq_ref[...], normed_ref[...]
    width = d_q.shape[1]
    weight = joined(packs)
    part = mm(d_kv, weight[:, KEYS:QUERY], NT) + mm(d_q, weight[:, QUERY : QUERY + width], NT)
    half = part.shape[0] // 2
    for at in range(2):
        put_halves(at, scal[1], part[at * half : (at + 1) * half], halves)
    g_kv, g_q, g_out = mm(normed, d_kv, TN), mm(normed, d_q, TN), gout_ref[...]
    rows = grads[0].shape[0]
    for at, ref in enumerate(grads):
        cut = slice(at * rows, (at + 1) * rows)
        ref[...] = jnp.zeros_like(ref)
        ref[:, KEYS:QUERY] = g_kv[cut].astype(BF16)
        ref[:, QUERY : QUERY + width] = g_q[cut].astype(BF16)
        ref[:, OUT : OUT + width] = g_out[cut]


def mix_kernel(scal, stream_ref, *refs, parts):
    mixed = stream_ref[...].astype(F32) + arrived(scal[1], refs[:parts])
    packs, (mixed_ref, in_ref) = refs[parts : parts + 4], refs[parts + 4 :]
    mixed_ref[...] = mixed
    in_ref[...] = normed_of(mixed, gain_row(packs, 1))[2].astype(BF16)


def shared_kernel(scal, in_ref, *refs):
    packs, (branch_ref, gate_ref, up_ref) = refs[:12], refs[12:]
    gate = mm(in_ref[...], joined(packs[:4]))
    up = mm(in_ref[...], joined(packs[4:8]))
    gate_ref[...] = gate
    up_ref[...] = up
    hidden = (gate / (1.0 + jnp.exp(-gate)) * up).astype(BF16)
    branch_ref[...] = mm(hidden, joined(packs[8:]), NT)


def glu_back(gate, up, d_hidden):
    sigmoid = 1.0 / (1.0 + jnp.exp(-gate))
    active = gate * sigmoid
    hidden = (active * up).astype(BF16)
    d_gate = (d_hidden * up * (sigmoid * (1.0 + gate * (1.0 - sigmoid)))).astype(BF16)
    return hidden, d_gate, (d_hidden * active).astype(BF16)


def shared_back_kernel(scal, d_ref, in_ref, gate_ref, up_ref, *refs):
    packs, (out_ref, *grad_refs) = refs[:12], refs[12:]
    hid = gate_ref.shape[1]
    cut = lambda at: joined(packs[4 * at : 4 * at + 4])
    d_branch, ffn_in = d_ref[...], in_ref[...]
    hidden, d_gate, d_up = glu_back(gate_ref[...], up_ref[...], mm(d_branch, cut(2)))
    out_ref[...] = mm(d_gate, cut(0), NT) + mm(d_up, cut(1), NT)
    grads = (mm(ffn_in, d_gate, TN), mm(ffn_in, d_up, TN), mm(d_branch, hidden, TN))
    rows = grad_refs[0].shape[0]
    for at, grad in enumerate(grads):
        for r, ref in enumerate(grad_refs):
            ref[:, at * hid : (at + 1) * hid] = grad[r * rows : (r + 1) * rows].astype(BF16)


def load_pair(own_ref, sib_ref, pair, block):
    half = own_ref.shape[0]
    pair[:half, :] = own_ref[...]
    pair[half:, :] = swap_pairs(sib_ref[...].astype(F32), block).astype(BF16)


def one_hot_cols(pos_col, slots):
    hit = lax.broadcasted_iota(jnp.int32, (pos_col.shape[0], slots), 1) == pos_col
    return jnp.where(hit, 1.0, 0.0).astype(BF16)


def hit_rows(pos_row, slots):
    return lax.broadcasted_iota(jnp.int32, (slots, pos_row.shape[1]), 0) == pos_row


def start_pair(own_ref, sib_ref, init_ref, pair, acc, block):
    @pl.when(pl.program_id(0) == 0)
    def _():
        half = own_ref.shape[0]
        load_pair(own_ref, sib_ref, pair, block)
        acc[:half, :] = init_ref[...]
        acc[half:, :] = jnp.zeros_like(init_ref)


def finish_pair(own_out, sib_out, acc):
    @pl.when(pl.program_id(0) == pl.num_programs(0) - 1)
    def _():
        half = own_out.shape[0]
        own_out[...] = acc[:half, :]
        sib_out[...] = acc[half:, :].astype(BF16)


def pack_kernel(scal, in_ref, out_ref, own_ref, first_ref, last_ref):
    third = first_ref.shape[2]
    own_ref[0, :2] = in_ref[0, 0]
    own_ref[0, 2] = out_ref[0, 0]
    first_ref[0] = own_ref[0, :, pl.ds(pl.multiple_of(scal[4] * third, third), third), :]
    last_ref[0] = own_ref[0, :, 2 * third :, :]


def expert_weights(scal, refs):
    def far(refs, part):
        straight, around, last = [ref[0, part] for ref in refs]
        low = jnp.where(scal[4] == 0, straight, around)
        middle = jnp.where(scal[4] == 0, around, straight)
        return [low, middle, last]

    return [
        jnp.concatenate(
            [refs[0][0, part], refs[1][0, part]] + far(refs[2:5], part) + far(refs[5:8], part), axis=0
        )
        for part in range(3)
    ]


def expert_kernel(scal, own_ref, sib_ref, init_ref, row_ref, col_ref, mix_ref, *refs, block):
    weights, (own_out, sib_out, x_ref, gate_ref, up_ref, acc, pair) = refs[:8], refs[8:]
    slots = x_ref.shape[1]
    start_pair(own_ref, sib_ref, init_ref, pair, acc, block)
    w_gate, w_up, w_out = expert_weights(scal, weights)
    hit = jnp.where(hit_rows(row_ref[0], slots), 1.0, 0.0).astype(BF16)
    chosen = mm(hit, pair[...]).astype(BF16)
    x_ref[0] = chosen
    gate = mm(chosen, w_gate)
    up = mm(chosen, w_up)
    gate_ref[0] = gate
    up_ref[0] = up
    hidden = (gate / (1.0 + jnp.exp(-gate)) * up).astype(BF16)
    rows = mm(hidden, w_out, NT).astype(BF16)
    acc[...] += mix_ref[0] * mm(one_hot_cols(col_ref[0], slots), rows)
    finish_pair(own_out, sib_out, acc)


def expert_back_kernel(
    scal, own_ref, sib_ref, init_ref, row_ref, col_ref, mix_ref, x_ref, gate_ref, up_ref, *refs,
    block, chunks
):
    weights, (own_out, sib_out), grads = refs[:8], refs[8:10], refs[10:-2]
    acc, pair = refs[-2:]
    slots = x_ref.shape[1]
    start_pair(own_ref, sib_ref, init_ref, pair, acc, block)
    w_gate, w_up, w_out = expert_weights(scal, weights)
    hit = hit_rows(row_ref[0], slots)
    weight = jnp.sum(jnp.where(hit, mix_ref[0], 0.0), axis=1, keepdims=True)
    hit = jnp.where(hit, 1.0, 0.0).astype(BF16)
    d_rows = (mm(hit, pair[...]) * weight).astype(BF16)
    hidden, d_gate, d_up = glu_back(gate_ref[0], up_ref[0], mm(d_rows, w_out))
    chosen = x_ref[0]
    step = pl.program_id(0)
    per_chunk = pl.num_programs(0) // chunks
    parts = (mm(chosen, d_gate, TN), mm(chosen, d_up, TN), mm(d_rows, hidden, TN))
    parts = [p.astype(BF16) for p in parts]
    for chunk in range(chunks):

        @pl.when(step // per_chunk == chunk)
        def _():
            for at in range(3):
                grads[2 * chunk][0, at] = parts[at][: 2 * block]
                grads[2 * chunk + 1][0, at] = parts[at][2 * block :]

    d_x = mm(d_gate, w_gate, NT) + mm(d_up, w_up, NT)
    acc[...] += mm(one_hot_cols(col_ref[0], slots), d_x.astype(BF16))
    finish_pair(own_out, sib_out, acc)


def join_kernel(scal, own_ref, got_ref, *halves, block):
    part = own_ref[...] + swap_pairs(got_ref[...].astype(F32), block)
    put_halves(pl.program_id(0), scal[1], part, halves)


def mix_back_kernel(scal, mixed_ref, next_ref, *refs, parts):
    packs, (d_ref, attn_ref, gain_ref) = refs[parts : parts + 4], refs[parts + 4 :]
    back, gain_grad = norm_back(arrived(scal[1], refs[:parts]), mixed_ref[...], gain_row(packs, 1))
    d_mixed = back + next_ref[...].astype(F32)
    d_ref[...] = d_mixed
    attn_ref[...] = d_mixed.astype(BF16)
    sum_tiles(gain_ref, gain_grad)


def sum_tiles(ref, value):
    value = jnp.broadcast_to(value, ref.shape)

    @pl.when(pl.program_id(0) == 0)
    def _():
        ref[...] = value

    @pl.when(pl.program_id(0) > 0)
    def _():
        ref[...] += value


def input_back_kernel(scal, stream_ref, mixed_ref, *refs, parts, block, final):
    packs, outs = refs[parts : parts + 4], refs[parts + 4 :]
    stream = stream_ref[...].astype(F32)
    back, gain_grad = norm_back(arrived(scal[1], refs[:parts]), stream, gain_row(packs, 0))
    d_stream = back + mixed_ref[...]
    if final:
        outs[0][...] = relative(d_stream, scal[0], block)
    else:
        outs[0][...] = d_stream
        outs[1][...] = d_stream.astype(BF16)
    sum_tiles(outs[-1], gain_grad)


def store_expert(in_ref, out_ref, gate, up, out):
    blocks = gate.shape[1] // 128
    for at, part in enumerate((gate, up)):
        for col in range(blocks):
            rows = pl.ds(col * 2 + at, part.shape[0], stride=2 * blocks)
            in_ref[0, 0, rows, :] = part[:, col * 128 : (col + 1) * 128]
    out_ref[0, 0] = out


def own_kernel(scal, part_ref, got_ref, *refs):
    give_ref, in_ref, out_ref = refs[-3:]
    half = give_ref.shape[2]
    total = [part_ref[0, at].astype(F32) + got_ref[0, at].astype(F32) for at in range(3)]
    for at in range(3):
        give_ref[0, at] = total[at][half:].astype(BF16)
    store_expert(in_ref, out_ref, *[t[:half] for t in total])


def other_kernel(scal, got_ref, *refs):
    store_expert(*refs[-2:], *[got_ref[0, at].astype(F32) for at in range(3)])

CHUNKS, PARTS = 2, (2, 1)
SLOTS = {
    "start": ["pack 0", ("experts", 0)],
    ("attend", 0): ["slots"],
    ("attend half", 0): [("experts", 0), "pack 1"],
    ("mixed", 0): [("experts", 0), "pack 1", ("experts", 1), "pack 2"],
    ("branch half", 0): [("experts", 1), "pack 2"],
    ("attend sum", 1): [("experts", 1)],
    (1, "experts"): [(1, 0)],
    (1, "project"): [(1, "packs")],
    (1, "attention sum"): [(1, 0), (1, "packs")],
    (0, "experts"): [(1, "packs"), (0, 0)],
    (0, "ffn sum"): [(0, "shared")],
    (0, "attention"): [(0, 0), (0, 1)],
    (0, "project"): [(1, 0), (1, "packs"), (0, "shared"), (0, "attention")],
    (0, "attention sum"): [(1, 0), (0, "shared"), (0, "attention")],
    (0, "input"): [(0, 0), (0, 1)],
}
TAIL = (
    ["gains", (0, "shared"), (0, "attention")],
    ["gains", (0, 0), (0, "attention")],
    ["gains", (0, 1)],
    [(0, 1)],
)


class Outs:
    def __init__(self, scal, layers, experts, block, hid):
        self.scal, self.per_core = scal, experts // 2
        self.shapes = (
            sds((layers, experts, block * 2 * hid // 128, 128), F32),
            sds((layers, experts, block, hid), F32),
        )
        self.held = None

    def put(self, kernel, ins, extra, layer, first, other):
        count = ins[0].shape[0]
        lead = lambda a: (a, (1,) + a.shape[1:], lambda e, s: (e, 0, 0, 0))
        place = lambda e, s: (layer, (s[2] ^ other) * self.per_core + first + e, 0, 0)
        moved = lambda s: count * s.size * 4 // (s.shape[0] * s.shape[1])
        slot = lambda s: (s, (1, 1) + s.shape[2:], place, moved(s))
        held = [] if self.held is None else [(h, "any", None) for h in self.held]
        base = 1 + len(ins)
        *rest, gin, gout = call(
            kernel,
            self.scal,
            (count,),
            [lead(i) for i in ins] + held,
            [lead(x) for x in extra] + [slot(s) for s in self.shapes],
            alias={base + at: len(extra) + at for at in range(len(held))},
            limit=16,
        )
        self.held = (gin, gout)
        return rest


def expert_flow(outs, near, far, layer, first):
    near, far = yield [near, far]
    near, got = yield [near, swap(far, "fsdp", 2)]
    part, got = yield list(ctx_last(add(near, got)))
    block = near.shape[2] // 2
    give = sds(near.shape[:2] + (block,) + near.shape[3:], BF16)
    (give,) = outs.put(own_kernel, (part, got), (give,), layer, first, 0)
    (got,) = yield [swap(give, "fsdp", 1)]
    outs.put(other_kernel, (got,), (), layer, first, 1)
    yield []


def pack_flow(place, name, parts):
    parts = yield list(parts)
    own, far, got, far_got = yield [parts[0], parts[2], swap(parts[1], "fsdp", 1), swap(parts[3], "fsdp", 1)]
    own, far = add(own, got), add(far, far_got)
    own, got = yield [own, swap(far, "fsdp", 2)]
    part, got = yield list(ctx_last(add(own, got)))
    place[name] = part.astype(F32) + got.astype(F32)
    yield []


def weight_flow(place, at, own, first, last):
    own, first, last = yield [own, first, last]
    own, sib, straight, last = yield [own, swap(own, "fsdp", 1), swap(first, "fsdp", 2), last]
    around, last = swap(straight, "ctx", 1), swap(last, "fsdp", 2)
    held = yield [straight, around, last, swap(straight, "fsdp", 1)]
    straight, around, last, cross = held
    place[at] = [own, sib, straight, around, last]
    place[at] += [cross, swap(around, "fsdp", 1), swap(last, "fsdp", 1)]
    yield []


def block_flow(place, at, own):
    (own,) = yield [own]
    own, far = yield [own, swap(own, "fsdp", 2)]
    place[at] = [own, swap(own, "fsdp", 1), far, swap(far, "fsdp", 1)]
    yield []


def ancestry(parent_row):
    count = parent_row.shape[0]
    block_ids = jnp.arange(count, dtype=jnp.int32)
    step_map = ((parent_row[:, None] == block_ids[None, :]) & (block_ids[:, None] > 0)).astype(F32)
    reach = on_path = jnp.eye(count, dtype=F32)
    for _ in range(count):
        reach = jnp.dot(reach, step_map, precision=lax.Precision.HIGHEST)
        on_path = on_path + reach
    return on_path


def shards(
    tokens,
    parents,
    routes,
    gates,
    attn_gain,
    ffn_gain,
    qkv_weight,
    out_weight,
    shared_in,
    shared_out,
    expert_in,
    expert_out,
    cotangent,
):
    rows, width = tokens.shape[1], tokens.shape[2]
    layers, experts = expert_in.shape[0], expert_in.shape[1]
    block, heads_width = qkv_weight.shape[1], qkv_weight.shape[3]
    hid = expert_in.shape[4]
    ctx = lax.axis_size("ctx")
    tree_len = rows * ctx
    me, here = lax.axis_index("fsdp"), lax.axis_index("ctx")
    core, bit = me & 1, lax.axis_index("tp") & 1
    half_at = here & 1
    per_core = experts // 2
    capacity = 2 * (3 * rows // 8)
    scal = jnp.stack([me, bit, core, here * rows, half_at]).astype(jnp.int32)

    def pack_attention(at):
        cols = [qkv_weight[at][:, part] for part in (1, 2, 0)]
        pad = jnp.zeros((block, OUT - QUERY - heads_width), BF16)
        gains = jnp.stack([attn_gain[at], ffn_gain[at]], axis=1)
        tail = jnp.zeros((block, PACK - GAINS - 2), BF16)
        return jnp.concatenate(cols + [pad, out_weight[at].T, gains, tail], axis=1)

    def pack_shared(at):
        return [shared_in[at].reshape(block, 2 * hid), shared_out[at].T]

    ein = lax.optimization_barrier(expert_in.transpose(0, 1, 3, 2, 4))
    eout = expert_out.transpose(0, 1, 3, 2)

    def pack_experts(at):
        third = block // 3
        whole_pack = sds((experts, 3, block, hid), BF16)
        part = sds((experts, 3, third, hid), BF16)
        lead = lambda a: (a, (1,) + a.shape[1:], lambda e, s: (e, 0, 0, 0))
        return call(
            pack_kernel,
            scal,
            (experts,),
            [
                (ein, (1, 1) + ein.shape[2:], lambda e, s: (at, e, 0, 0, 0)),
                (eout, (1, 1) + eout.shape[2:], lambda e, s: (at, e, 0, 0)),
            ],
            [lead(whole_pack), lead(part), lead(part)],
            limit=16,
        )

    ancestors = ancestry(parents[0])
    segment = tree_len // ancestors.shape[0]
    anc_row = lax.dynamic_slice_in_dim(ancestors, here * rows // segment, 1, 0)
    path = jnp.repeat(anc_row, segment, axis=1)

    chosen = routes[0][:, :, None] == jnp.arange(experts, dtype=jnp.int32)[None, None, :]
    mixing = jnp.sum(jnp.where(chosen, gates[0][:, :, None], 0.0), axis=1)
    mixing = jnp.concatenate([mixing, swap(mixing, "fsdp", 1)], axis=0)
    mixing = lax.dynamic_slice_in_dim(mixing, core * per_core, per_core, 1)
    named = mixing > 0.0
    pair = mixing.shape[0]
    earlier = (jnp.arange(pair)[:, None] > jnp.arange(pair)[None, :]).astype(BF16)
    slot = mm(earlier, named.astype(BF16)).astype(jnp.int32)
    slot = jnp.where(named, slot, -1).T
    mixing = mixing.T
    slot_row, slot_col = slot[:, None, :], slot[:, :, None]
    mix_row, mix_col = mixing[:, None, :], mixing[:, :, None]

    lead = lambda a: (
        a,
        (1,) + tuple(a.shape[1:]),
        lambda e, s: (e,) + (0,) * (len(a.shape) - 1),
    )

    matrix = 2 * rows * width
    expert_flops = 2 * per_core * capacity * width * hid
    pair_scratch = [pltpu.VMEM((2 * rows, width), F32), pltpu.VMEM((2 * rows, width), BF16)]
    halves = half_shapes(rows, width, CHUNKS)
    row_f32, row_bf16 = sds((rows, width), F32), sds((rows, width), BF16)

    flows, held = {}, {}

    def open_flow(name, flow):
        flows[name] = flow
        held[name] = next(flow)

    def slot(name, *values):
        names = SLOTS.get(name, ())
        values, arrays = lax.optimization_barrier((list(values), [held[n] for n in names]))
        for n, a in zip(names, arrays):
            if n == "slots":
                tables.extend(a)
            else:
                held[n] = flows[n].send(a)
        return values

    tables = []

    def finish(*names):
        for name in names:
            held[name] = flows[name].send(held[name])

    small, routed = {}, {}
    open_flow("pack 0", block_flow(small, 0, pack_attention(0)))
    for at in range(layers):
        open_flow(("experts", at), weight_flow(routed, at, *pack_experts(at)))
    open_flow("pack 1", block_flow(small, 1, jnp.concatenate(pack_shared(0), axis=1)))
    rest = [pack_attention(at) for at in range(1, layers)]
    rest = [v for pack in rest for v in (pack, jnp.zeros((block, 128), BF16))]
    rest += [v for at in range(1, layers) for v in pack_shared(at)]
    open_flow("pack 2", block_flow(small, 2, jnp.concatenate(rest, axis=1)))

    held["slots"] = [slot_row, slot_col, mix_row, mix_col]

    def attention_ins(at):
        if at == 0:
            return [whole(p) for p in small[0]]
        return [(p, (block, 1024), lambda *_: (0, at - 1)) for p in small[2]]

    def shared_ins(at):
        packs, first = (small[1], 0) if at == 0 else (small[2], 1024 * (layers - 1) // hid + 3 * at - 3)
        index = lambda which: lambda *_: (0, first + which)
        return [(p, (block, hid), index(which)) for which in range(3) for p in packs]

    def expert_ins(at):
        index = lambda e, s: (s[2] * per_core + e, 0, 0, 0)
        return [(a, (1,) + a.shape[1:], index) for a in routed[at]]

    stream, cot = call(
        functools.partial(order_kernel, block=block),
        scal,
        (2,),
        [tiled(tokens[0]), tiled(cotangent[0])],
        [tiled(row_bf16)] * 2,
    )
    finish("pack 0")
    slot("start")

    saved = []
    mixed = arrivals = None
    for at in range(layers):
        outs = [
            tiled(row_bf16),
            tiled(sds((rows, heads_width), BF16)),
            tiled(sds((rows, 2 * heads_width), BF16)),
        ]
        weights = attention_ins(at)
        if at == 0:
            normed, query, kv = call(
                first_kernel, scal, (2,), [tiled(stream)] + weights, outs, flops=matrix * 576
            )
        else:
            stream, normed, query, kv = call(
                functools.partial(next_kernel, parts=len(arrivals)),
                scal,
                (2,),
                [tiled(mixed)] + [whole(a) for a in arrivals] + weights,
                [tiled(row_f32)] + outs,
                flops=matrix * 576,
            )
        (kv,) = slot(("project", at), kv)
        kv = lax.all_gather(kv, "ctx", axis=0, tiled=True)
        heads, *part = call(
            attend_kernel,
            scal,
            (2,),
            [whole(path), tiled(query), whole(kv)] + weights,
            [tiled(sds((rows, heads_width), BF16))] + halves,
            flops=4 * rows * tree_len * heads_width + matrix * heads_width,
            exps=rows * tree_len * heads_width // HEAD_DIM,
            limit=40,
        )
        part = slot(("attend", at), *part)
        arrivals = tp_sum(part, functools.partial(slot, ("attend half", at)))
        arrivals = slot(("attend sum", at), *arrivals)
        mixed, ffn_in = call(
            functools.partial(mix_kernel, parts=len(arrivals)),
            scal,
            (2,),
            [tiled(stream)] + [whole(a) for a in arrivals] + weights,
            [tiled(row_f32), tiled(row_bf16)],
        )
        sib_in = swap(ffn_in, "fsdp", 1)
        ffn_in, sib_in = slot(("mixed", at), ffn_in, sib_in)
        branch, gate, up = call(
            shared_kernel,
            scal,
            (2,),
            [tiled(ffn_in)] + shared_ins(at),
            [tiled(row_f32)] + [tiled(sds((rows, hid), F32))] * 2,
            flops=3 * matrix * hid,
            exps=rows * hid,
        )
        own, sib, x, e_gate, e_up = call(
            functools.partial(expert_kernel, block=block),
            scal,
            (per_core,),
            [whole(ffn_in), whole(sib_in), whole(branch)]
            + [lead(tables[at]) for at in (0, 1, 3)]
            + expert_ins(at),
            [whole(row_f32), whole(row_bf16), lead(sds((per_core, capacity, width), BF16))]
            + [lead(sds((per_core, capacity, hid), F32))] * 2,
            scratch=pair_scratch,
            flops=5 * expert_flops,
            exps=per_core * capacity * hid,
            limit=48,
        )
        own, sib = slot(("experts", at), own, sib)
        part = call(
            functools.partial(join_kernel, block=block),
            scal,
            (2,),
            [tiled(own), tiled(swap(sib, "fsdp", 1))],
            halves,
        )
        saved.append(
            (stream, normed, query, kv, heads, mixed, ffn_in, gate, up, x, e_gate, e_up)
        )
        part = slot(("join", at), *part)
        arrivals = tp_sum(part, functools.partial(slot, ("branch half", at)))
        arrivals = slot(("branch sum", at), *arrivals)
    (result,) = call(
        functools.partial(last_kernel, block=block),
        scal,
        (2,),
        [tiled(mixed)] + [whole(a) for a in arrivals],
        [tiled(row_bf16)],
    )

    outs = Outs(scal, layers, experts, block, hid)
    packed = {}
    gain_grads = [None] * (2 * layers)
    d_next, d_branch = cot, cot
    for at in reversed(range(layers)):
        stream, normed, query, kv, heads, mixed, ffn_in, gate, up, x, e_gate, e_up = saved[at]
        weights = attention_ins(at)
        sib_d = swap(d_branch, "fsdp", 1)
        d_ffn, *g_shared = call(
            shared_back_kernel,
            scal,
            (1,),
            [whole(a) for a in (d_branch, ffn_in, gate, up)] + shared_ins(at),
            [whole(row_f32)] + [whole(sds((block, 3 * hid), BF16))] * 4,
            flops=6 * matrix * hid,
            exps=rows * hid,
        )
        chunks = PARTS[at]
        size = per_core // chunks
        part_of = lambda chunk: (
            sds((size, 3, 2 * block, hid), BF16),
            (1, 3, 2 * block, hid),
            lambda e, s: (jnp.clip(e - chunk * size, 0, size - 1), 0, 0, 0),
        )
        own, sib, *grads = call(
            functools.partial(expert_back_kernel, block=block, chunks=chunks),
            scal,
            (per_core,),
            [whole(d_branch), whole(sib_d), whole(d_ffn)]
            + [lead(a) for a in (*tables[:3], x, e_gate, e_up)]
            + expert_ins(at),
            [whole(row_f32), whole(row_bf16)]
            + [part_of(chunk) for chunk in range(chunks) for _ in range(2)],
            scratch=pair_scratch,
            flops=8 * expert_flops,
            exps=per_core * capacity * hid,
            limit=56,
        )
        for chunk in range(chunks):
            near, far = grads[2 * chunk : 2 * chunk + 2]
            open_flow((at, chunk), expert_flow(outs, near, far, at, chunk * size))
        if at == 0:
            open_flow((0, "shared"), pack_flow(packed, (0, "shared"), g_shared))
        own, sib = slot((at, "experts"), own, sib)
        part = call(
            functools.partial(join_kernel, block=block),
            scal,
            (2,),
            [tiled(own), tiled(swap(sib, "fsdp", 1))],
            halves,
        )
        part = slot((at, "join"), *part)
        arrivals = tp_sum(part, functools.partial(slot, (at, "ffn half")))
        arrivals = slot((at, "ffn sum"), *arrivals)
        d_mixed, d_attn, gain = call(
            functools.partial(mix_back_kernel, parts=len(arrivals)),
            scal,
            (2,),
            [tiled(mixed), tiled(d_next)] + [whole(a) for a in arrivals] + weights,
            [tiled(row_f32), tiled(row_bf16), whole(sds((8, width), F32))],
        )
        gain_grads[layers + at] = gain[:1]
        kv_shape = sds((rows, 2 * heads_width), BF16)
        kv_outs = [kv_shape] * 2 if ctx == 2 else [sds((tree_len, 2 * heads_width), BF16)]
        dq, g_out, *dkv = call(
            attend_back_kernel,
            scal,
            (2,),
            [whole(path), tiled(query), whole(kv), tiled(d_attn), tiled(heads)] + weights,
            [tiled(sds((rows, heads_width), BF16)), whole(sds((width, heads_width), BF16))]
            + [whole(k) for k in kv_outs],
            scratch=[
                pltpu.VMEM((tree_len, 2 * heads_width), F32),
                pltpu.VMEM((width, heads_width), F32),
            ],
            flops=10 * rows * tree_len * heads_width + 2 * matrix * heads_width,
            exps=rows * tree_len * heads_width // HEAD_DIM,
            limit=56,
        )
        dq, *dkv = slot((at, "attention"), dq, *dkv)
        if ctx == 2:
            kv_own, kv_got = dkv[0], swap(dkv[1], "ctx", 1)
        else:
            parts = dkv[0].reshape((ctx, rows) + dkv[0].shape[1:])
            parts = lax.all_to_all(parts, "ctx", 0, 0, tiled=True)
            kv_own, kv_got = jnp.sum(parts.astype(F32), axis=0), jnp.zeros(kv_shape.shape, F32)
        *part, g0, g1, g2, g3 = call(
            functools.partial(project_back_kernel, chunks=CHUNKS),
            scal,
            (1,),
            [whole(a) for a in (dq, kv_own, kv_got, normed, g_out)] + weights,
            halves + [whole(sds((block, PACK), BF16))] * 4,
            flops=2 * matrix * 576,
        )
        g_attention = [g0, g1, g2, g3]
        if at == 0:
            open_flow((0, "attention"), pack_flow(packed, (0, "attention"), g_attention))
        else:
            both = [jnp.concatenate(g, axis=1) for g in zip(g_shared, g_attention)]
            open_flow((at, "packs"), pack_flow(packed, at, both))
        part = slot((at, "project"), *part)
        arrivals = tp_sum(part, functools.partial(slot, (at, "attention half")))
        arrivals = slot((at, "attention sum"), *arrivals)
        final = at == 0
        *rest, gain = call(
            functools.partial(
                input_back_kernel, parts=len(arrivals), block=block, final=final
            ),
            scal,
            (2,),
            [tiled(stream), tiled(d_mixed)] + [whole(a) for a in arrivals] + weights,
            [tiled(row_f32)] + ([] if final else [tiled(row_bf16)]) + [whole(sds((8, width), F32))],
        )
        gain_grads[at] = gain[:1]
        d_next, *rest = slot((at, "input"), *rest)
        if not final:
            (d_branch,) = rest
    gains = jnp.concatenate(gain_grads, axis=0).astype(BF16)
    cuts = [gains[:, r * block : (r + 1) * block] for r in range(4)]
    open_flow("gains", pack_flow(packed, "gains", cuts))
    finish("gains")
    for step in TAIL:
        finish(*step)
    gains = packed["gains"]
    later = [packed[at] for at in range(1, layers)]
    g_shared = jnp.stack([packed[0, "shared"]] + [p[:, : 3 * hid] for p in later])
    g_attention = jnp.stack([packed[0, "attention"]] + [p[:, 3 * hid :] for p in later])
    cut = lambda first: g_attention[:, :, first : first + heads_width]
    g_in, g_out = outs.held
    blocks = hid // 128
    g_in = g_in.reshape(layers * experts * block, blocks, 2, 128).transpose(0, 2, 1, 3)
    return (
        result[None],
        d_next[None],
        gains[:layers],
        gains[layers:],
        jnp.stack([cut(QUERY), cut(KEYS), cut(KEYS + heads_width)], axis=2),
        cut(OUT).transpose(0, 2, 1),
        g_shared[:, :, : 2 * hid].reshape(layers, block, 2, hid),
        g_shared[:, :, 2 * hid :].transpose(0, 2, 1),
        g_in.reshape(layers, experts, block, 2, hid),
        g_out.transpose(0, 1, 3, 2),
    )


def solution(mesh):
    return jax.shard_map(
        shards,
        mesh=mesh,
        in_specs=(
            P("fsdp", "ctx", None),
            P("fsdp", None),
            P("fsdp", "ctx", None),
            P("fsdp", "ctx", None),
            P(None, "fsdp"),
            P(None, "fsdp"),
            P(None, "fsdp", None, "tp"),
            P(None, "tp", "fsdp"),
            P(None, "fsdp", None, "tp"),
            P(None, "tp", "fsdp"),
            P(None, None, "fsdp", None, "tp"),
            P(None, None, "tp", "fsdp"),
            P("fsdp", "ctx", None),
        ),
        out_specs=(
            P("fsdp", "ctx", None),
            P("fsdp", "ctx", None),
            P(None, "fsdp"),
            P(None, "fsdp"),
            P(None, "fsdp", None, "tp"),
            P(None, "tp", "fsdp"),
            P(None, "fsdp", None, "tp"),
            P(None, "tp", "fsdp"),
            P(None, None, "fsdp", None, "tp"),
            P(None, None, "tp", "fsdp"),
        ),
        check_vma=False,
    )
```

time: 942 us -> 799 us (0.85)
  other arithmetic: 123 us -> 26.7 us
  Pallas kernels: 116 us -> 197 us
  waiting for transfers between devices: 422 us -> 374 us
  matrix products: 49.2 us -> 1.44 us
  starting transfers between devices: 112 us -> 74.1 us
  blocking collectives: 22.6 us -> 43.3 us
  local copies, waits for them, and re-layouts: 87.7 us -> 75 us
    pallas_call x8 -> x36, Pallas kernels: 116 us -> 197 us  [call(): pl.pallas_call(kernel, out_shape=[o[0] for o in outs], grid_spec=pltpu.Pr...]
    ppermute x115 -> x107, waiting for transfers between devices: 422 us -> 374 us  [swap(): return lax.ppermute(values, axis, [(k, k ^ mask) for k in range(count)])]
    dot_general x43 -> x1, matrix products: 48.8 us -> 1.07 us  [mm(): return lax.dot_general(a, b, dims, preferred_element_type=F32)]
    select_n x20 -> x0, other arithmetic: 31.8 us -> none  [the longest x4 15.4 us: settle_experts(): first = jnp.where(core == 0, own, other)]
    ppermute x115 -> x107, starting transfers between devices: 103 us -> 74.1 us  [swap(): return lax.ppermute(values, axis, [(k, k ^ mask) for k in range(count)])]
    all_gather x2, blocking collectives: 22.6 us -> 43.3 us  [shards(): kv = lax.all_gather(kv, 'ctx', axis=0, tiled=True)]
    concatenate x14 -> x6, other arithmetic: 18.5 us -> 0.33 us  [the longest x4 0.27 us: shards(): both = [jnp.concatenate(g, axis=1) for g in zip(g_shared, g_attention)]]
    transpose x6 -> x2, other arithmetic: 16.2 us -> 2.19 us  [the longest x1 1.99 us: shards(): g_shared[:, :, 2 * hid:].transpose(0, 2, 1)]
  transfers between devices with their start and end apart: 117 -> 107, of which waited for: 41 -> 54; matrix products, arithmetic and copies ran while one was open for 22% -> 7% of each run, Pallas kernels for 12% -> 21%
where the time goes in v2:
time: 799 us; the launch traced here: 794 us
  waiting for transfers between devices  374 us (47%)
  Pallas kernels  197 us (25%)
  local copies, waits for them, and re-layouts  75 us (9%)
  starting transfers between devices  74.1 us (9%)
  blocking collectives  43.3 us (5%)
  other arithmetic  26.7 us (3%)
    ppermute x107, waiting for transfers between devices, swap(): return lax.ppermute(values, axis, [(k, k ^ mask) for k in range(count)])  374 us
    pallas_call x36, Pallas kernels, call(): pl.pallas_call(kernel, out_shape=[o[0] for o in outs], grid_spec=pltpu.Pr...  197 us
    ppermute x107, starting transfers between devices, swap(): return lax.ppermute(values, axis, [(k, k ^ mask) for k in range(count)])  74.1 us
    unnamed x249, local copies, waits for them, and re-layouts  52.3 us
    all_gather x2, blocking collectives, shards(): kv = lax.all_gather(kv, 'ctx', axis=0, tiled=True)  43.3 us
    convert_element_type x45, other arithmetic, add(): return (a.astype(F32) + b.astype(F32)).astype(BF16)  20.1 us
  transfers between devices with their start and end apart: 107, of which 54 were waited for; matrix products, arithmetic and copies ran while one was open for 7% of the time, Pallas kernels for 21%

profile of v2, /device:TPU:0, one launch (start us, length us, event | category | flops | bytes accessed | tf_op | source)
XLA Modules:
  0.0 793.8 jit_solution(9771047820724218379)
XLA Ops:
  39.4 12.3 %all_gather.6.kv_ref = bf16[1024,384]{1,0:T(8,128)(2,1)S(1)} all-gather(bf16[512,384]{1,0:T(8,128)(2,1)S(1)} %get-tuple-element.310), channel_id=1, replica_groups=mesh['fsdp'=4,'ctx'=2,'tp'=4] {'ctx'}, dimensions={0}, use_global_device_ids=true | all-gather | bytes 1179648 | tf_op jit(solution)/shard_map/all_gather | solution.py:785
  74.9 9.8 %collective-permute-done.8 = bf16[128,768]{1,0:T(8,128)(2,1)S(1)} collective-permute-done((bf16[128,768]{1,0:T(8,128)(2,1)S(1)}, bf16[128,768]{1,0:T(8,128)(2,1)S(1)}, u32[]{:S(2)}, u32[]{:S(2)}) %collective-permute-start.8) | collective-permute-done | bytes 196640 | tf_op jit(solution)/shard_map/ppermute | solution.py:35
  110.7 9.3 %collective-permute-done.16.refs_2_.refs_6_.refs_10_ = bf16[192,1536]{1,0:T(8,128)(2,1)S(1)} collective-permute-done((bf16[192,1536]{1,0:T(8,128)(2,1)S(1)}, bf16[192,1536]{1,0:T(8,128)(2,1)S(1)}, u32[]{:S(2)}, u32[]{:S(2)}) %collective-permute-start.16) | collective-permute-done | bytes 589856 | tf_op jit(solution)/shard_map/ppermute | solution.py:35
  121.2 9.0 %collective-permute-done.17.refs_1_.refs_5_.refs_9_ = bf16[192,1536]{1,0:T(8,128)(2,1)S(1)} collective-permute-done((bf16[192,1536]{1,0:T(8,128)(2,1)S(1)}, bf16[192,1536]{1,0:T(8,128)(2,1)S(1)}, u32[]{:S(2)}, u32[]{:S(2)}) %collective-permute-start.17) | collective-permute-done | bytes 589856 | tf_op jit(solution)/shard_map/ppermute | solution.py:35
  142.8 17.5 %shard_map.211 = (f32[512,768]{1,0:T(8,128)S(1)}, bf16[512,768]{1,0:T(8,128)(2,1)S(1)}, bf16[4,384,768]{2,1,0:T(8,128)(2,1)}, f32[4,384,512]{2,1,0:T(8,128)}, f32[4,384,512]{2,1,0:T(8,128)}) custom-call(s32[5]{0:T(128)S(1)} %stack.53.scal, bf16[512,768]{1,0:T(8,128)(2,1)} %get-tuple-element.336.in_ref.own_ref, ...), custom_call_target="tpu_custom_call" | custom-call | flops 6039797 | bytes 33079 | tf_op jit(solution)/shard_map/pallas_call | solution.py:84
  175.0 13.1 %collective-permute-done.26.refs_6_.refs_2_.refs_10_ = bf16[192,2560]{1,0:T(8,128)(2,1)S(1)} collective-permute-done((bf16[192,2560]{1,0:T(8,128)(2,1)S(1)}, bf16[192,2560]{1,0:T(8,128)(2,1)S(1)}, u32[]{:S(2)}, u32[]{:S(2)}) %collective-permute-start.26) | collective-permute-done | bytes 983072 | tf_op jit(solution)/shard_map/ppermute | solution.py:35
  191.7 14.2 %collective-permute-done.27 = bf16[128,768]{1,0:T(8,128)(2,1)S(1)} collective-permute-done((bf16[128,768]{1,0:T(8,128)(2,1)S(1)}, bf16[128,768]{1,0:T(8,128)(2,1)S(1)}, u32[]{:S(2)}, u32[]{:S(2)}) %collective-permute-start.27) | collective-permute-done | bytes 196640 | tf_op jit(solution)/shard_map/ppermute | solution.py:35
  222.6 31.0 %all_gather.7.kv_ref = bf16[1024,384]{1,0:T(8,128)(2,1)S(1)} all-gather(bf16[512,384]{1,0:T(8,128)(2,1)S(1)} %get-tuple-element.372), channel_id=1, replica_groups=mesh['fsdp'=4,'ctx'=2,'tp'=4] {'ctx'}, dimensions={0}, use_global_device_ids=true | all-gather | bytes 1179648 | tf_op jit(solution)/shard_map/all_gather | solution.py:785
  271.8 11.9 %collective-permute-done.35 = bf16[128,768]{1,0:T(8,128)(2,1)S(1)} collective-permute-done((bf16[128,768]{1,0:T(8,128)(2,1)S(1)}, bf16[128,768]{1,0:T(8,128)(2,1)S(1)}, u32[]{:S(2)}, u32[]{:S(2)}) %collective-permute-start.35) | collective-permute-done | bytes 196640 | tf_op jit(solution)/shard_map/ppermute | solution.py:35
  314.3 16.5 %shard_map.217 = (f32[512,768]{1,0:T(8,128)S(1)}, bf16[512,768]{1,0:T(8,128)(2,1)S(1)}, bf16[4,384,768]{2,1,0:T(8,128)(2,1)}, f32[4,384,512]{2,1,0:T(8,128)}, f32[4,384,512]{2,1,0:T(8,128)}) custom-call(s32[5]{0:T(128)S(1)} %stack.53.scal, bf16[512,768]{1,0:T(8,128)(2,1)S(1)} %get-tuple-element.391.in_ref.own_ref, ...), custom_call_target="tpu_custom_call" | custom-call | flops 6039797 | bytes 33079 | tf_op jit(solution)/shard_map/pallas_call | solution.py:84
  332.9 28.1 %shard_map.221 = (f32[512,768]{1,0:T(8,128)}, bf16[512,768]{1,0:T(8,128)(2,1)}, bf16[4,3,384,512]{3,2,1,0:T(8,128)(2,1)}, bf16[4,3,384,512]{3,2,1,0:T(8,128)(2,1)}) custom-call(s32[5]{0:T(128)} %copy-done.62, bf16[512,768]{1,0:T(8,128)(2,1)} %copy-done.22, bf16[512,768]{1,0:T(8,128)(2,1)} %collective-permute-done.52.sib_ref, f32[512,768]{1,0:T(8,128)} %copy-done.38, ...), custom_call_target="tpu_custom_call" | custom-call | flops 9663676 | bytes 42516 | tf_op jit(solution)/shard_map/pallas_call | solution.py:84
  380.3 13.2 %collective-permute-done.56 = bf16[128,768]{1,0:T(8,128)(2,1)S(1)} collective-permute-done((bf16[128,768]{1,0:T(8,128)(2,1)S(1)}, bf16[128,768]{1,0:T(8,128)(2,1)S(1)}, u32[]{:S(2)}, u32[]{:S(2)}) %collective-permute-start.56) | collective-permute-done | bytes 196640 | tf_op jit(solution)/shard_map/ppermute | solution.py:35
  409.5 13.0 %shard_map.224 = (bf16[512,192]{1,0:T(8,128)(2,1)}, bf16[768,192]{1,0:T(8,128)(2,1)}, bf16[512,384]{1,0:T(8,128)(2,1)}, bf16[512,384]{1,0:T(8,128)(2,1)}) custom-call(s32[5]{0:T(128)} %copy-done.62, f32[1,1024]{1,0:T(1,128)} %bitcast.109, bf16[512,192]{1,0:T(8,128)(2,1)} %copy-done.48, bf16[1024,384]{1,0:T(8,128)(2,1)} %copy-done.28, ...), custom_call_target="tpu_custom_call" | custom-call | flops 1308622 | bytes 7180 | tf_op jit(solution)/shard_map/pallas_call | solution.py:84
  422.5 11.3 %collective-permute-done.60.got_ref = bf16[512,384]{1,0:T(8,128)(2,1)S(1)} collective-permute-done((bf16[512,384]{1,0:T(8,128)(2,1)}, bf16[512,384]{1,0:T(8,128)(2,1)S(1)}, u32[]{:S(2)}, u32[]{:S(2)}) %collective-permute-start.60) | collective-permute-done | bytes 393248 | tf_op jit(solution)/shard_map/ppermute | solution.py:35
  455.3 12.4 %collective-permute-done.63 = bf16[128,768]{1,0:T(8,128)(2,1)S(1)} collective-permute-done((bf16[128,768]{1,0:T(8,128)(2,1)S(1)}, bf16[128,768]{1,0:T(8,128)(2,1)S(1)}, u32[]{:S(2)}, u32[]{:S(2)}) %collective-permute-start.63) | collective-permute-done | bytes 196640 | tf_op jit(solution)/shard_map/ppermute | solution.py:35
  504.1 28.9 %shard_map.228 = (f32[512,768]{1,0:T(8,128)}, bf16[512,768]{1,0:T(8,128)(2,1)}, bf16[2,3,384,512]{3,2,1,0:T(8,128)(2,1)}, bf16[2,3,384,512]{3,2,1,0:T(8,128)(2,1...) custom-call(s32[5]{0:T(128)} %copy-done.62, bf16[512,768]{1,0:T(8,128)(2,1)} %copy-done.37, ...), custom_call_target="tpu_custom_call" | custom-call | flops 9663676 | bytes 42516 | tf_op jit(solution)/shard_map/pallas_call | solution.py:84
  559.7 9.9 %collective-permute-done.74 = bf16[128,768]{1,0:T(8,128)(2,1)S(1)} collective-permute-done((bf16[128,768]{1,0:T(8,128)(2,1)S(1)}, bf16[128,768]{1,0:T(8,128)(2,1)S(1)}, u32[]{:S(2)}, u32[]{:S(2)}) %collective-permute-start.74) | collective-permute-done | bytes 196640 | tf_op jit(solution)/shard_map/ppermute | solution.py:35
  571.6 9.2 %collective-permute-done.75 = bf16[128,768]{1,0:T(8,128)(2,1)S(1)} collective-permute-done((bf16[128,768]{1,0:T(8,128)(2,1)S(1)}, bf16[128,768]{1,0:T(8,128)(2,1)S(1)}, u32[]{:S(2)}, u32[]{:S(2)}) %collective-permute-start.75) | collective-permute-done | bytes 196640 | tf_op jit(solution)/shard_map/ppermute | solution.py:35
  580.9 11.4 %collective-permute-done.76 = bf16[128,768]{1,0:T(8,128)(2,1)S(1)} collective-permute-done((bf16[128,768]{1,0:T(8,128)(2,1)S(1)}, bf16[128,768]{1,0:T(8,128)(2,1)S(1)}, u32[]{:S(2)}, u32[]{:S(2)}) %collective-permute-start.76) | collective-permute-done | bytes 196640 | tf_op jit(solution)/shard_map/ppermute | solution.py:35
  615.4 12.3 %shard_map.231 = (bf16[512,192]{1,0:T(8,128)(2,1)}, bf16[768,192]{1,0:T(8,128)(2,1)}, bf16[512,384]{1,0:T(8,128)(2,1)}, bf16[512,384]{1,0:T(8,128)(2,1)}) custom-call(s32[5]{0:T(128)} %copy-done.62, f32[1,1024]{1,0:T(1,128)} %bitcast.110, bf16[512,192]{1,0:T(8,128)(2,1)} %copy-done.49, bf16[1024,384]{1,0:T(8,128)(2,1)} %copy-done.27, ...), custom_call_target="tpu_custom_call" | custom-call | flops 1308622 | bytes 4624 | tf_op jit(solution)/shard_map/pallas_call | solution.py:84
  661.1 9.9 %collective-permute-done.87 = bf16[128,768]{1,0:T(8,128)(2,1)S(1)} collective-permute-done((bf16[128,768]{1,0:T(8,128)(2,1)S(1)}, bf16[128,768]{1,0:T(8,128)(2,1)S(1)}, u32[]{:S(2)}, u32[]{:S(2)}) %collective-permute-start.87) | collective-permute-done | bytes 196640 | tf_op jit(solution)/shard_map/ppermute | solution.py:35
  672.4 9.6 %collective-permute-done.88 = bf16[128,768]{1,0:T(8,128)(2,1)S(1)} collective-permute-done((bf16[128,768]{1,0:T(8,128)(2,1)S(1)}, bf16[128,768]{1,0:T(8,128)(2,1)S(1)}, u32[]{:S(2)}, u32[]{:S(2)}) %collective-permute-start.88) | collective-permute-done | bytes 196640 | tf_op jit(solution)/shard_map/ppermute | solution.py:35
  694.8 14.5 %collective-permute-done.92 = bf16[192,1536]{1,0:T(8,128)(2,1)S(1)} collective-permute-done((bf16[192,1536]{1,0:T(8,128)(2,1)S(1)}, bf16[192,1536]{1,0:T(8,128)(2,1)S(1)}, u32[]{:S(2)}, u32[]{:S(2)}) %collective-permute-start.92) | collective-permute-done | bytes 589856 | tf_op jit(solution)/shard_map/ppermute | solution.py:35
  725.4 41.9 %collective-permute-done.100 = bf16[4,192]{1,0:T(4,128)(2,1)S(1)} collective-permute-done((bf16[4,192]{1,0:T(4,128)(2,1)S(1)}, bf16[4,192]{1,0:T(4,128)(2,1)S(1)}, u32[]{:S(2)}, u32[]{:S(2)}) %collective-permute-start.100) | collective-permute-done | bytes 1568 | tf_op jit(solution)/shard_map/ppermute | solution.py:35
  (574 shorter events, 421.2 us)
Async XLA Ops:
  25.7 43.2 %collective-permute-start.6 = (bf16[8,3,192,512]{3,2,1,0:T(8,128)(2,1)}, bf16[8,3,192,512]{3,2,1,0:T(8,128)(2,1)}, u32[]{:S(2)}, u32[]{:S(2)}) collective-permute-start(bf16[8,3,192,512]{3,2,1,0:T(8,128)(2,1)} %get-tuple-element.344.refs_0_), channel_id=1, source_target_pairs={{0,8},{8,0},{16,24},{24,16},{1,9},{9,1},{17,25},{25,17},{2,10},{10... | collective-permute-start | bytes 14155784 | tf_op jit(solution)/shard_map/ppermute | solution.py:35
  71.5 48.5 %collective-permute-start.13 = (bf16[8,3,64,512]{3,2,1,0:T(8,128)(2,1)}, bf16[8,3,64,512]{3,2,1,0:T(8,128)(2,1)}, u32[]{:S(2)}, u32[]{:S(2)}) collective-permute-start(bf16[8,3,64,512]{3,2,1,0:T(8,128)(2,1)} %collective-permute-done.7.refs_2_), channel_id=1, source_target_pairs={{0,4},{4,0},{1,5},{5,1},{2,6},{6,2},{3,7},{7,3},{8,12},{12,8},{9,1... | collective-permute-start | bytes 4718600 | tf_op jit(solution)/shard_map/ppermute | solution.py:35
  73.0 47.0 %collective-permute-start.14 = (bf16[8,3,64,512]{3,2,1,0:T(8,128)(2,1)}, bf16[8,3,64,512]{3,2,1,0:T(8,128)(2,1)}, u32[]{:S(2)}, u32[]{:S(2)}) collective-permute-start(bf16[8,3,64,512]{3,2,1,0:T(8,128)(2,1)} %get-tuple-element.331), channel_id=1, source_target_pairs={{0,16},{8,24},{16,0},{24,8},{1,17},{9,25},{17,1},{25,9},{2,18},{10... | collective-permute-start | bytes 4718600 | tf_op jit(solution)/shard_map/ppermute | solution.py:35
  74.5 45.5 %collective-permute-start.15 = (bf16[8,3,64,512]{3,2,1,0:T(8,128)(2,1)}, bf16[8,3,64,512]{3,2,1,0:T(8,128)(2,1)}, u32[]{:S(2)}, u32[]{:S(2)}) collective-permute-start(bf16[8,3,64,512]{3,2,1,0:T(8,128)(2,1)} %collective-permute-done.7.refs_2_), channel_id=1, source_target_pairs={{0,8},{8,0},{16,24},{24,16},{1,9},{9,1},{17,25},{25,17},{2,10},{10... | collective-permute-start | bytes 4718600 | tf_op jit(solution)/shard_map/ppermute | solution.py:35
  120.1 68.1 %collective-permute-start.24 = (bf16[8,3,192,512]{3,2,1,0:T(8,128)(2,1)}, bf16[8,3,192,512]{3,2,1,0:T(8,128)(2,1)}, u32[]{:S(2)}, u32[]{:S(2)}) collective-permute-start(bf16[8,3,192,512]{3,2,1,0:T(8,128)(2,1)} %copy-done.11), channel_id=1, source_target_pairs={{0,8},{8,0},{16,24},{24,16},{1,9},{9,1},{17,25},{25,17},{2,10},{10... | collective-permute-start | bytes 14155784 | tf_op jit(solution)/shard_map/ppermute | solution.py:35
  130.2 58.0 %collective-permute-start.25 = (bf16[8,3,64,512]{3,2,1,0:T(8,128)(2,1)}, bf16[8,3,64,512]{3,2,1,0:T(8,128)(2,1)}, u32[]{:S(2)}, u32[]{:S(2)}) collective-permute-start(bf16[8,3,64,512]{3,2,1,0:T(8,128)(2,1)} %copy-done.87), channel_id=1, source_target_pairs={{0,16},{8,24},{16,0},{24,8},{1,17},{9,25},{17,1},{25,9},{2,18},{10... | collective-permute-start | bytes 4718600 | tf_op jit(solution)/shard_map/ppermute | solution.py:35
  209.4 86.1 %collective-permute-start.39 = (bf16[8,3,64,512]{3,2,1,0:T(8,128)(2,1)}, bf16[8,3,64,512]{3,2,1,0:T(8,128)(2,1)S(1)}, u32[]{:S(2)}, u32[]{:S(2)}) collective-permute-start(bf16[8,3,64,512]{3,2,1,0:T(8,128)(2,1)} %collective-permute-done.25.refs_2_), channel_id=1, source_target_pairs={{0,4},{4,0},{1,5},{5,1},{2,6},{6,2},{3,7},{7,3},{8,12},{12,8},{9,1... | collective-permute-start | bytes 4718600 | tf_op jit(solution)/shard_map/ppermute | solution.py:35
  213.7 81.8 %collective-permute-start.41 = (bf16[8,3,64,512]{3,2,1,0:T(8,128)(2,1)}, bf16[8,3,64,512]{3,2,1,0:T(8,128)(2,1)S(1)}, u32[]{:S(2)}, u32[]{:S(2)}) collective-permute-start(bf16[8,3,64,512]{3,2,1,0:T(8,128)(2,1)} %collective-permute-done.25.refs_2_), channel_id=1, source_target_pairs={{0,8},{8,0},{16,24},{24,16},{1,9},{9,1},{17,25},{25,17},{2,10},{10... | collective-permute-start | bytes 4718600 | tf_op jit(solution)/shard_map/ppermute | solution.py:35
  217.6 77.9 %collective-permute-start.40 = (bf16[8,3,64,512]{3,2,1,0:T(8,128)(2,1)S(1)}, bf16[8,3,64,512]{3,2,1,0:T(8,128)(2,1)S(1)}, u32[]{:S(2)}, u32[]{:S(2)}) collective-permute-start(bf16[8,3,64,512]{3,2,1,0:T(8,128)(2,1)S(1)} %copy-done.86), channel_id=1, source_target_pairs={{0,16},{8,24},{16,0},{24,8},{1,17},{9,25},{17,1},{25,9},{2,18},{10... | collective-permute-start | bytes 4718600 | tf_op jit(solution)/shard_map/ppermute | solution.py:35
  366.1 113.6 %collective-permute-start.67 = (bf16[4,3,384,512]{3,2,1,0:T(8,128)(2,1)}, bf16[4,3,384,512]{3,2,1,0:T(8,128)(2,1)}, u32[]{:S(2)}, u32[]{:S(2)}) collective-permute-start(bf16[4,3,384,512]{3,2,1,0:T(8,128)(2,1)} %get-tuple-element.464), channel_id=1, source_target_pairs={{0,16},{8,24},{16,0},{24,8},{1,17},{9,25},{17,1},{25,9},{2,18},{10... | collective-permute-start | bytes 14155784 | tf_op jit(solution)/shard_map/ppermute | solution.py:35
  487.2 157.5 %collective-permute-start.81 = (bf16[4,3,384,512]{3,2,1,0:T(8,128)(2,1)}, bf16[4,3,384,512]{3,2,1,0:T(8,128)(2,1)}, u32[]{:S(2)}, u32[]{:S(2)}) collective-permute-start(bf16[4,3,384,512]{3,2,1,0:T(8,128)(2,1)} %add_convert_fusion.part_ref), channel_id=1, source_target_pairs={{0,4},{4,0},{1,5},{5,1},{2,6},{6,2},{3,7},{7,3},{8,12},{12,8},{9,1... | collective-permute-start | bytes 14155784 | tf_op jit(solution)/shard_map/ppermute | solution.py:35
  489.3 43.7 %collective-permute-start.71 = (bf16[192,2432]{1,0:T(8,128)(2,1)}, bf16[192,2432]{1,0:T(8,128)(2,1)}, u32[]{:S(2)}, u32[]{:S(2)}) collective-permute-start(bf16[192,2432]{1,0:T(8,128)(2,1)} %add_convert_fusion.4), channel_id=1, source_target_pairs={{0,16},{8,24},{16,0},{24,8},{1,17},{9,25},{17,1},{25,9},{2,18},{10... | collective-permute-start | bytes 2801672 | tf_op jit(solution)/shard_map/ppermute | solution.py:35
  543.8 48.5 %collective-permute-start.49 = (bf16[128,768]{1,0:T(8,128)(2,1)S(1)}, bf16[128,768]{1,0:T(8,128)(2,1)S(1)}, u32[]{:S(2)}, u32[]{:S(2)}) collective-permute-start(bf16[128,768]{1,0:T(8,128)(2,1)S(1)} %add_convert_fusion.30), channel_id=1, source_target_pairs={{0,2},{1,3},{2,0},{3,1},{4,6},{5,7},{6,4},{7,5},{8,10},{9,11},{10,... | collective-permute-start | bytes 589832 | tf_op jit(solution)/shard_map/ppermute | solution.py:35
  543.9 83.8 %collective-permute-start.79 = (bf16[2,3,384,512]{3,2,1,0:T(8,128)(2,1)}, bf16[2,3,384,512]{3,2,1,0:T(8,128)(2,1)}, u32[]{:S(2)}, u32[]{:S(2)}) collective-permute-start(bf16[2,3,384,512]{3,2,1,0:T(8,128)(2,1)} %get-tuple-element.514), channel_id=1, source_target_pairs={{0,16},{8,24},{16,0},{24,8},{1,17},{9,25},{17,1},{25,9},{2,18},{10... | collective-permute-start | bytes 7077896 | tf_op jit(solution)/shard_map/ppermute | solution.py:35
  557.6 48.3 %collective-permute-start.50 = (bf16[128,768]{1,0:T(8,128)(2,1)S(1)}, bf16[128,768]{1,0:T(8,128)(2,1)S(1)}, u32[]{:S(2)}, u32[]{:S(2)}) collective-permute-start(bf16[128,768]{1,0:T(8,128)(2,1)S(1)} %add_convert_fusion.29.refs_0_), channel_id=1, source_target_pairs={{0,1},{1,0},{2,3},{3,2},{4,5},{5,4},{6,7},{7,6},{8,9},{9,8},{10,11... | collective-permute-start | bytes 589832 | tf_op jit(solution)/shard_map/ppermute | solution.py:35
  592.4 51.4 %collective-permute-start.82 = (bf16[192,2432]{1,0:T(8,128)(2,1)S(1)}, bf16[192,2432]{1,0:T(8,128)(2,1)}, u32[]{:S(2)}, u32[]{:S(2)}) collective-permute-start(bf16[192,2432]{1,0:T(8,128)(2,1)S(1)} %add_convert_fusion.3), channel_id=1, source_target_pairs={{0,4},{4,0},{1,5},{5,1},{2,6},{6,2},{3,7},{7,3},{8,12},{12,8},{9,1... | collective-permute-start | bytes 2801672 | tf_op jit(solution)/shard_map/ppermute | solution.py:35
  639.6 72.5 %collective-permute-start.95 = (bf16[2,3,384,512]{3,2,1,0:T(8,128)(2,1)S(1)}, bf16[2,3,384,512]{3,2,1,0:T(8,128)(2,1)S(1)}, u32[]{:S(2)}, u32[]{:S(2)}) collective-permute-start(bf16[2,3,384,512]{3,2,1,0:T(8,128)(2,1)S(1)} %add_convert_fusion.2.part_ref), channel_id=1, source_target_pairs={{0,4},{4,0},{1,5},{5,1},{2,6},{6,2},{3,7},{7,3},{8,12},{12,8},{9,1... | collective-permute-start | bytes 7077896 | tf_op jit(solution)/shard_map/ppermute | solution.py:35
  643.8 68.3 %collective-permute-start.96 = (bf16[2,3,384,512]{3,2,1,0:T(8,128)(2,1)}, bf16[2,3,384,512]{3,2,1,0:T(8,128)(2,1)S(1)}, u32[]{:S(2)}, u32[]{:S(2)}) collective-permute-start(bf16[2,3,384,512]{3,2,1,0:T(8,128)(2,1)} %get-tuple-element.563), channel_id=1, source_target_pairs={{0,16},{8,24},{16,0},{24,8},{1,17},{9,25},{17,1},{25,9},{2,18},{10... | collective-permute-start | bytes 7077896 | tf_op jit(solution)/shard_map/ppermute | solution.py:35
  654.0 55.3 %collective-permute-start.91 = (bf16[4,3,192,512]{3,2,1,0:T(8,128)(2,1)S(1)}, bf16[4,3,192,512]{3,2,1,0:T(8,128)(2,1)S(1)}, u32[]{:S(2)}, u32[]{:S(2)}) collective-permute-start(bf16[4,3,192,512]{3,2,1,0:T(8,128)(2,1)S(1)} %get-tuple-element.546), channel_id=1, source_target_pairs={{0,8},{8,0},{16,24},{24,16},{1,9},{9,1},{17,25},{25,17},{2,10},{10... | collective-permute-start | bytes 7077896 | tf_op jit(solution)/shard_map/ppermute | solution.py:35
  713.0 58.5 %collective-permute-start.104 = (bf16[2,3,384,512]{3,2,1,0:T(8,128)(2,1)S(1)}, bf16[2,3,384,512]{3,2,1,0:T(8,128)(2,1)S(1)}, u32[]{:S(2)}, u32[]{:S(2)}) collective-permute-start(bf16[2,3,384,512]{3,2,1,0:T(8,128)(2,1)S(1)} %add_convert_fusion.1.part_ref), channel_id=1, source_target_pairs={{0,4},{4,0},{1,5},{5,1},{2,6},{6,2},{3,7},{7,3},{8,12},{12,8},{9,1... | collective-permute-start | bytes 7077896 | tf_op jit(solution)/shard_map/ppermute | solution.py:35
  716.3 51.5 %collective-permute-start.101 = (bf16[192,896]{1,0:T(8,128)(2,1)S(1)}, bf16[192,896]{1,0:T(8,128)(2,1)S(1)}, u32[]{:S(2)}, u32[]{:S(2)}) collective-permute-start(bf16[192,896]{1,0:T(8,128)(2,1)S(1)} %add_convert_fusion.10), channel_id=1, source_target_pairs={{0,16},{8,24},{16,0},{24,8},{1,17},{9,25},{17,1},{25,9},{2,18},{10... | collective-permute-start | bytes 1032200 | tf_op jit(solution)/shard_map/ppermute | solution.py:35
  723.0 46.2 %collective-permute-start.105 = (bf16[2,3,192,512]{3,2,1,0:T(8,128)(2,1)S(1)}, bf16[2,3,192,512]{3,2,1,0:T(8,128)(2,1)S(1)}, u32[]{:S(2)}, u32[]{:S(2)}) collective-permute-start(bf16[2,3,192,512]{3,2,1,0:T(8,128)(2,1)S(1)} %get-tuple-element.586), channel_id=1, source_target_pairs={{0,8},{8,0},{16,24},{24,16},{1,9},{9,1},{17,25},{25,17},{2,10},{10... | collective-permute-start | bytes 3538952 | tf_op jit(solution)/shard_map/ppermute | solution.py:35
  723.1 44.2 %collective-permute-start.100 = (bf16[4,192]{1,0:T(4,128)(2,1)S(1)}, bf16[4,192]{1,0:T(4,128)(2,1)S(1)}, u32[]{:S(2)}, u32[]{:S(2)}) collective-permute-start(bf16[4,192]{1,0:T(4,128)(2,1)S(1)} %add_convert_fusion.44), channel_id=1, source_target_pairs={{0,4},{4,0},{1,5},{5,1},{2,6},{6,2},{3,7},{7,3},{8,12},{12,8},{9,1... | collective-permute-start | bytes 4616 | tf_op jit(solution)/shard_map/ppermute | solution.py:35
  724.7 55.2 %collective-permute-start.103 = (bf16[192,1536]{1,0:T(8,128)(2,1)S(1)}, bf16[192,1536]{1,0:T(8,128)(2,1)S(1)}, u32[]{:S(2)}, u32[]{:S(2)}) collective-permute-start(bf16[192,1536]{1,0:T(8,128)(2,1)S(1)} %add_convert_fusion.6), channel_id=1, source_target_pairs={{0,4},{4,0},{1,5},{5,1},{2,6},{6,2},{3,7},{7,3},{8,12},{12,8},{9,1... | collective-permute-start | bytes 1769480 | tf_op jit(solution)/shard_map/ppermute | solution.py:35
  (203 other events, 5684.8 us)

commit v3 on v2

--- a/solution.py
+++ b/solution.py
@@ -52,7 +52,7 @@
     count = lax.axis_size("tp")
     chunks = len(halves) // 2
     totals = [add(k, swap(g, "tp", 1)) for k, g in zip(halves[:chunks], halves[chunks:])]
-    totals = between(*totals)
+    totals[0] = between(totals[0])[0]
     step = 2
     while step < count:
         totals = [add(total, swap(total, "tp", step)) for total in totals]
@@ -69,7 +69,9 @@
     return part, swap(part, "ctx", step)
 
 
-def call(kernel, scal, grid, ins, outs, scratch=(), flops=0, exps=0, alias=None, limit=32):
+def call(
+    kernel, scal, grid, ins, outs, scratch=(), flops=0, exps=0, alias=None, limit=32, light=LIGHT
+):
     def spec(item):
         shape, block, index = item[0].shape, item[1], item[2]
         if block == "any":
@@ -94,7 +96,7 @@
         compiler_params=pltpu.CompilerParams(
             dimension_semantics=("arbitrary",) * len(grid), vmem_limit_bytes=limit * MIB
         ),
-        cost_estimate=pl.CostEstimate(flops=flops // LIGHT, transcendentals=0, bytes_accessed=moved // LIGHT),
+        cost_estimate=pl.CostEstimate(flops=flops // light, transcendentals=0, bytes_accessed=moved // light),
         input_output_aliases=alias or {},
     )(scal, *[i[0] for i in ins])
 
@@ -218,7 +220,16 @@
     return [slice(at, at + HEAD_DIM) for at in range(0, width, HEAD_DIM)]
 
 
-def attend_kernel(scal, path_ref, q_ref, kv_ref, *refs):
+def all_keys(scal, refs):
+    if len(refs) == 1:
+        return refs[0][...]
+    own, got = refs[0][...], refs[1][...]
+    first = scal[4] == 0
+    return jnp.concatenate([jnp.where(first, own, got), jnp.where(first, got, own)], axis=0)
+
+
+def attend_kernel(scal, path_ref, q_ref, *refs, parts):
+    kv_ref, refs = all_keys(scal, refs[:parts]), refs[parts:]
     packs, heads_ref, halves = refs[:4], refs[4], refs[5:]
     rows, width = q_ref.shape
     allowed = allowed_of(scal, path_ref, rows, kv_ref.shape[0])
@@ -233,7 +244,8 @@
     put_halves(pl.program_id(0), scal[1], mm(heads, weight, NT), halves)
 
 
-def attend_back_kernel(scal, path_ref, q_ref, kv_ref, d_ref, heads_ref, *refs):
+def attend_back_kernel(scal, path_ref, q_ref, d_ref, heads_ref, *refs, parts):
+    kv_ref, refs = all_keys(scal, refs[:parts]), refs[parts:]
     packs, (dq_ref, gout_ref), (dkv_refs, scratch) = refs[:4], refs[4:6], (refs[6:-2], refs[-2:])
     dkv_acc, gout_acc = scratch
     rows, width = q_ref.shape
@@ -341,36 +353,63 @@
             ref[:, at * hid : (at + 1) * hid] = grad[r * rows : (r + 1) * rows].astype(BF16)
 
 
-def load_pair(own_ref, sib_ref, pair, block):
-    half = own_ref.shape[0]
-    pair[:half, :] = own_ref[...]
-    pair[half:, :] = swap_pairs(sib_ref[...].astype(F32), block).astype(BF16)
-
-
-def one_hot_cols(pos_col, slots):
-    hit = lax.broadcasted_iota(jnp.int32, (pos_col.shape[0], slots), 1) == pos_col
-    return jnp.where(hit, 1.0, 0.0).astype(BF16)
-
-
-def hit_rows(pos_row, slots):
-    return lax.broadcasted_iota(jnp.int32, (slots, pos_row.shape[1]), 0) == pos_row
-
-
-def start_pair(own_ref, sib_ref, init_ref, pair, acc, block):
+def column(table_ref, rows, at):
+    values = table_ref[rows, :]
+    lane = lax.broadcasted_iota(jnp.int32, values.shape, 1)
+    return jnp.sum(jnp.where(lane == at, values, 0.0), axis=1, keepdims=True)
+
+
+def spread(first, second, places, weights):
+    one, two = weights
+    return jnp.where(places == first, one, jnp.where(places == second, two, 0.0)).astype(BF16)
+
+
+def rows_of(lists_ref, half, tokens, slots, weighted):
+    cut = slice(half * tokens, (half + 1) * tokens)
+    first, second, one, two = [lists_ref[at : at + 1, cut] for at in range(4)]
+    places = lax.broadcasted_iota(jnp.int32, (slots, tokens), 0)
+    weights = (one, two) if weighted else (1.0, 1.0)
+    return spread(first.astype(jnp.int32), second.astype(jnp.int32), places, weights)
+
+
+def cols_of(table_ref, half, tokens, slots, weighted):
+    cut = slice(half * tokens, (half + 1) * tokens)
+    first, second = [column(table_ref, cut, at).astype(jnp.int32) for at in range(2)]
+    weights = [column(table_ref, cut, at) for at in (2, 3)] if weighted else (1.0, 1.0)
+    places = lax.broadcasted_iota(jnp.int32, (tokens, slots), 1)
+    return spread(first, second, places, weights)
+
+
+def to_slots(own_ref, sib_ref, lists_ref, slot_ref, block, weighted):
     @pl.when(pl.program_id(0) == 0)
     def _():
-        half = own_ref.shape[0]
-        load_pair(own_ref, sib_ref, pair, block)
-        acc[:half, :] = init_ref[...]
-        acc[half:, :] = jnp.zeros_like(init_ref)
-
-
-def finish_pair(own_out, sib_out, acc):
+        tokens, slots = own_ref.shape[0], slot_ref.shape[1]
+        sib = swap_pairs(sib_ref[...].astype(F32), block).astype(BF16)
+        for half, values in enumerate((own_ref[...], sib)):
+            picks = rows_of(lists_ref, half, tokens, slots, weighted)
+            slot_ref[half] = mm(picks, values).astype(BF16)
+
+
+def from_slots(slot_ref, table_ref, own_out, sib_out, weighted):
     @pl.when(pl.program_id(0) == pl.num_programs(0) - 1)
     def _():
-        half = own_out.shape[0]
-        own_out[...] = acc[:half, :]
-        sib_out[...] = acc[half:, :].astype(BF16)
+        tokens, slots = own_out.shape[0], slot_ref.shape[1]
+        for half, ref in enumerate((own_out, sib_out)):
+            picks = cols_of(table_ref, half, tokens, slots, weighted)
+            ref[...] = mm(picks, slot_ref[half]).astype(ref.dtype)
+
+
+def of_expert(slot_ref):
+    count = slot_ref.shape[1] // pl.num_programs(0)
+    rows = pl.ds(pl.multiple_of(pl.program_id(0) * count, count), count)
+    return jnp.concatenate([slot_ref[0, rows, :], slot_ref[1, rows, :]], axis=0)
+
+
+def put_expert(slot_ref, values):
+    count = slot_ref.shape[1] // pl.num_programs(0)
+    rows = pl.ds(pl.multiple_of(pl.program_id(0) * count, count), count)
+    slot_ref[0, rows, :] = values[:count]
+    slot_ref[1, rows, :] = values[count:]
 
 
 def pack_kernel(scal, in_ref, out_ref, own_ref, first_ref, last_ref):
@@ -382,6 +421,9 @@
 
 
 def expert_weights(scal, refs):
+    if len(refs) == 4:
+        return [joined(refs, 0, part) for part in range(3)]
+
     def far(refs, part):
         straight, around, last = [ref[0, part] for ref in refs]
         low = jnp.where(scal[4] == 0, straight, around)
@@ -396,58 +438,58 @@
     ]
 
 
-def expert_kernel(scal, own_ref, sib_ref, init_ref, row_ref, col_ref, mix_ref, *refs, block):
-    weights, (own_out, sib_out, x_ref, gate_ref, up_ref, acc, pair) = refs[:8], refs[8:]
-    slots = x_ref.shape[1]
-    start_pair(own_ref, sib_ref, init_ref, pair, acc, block)
+def expert_kernel(scal, own_ref, sib_ref, lists_ref, table_ref, *refs, block, sources):
+    weights, (own_out, sib_out, x_ref, gate_ref, up_ref, x_all, y_all) = refs[:sources], refs[sources:]
+    to_slots(own_ref, sib_ref, lists_ref, x_all, block, False)
     w_gate, w_up, w_out = expert_weights(scal, weights)
-    hit = jnp.where(hit_rows(row_ref[0], slots), 1.0, 0.0).astype(BF16)
-    chosen = mm(hit, pair[...]).astype(BF16)
-    x_ref[0] = chosen
+    chosen = of_expert(x_all)
     gate = mm(chosen, w_gate)
     up = mm(chosen, w_up)
-    gate_ref[0] = gate
-    up_ref[0] = up
+    x_ref[0], gate_ref[0], up_ref[0] = chosen, gate.astype(BF16), up.astype(BF16)
     hidden = (gate / (1.0 + jnp.exp(-gate)) * up).astype(BF16)
-    rows = mm(hidden, w_out, NT).astype(BF16)
-    acc[...] += mix_ref[0] * mm(one_hot_cols(col_ref[0], slots), rows)
-    finish_pair(own_out, sib_out, acc)
+    put_expert(y_all, mm(hidden, w_out, NT).astype(BF16))
+    from_slots(y_all, table_ref, own_out, sib_out, True)
 
 
 def expert_back_kernel(
-    scal, own_ref, sib_ref, init_ref, row_ref, col_ref, mix_ref, x_ref, gate_ref, up_ref, *refs,
-    block, chunks
+    scal, own_ref, sib_ref, lists_ref, table_ref, a_ref, b_ref, *refs, block, sizes, sources, fresh
 ):
-    weights, (own_out, sib_out), grads = refs[:8], refs[8:10], refs[10:-2]
-    acc, pair = refs[-2:]
-    slots = x_ref.shape[1]
-    start_pair(own_ref, sib_ref, init_ref, pair, acc, block)
+    given, refs = ((), refs) if fresh else (refs[:1], refs[1:])
+    weights, refs = refs[:sources], refs[sources:]
+    (own_out, sib_out), grads, refs = refs[:2], refs[2 : 2 + 2 * len(sizes)], refs[2 + 2 * len(sizes) :]
+    to_slots(own_ref, sib_ref, lists_ref, refs[-1], block, True)
     w_gate, w_up, w_out = expert_weights(scal, weights)
-    hit = hit_rows(row_ref[0], slots)
-    weight = jnp.sum(jnp.where(hit, mix_ref[0], 0.0), axis=1, keepdims=True)
-    hit = jnp.where(hit, 1.0, 0.0).astype(BF16)
-    d_rows = (mm(hit, pair[...]) * weight).astype(BF16)
-    hidden, d_gate, d_up = glu_back(gate_ref[0], up_ref[0], mm(d_rows, w_out))
-    chosen = x_ref[0]
+    d_rows = of_expert(refs[-1])
+    if fresh:
+        own_next, sib_next, x_all, y_all = refs[:4]
+        to_slots(a_ref, b_ref, lists_ref, x_all, block, False)
+        chosen = of_expert(x_all)
+        gate, up = mm(chosen, w_gate), mm(chosen, w_up)
+    else:
+        chosen, gate, up = a_ref[0], b_ref[0].astype(F32), given[0][0].astype(F32)
+    hidden, d_gate, d_up = glu_back(gate, up, mm(d_rows, w_out))
+    if fresh:
+        put_expert(y_all, mm(hidden, w_out, NT).astype(BF16))
+        from_slots(y_all, table_ref, own_next, sib_next, True)
     step = pl.program_id(0)
-    per_chunk = pl.num_programs(0) // chunks
     parts = (mm(chosen, d_gate, TN), mm(chosen, d_up, TN), mm(d_rows, hidden, TN))
     parts = [p.astype(BF16) for p in parts]
-    for chunk in range(chunks):
-
-        @pl.when(step // per_chunk == chunk)
+    for chunk, size in enumerate(sizes):
+        first = sum(sizes[:chunk])
+
+        @pl.when((step >= first) & (step < first + size))
         def _():
             for at in range(3):
                 grads[2 * chunk][0, at] = parts[at][: 2 * block]
                 grads[2 * chunk + 1][0, at] = parts[at][2 * block :]
 
     d_x = mm(d_gate, w_gate, NT) + mm(d_up, w_up, NT)
-    acc[...] += mm(one_hot_cols(col_ref[0], slots), d_x.astype(BF16))
-    finish_pair(own_out, sib_out, acc)
-
-
-def join_kernel(scal, own_ref, got_ref, *halves, block):
-    part = own_ref[...] + swap_pairs(got_ref[...].astype(F32), block)
+    put_expert(refs[-1], d_x.astype(BF16))
+    from_slots(refs[-1], table_ref, own_out, sib_out, False)
+
+
+def join_kernel(scal, own_ref, got_ref, shared_ref, *halves, block):
+    part = own_ref[...] + shared_ref[...] + swap_pairs(got_ref[...].astype(F32), block)
     put_halves(pl.program_id(0), scal[1], part, halves)
 
 
@@ -506,30 +548,82 @@
 def other_kernel(scal, got_ref, *refs):
     store_expert(*refs[-2:], *[got_ref[0, at].astype(F32) for at in range(3)])
 
-CHUNKS, PARTS = 2, (2, 1)
+
+def packed_kernel(scal, part_ref, got_ref, *refs, first, shared, blocks):
+    total = part_ref[...].astype(F32) + got_ref[...].astype(F32)
+    if first is not None:
+        refs, (qkv_ref, out_ref) = refs[:-2], refs[-2:]
+        width = qkv_ref.shape[3]
+        for at, col in enumerate((QUERY, KEYS, KEYS + width)):
+            qkv_ref[0, at] = total[:, first + col : first + col + width]
+        out_ref[0] = total[:, first + OUT : first + OUT + width].T
+    if shared:
+        sin_ref, sout_ref = refs[-2:]
+        hid = sout_ref.shape[2]
+        for at in range(2):
+            for col in range(blocks):
+                rows = pl.ds(col * 2 + at, total.shape[0], stride=2 * blocks)
+                lanes = at * hid + col * 128
+                sin_ref[0, rows, :] = total[:, lanes : lanes + 128]
+        sout_ref[0] = total[:, 2 * hid : 3 * hid]
+
+CHUNKS, PARTS = 2, ((1, 1, 1, 1), (2, 1, 1))
 SLOTS = {
     "start": ["pack 0", ("experts", 0)],
     ("attend", 0): ["slots"],
     ("attend half", 0): [("experts", 0), "pack 1"],
-    ("mixed", 0): [("experts", 0), "pack 1", ("experts", 1), "pack 2"],
-    ("branch half", 0): [("experts", 1), "pack 2"],
+    ("attend sum", 0): ["pack 2", ("experts", 1)],
+    ("mixed", 0): [("experts", 0), "pack 1", "pack 2"],
+    ("experts", 0): ["pack 1", "pack 2", ("experts", 1)],
     ("attend sum", 1): [("experts", 1)],
+    ("mixed", 1): [("experts", 1)],
     (1, "experts"): [(1, 0)],
+    (1, "attention"): [(1, 0), (1, 1)],
     (1, "project"): [(1, "packs")],
-    (1, "attention sum"): [(1, 0), (1, "packs")],
-    (0, "experts"): [(1, "packs"), (0, 0)],
-    (0, "ffn sum"): [(0, "shared")],
-    (0, "attention"): [(0, 0), (0, 1)],
-    (0, "project"): [(1, 0), (1, "packs"), (0, "shared"), (0, "attention")],
-    (0, "attention sum"): [(1, 0), (0, "shared"), (0, "attention")],
-    (0, "input"): [(0, 0), (0, 1)],
+    (1, "attention half"): [(1, 1), (1, 2)],
+    (1, "input"): [(1, 0), (1, 2), (1, "packs")],
+    (0, "experts"): [(1, 1), (1, "packs"), (0, 0)],
+    (0, "ffn half"): [(1, 0), (1, 2), (0, 0), (0, 1)],
+    (0, "ffn sum"): [(1, 1), (0, 1), (0, 2), (0, "shared")],
+    (0, "attention"): [(1, "packs"), (0, 0), (0, 2), (0, 3)],
+    (0, "project"): [(0, "attention"), "result"],
+    (0, "attention half"): [(1, 2), (0, 1), (0, 3), (0, "shared")],
+    (0, "attention sum"): [(0, 0), (0, 2), (0, "shared"), (0, "attention"), "result"],
+    (0, "input"): [(0, 1), (0, "attention")],
 }
 TAIL = (
-    ["gains", (0, "shared"), (0, "attention")],
-    ["gains", (0, 0), (0, "attention")],
-    ["gains", (0, 1)],
-    [(0, 1)],
+    ["gains", (0, "shared"), (0, "attention"), (0, 3), (0, 2)],
+    ["gains", "result"],
+    ["gains", (0, 3)],
 )
+
+
+class Packs:
+    def __init__(self, scal, layers, block, hid, width):
+        self.scal, self.blocks = scal, hid // 128
+        self.shapes = (
+            sds((layers, block * 2 * self.blocks, 128), F32),
+            sds((layers, block, hid), F32),
+            sds((layers, 3, block, width), F32),
+            sds((layers, width, block), F32),
+        )
+        self.held = [None] * 4
+
+    def put(self, layer, first, shared, part, got):
+        used = [0, 1] * shared + [2, 3] * (first is not None)
+        before = [at for at in used if self.held[at] is not None]
+        slot = lambda s: (s, (1,) + s.shape[1:], lambda *_: (layer,) + (0,) * (len(s.shape) - 1))
+        results = call(
+            functools.partial(packed_kernel, first=first, shared=shared, blocks=self.blocks),
+            self.scal,
+            (1,),
+            [whole(part), whole(got)] + [(self.held[at], "any", None) for at in before],
+            [slot(self.shapes[at]) for at in used],
+            alias={3 + n: used.index(at) for n, at in enumerate(before)},
+            limit=16,
+        )
+        for at, result in zip(used, results):
+            self.held[at] = result
 
 
 class Outs:
@@ -574,13 +668,13 @@
     yield []
 
 
-def pack_flow(place, name, parts):
+def pack_flow(done, parts):
     parts = yield list(parts)
     own, far, got, far_got = yield [parts[0], parts[2], swap(parts[1], "fsdp", 1), swap(parts[3], "fsdp", 1)]
     own, far = add(own, got), add(far, far_got)
     own, got = yield [own, swap(far, "fsdp", 2)]
     part, got = yield list(ctx_last(add(own, got)))
-    place[name] = part.astype(F32) + got.astype(F32)
+    done(part, got)
     yield []
 
 
@@ -595,7 +689,18 @@
     yield []
 
 
+def plain_flow(place, at, own, first, last):
+    (own,) = yield [own]
+    (own,) = yield [own]
+    own, far = yield [own, swap(own, "fsdp", 2)]
+    near = swap(own, "fsdp", 1)
+    near, far, cross = yield [near, far, swap(far, "fsdp", 1)]
+    place[at] = [own, near, far, cross]
+    yield []
+
+
 def block_flow(place, at, own):
+    (own,) = yield [own]
     (own,) = yield [own]
     own, far = yield [own, swap(own, "fsdp", 2)]
     place[at] = [own, swap(own, "fsdp", 1), far, swap(far, "fsdp", 1)]
@@ -676,18 +781,17 @@
     anc_row = lax.dynamic_slice_in_dim(ancestors, here * rows // segment, 1, 0)
     path = jnp.repeat(anc_row, segment, axis=1)
 
-    chosen = routes[0][:, :, None] == jnp.arange(experts, dtype=jnp.int32)[None, None, :]
-    mixing = jnp.sum(jnp.where(chosen, gates[0][:, :, None], 0.0), axis=1)
-    mixing = jnp.concatenate([mixing, swap(mixing, "fsdp", 1)], axis=0)
-    mixing = lax.dynamic_slice_in_dim(mixing, core * per_core, per_core, 1)
-    named = mixing > 0.0
-    pair = mixing.shape[0]
-    earlier = (jnp.arange(pair)[:, None] > jnp.arange(pair)[None, :]).astype(BF16)
-    slot = mm(earlier, named.astype(BF16)).astype(jnp.int32)
-    slot = jnp.where(named, slot, -1).T
-    mixing = mixing.T
-    slot_row, slot_col = slot[:, None, :], slot[:, :, None]
-    mix_row, mix_col = mixing[:, None, :], mixing[:, :, None]
+    places = 3 * rows // 8
+    info = jnp.concatenate([routes[0].astype(F32), gates[0]], axis=1)
+    info = jnp.concatenate([info, swap(info, "fsdp", 1)], axis=0)
+    local = info[:, :2].astype(jnp.int32) - core * per_core
+    hits = local[:, :, None] == jnp.arange(per_core, dtype=jnp.int32)
+    at = jnp.arange(2 * rows)
+    earlier = (at[:, None] > at[None, :]) & (at[:, None] // rows == at[None, :] // rows)
+    before = mm(earlier.astype(BF16), jnp.any(hits, axis=1).astype(BF16))
+    slot = before[:, None, :] + places * jnp.arange(per_core, dtype=F32)
+    slot = jnp.sum(jnp.where(hits, slot + 1.0, 0.0), axis=2) - 1.0
+    table = jnp.concatenate([slot, info[:, 2:]], axis=1)
 
     lead = lambda a: (
         a,
@@ -697,7 +801,7 @@
 
     matrix = 2 * rows * width
     expert_flops = 2 * per_core * capacity * width * hid
-    pair_scratch = [pltpu.VMEM((2 * rows, width), F32), pltpu.VMEM((2 * rows, width), BF16)]
+    slot_scratch = [pltpu.VMEM((2, per_core * places, width), BF16)]
     halves = half_shapes(rows, width, CHUNKS)
     row_f32, row_bf16 = sds((rows, width), F32), sds((rows, width), BF16)
 
@@ -709,6 +813,8 @@
 
     def slot(name, *values):
         names = SLOTS.get(name, ())
+        if not names:
+            return list(values)
         values, arrays = lax.optimization_barrier((list(values), [held[n] for n in names]))
         for n, a in zip(names, arrays):
             if n == "slots":
@@ -726,14 +832,15 @@
     small, routed = {}, {}
     open_flow("pack 0", block_flow(small, 0, pack_attention(0)))
     for at in range(layers):
-        open_flow(("experts", at), weight_flow(routed, at, *pack_experts(at)))
+        kind = weight_flow if at == 0 else plain_flow
+        open_flow(("experts", at), kind(routed, at, *pack_experts(at)))
     open_flow("pack 1", block_flow(small, 1, jnp.concatenate(pack_shared(0), axis=1)))
     rest = [pack_attention(at) for at in range(1, layers)]
     rest = [v for pack in rest for v in (pack, jnp.zeros((block, 128), BF16))]
     rest += [v for at in range(1, layers) for v in pack_shared(at)]
     open_flow("pack 2", block_flow(small, 2, jnp.concatenate(rest, axis=1)))
 
-    held["slots"] = [slot_row, slot_col, mix_row, mix_col]
+    held["slots"] = [table.T, table]
 
     def attention_ins(at):
         if at == 0:
@@ -757,8 +864,48 @@
         [tiled(row_bf16)] * 2,
     )
     finish("pack 0")
+    finish("pack 0")
     slot("start")
 
+    def experts_forward(at, own_in, sib_in):
+        kept = [lead(sds((per_core, capacity, width), BF16))]
+        kept += [lead(sds((per_core, capacity, hid), BF16))] * 2
+        return call(
+            functools.partial(
+                expert_kernel, block=block, sources=len(routed[at])
+            ),
+            scal,
+            (per_core,),
+            [whole(own_in), whole(sib_in), whole(tables[0]), whole(tables[1])] + expert_ins(at),
+            [whole(row_f32), whole(row_bf16)] + kept,
+            scratch=slot_scratch * 2,
+            flops=5 * expert_flops,
+            limit=48,
+        )
+
+    def join(own, sib, shared_part):
+        return call(
+            functools.partial(join_kernel, block=block),
+            scal,
+            (2,),
+            [tiled(own), tiled(swap(sib, "fsdp", 1)), tiled(shared_part)],
+            halves,
+        )
+
+    def result_flow(mixed, own, sib, branch):
+        own, sib = yield [own, sib]
+        part = yield list(join(own, sib, branch))
+        arrivals = yield tp_sum(part, lambda *values: values)
+        (result[0],) = call(
+            functools.partial(last_kernel, block=block),
+            scal,
+            (2,),
+            [tiled(mixed)] + [whole(a) for a in arrivals],
+            [tiled(row_bf16)],
+        )
+        yield []
+
+    result = [None]
     saved = []
     mixed = arrivals = None
     for at in range(layers):
@@ -782,12 +929,15 @@
                 flops=matrix * 576,
             )
         (kv,) = slot(("project", at), kv)
-        kv = lax.all_gather(kv, "ctx", axis=0, tiled=True)
+        if ctx == 2:
+            kv = [kv, swap(kv, "ctx", 1)]
+        else:
+            kv = [lax.all_gather(kv, "ctx", axis=0, tiled=True)]
         heads, *part = call(
-            attend_kernel,
+            functools.partial(attend_kernel, parts=len(kv)),
             scal,
             (2,),
-            [whole(path), tiled(query), whole(kv)] + weights,
+            [whole(path), tiled(query)] + [whole(k) for k in kv] + weights,
             [tiled(sds((rows, heads_width), BF16))] + halves,
             flops=4 * rows * tree_len * heads_width + matrix * heads_width,
             exps=rows * tree_len * heads_width // HEAD_DIM,
@@ -805,6 +955,9 @@
         )
         sib_in = swap(ffn_in, "fsdp", 1)
         ffn_in, sib_in = slot(("mixed", at), ffn_in, sib_in)
+        if at + 1 < layers:
+            own, sib, *hidden = experts_forward(at, ffn_in, sib_in)
+            own, sib = slot(("experts", at), own, sib)
         branch, gate, up = call(
             shared_kernel,
             scal,
@@ -814,48 +967,22 @@
             flops=3 * matrix * hid,
             exps=rows * hid,
         )
-        own, sib, x, e_gate, e_up = call(
-            functools.partial(expert_kernel, block=block),
-            scal,
-            (per_core,),
-            [whole(ffn_in), whole(sib_in), whole(branch)]
-            + [lead(tables[at]) for at in (0, 1, 3)]
-            + expert_ins(at),
-            [whole(row_f32), whole(row_bf16), lead(sds((per_core, capacity, width), BF16))]
-            + [lead(sds((per_core, capacity, hid), F32))] * 2,
-            scratch=pair_scratch,
-            flops=5 * expert_flops,
-            exps=per_core * capacity * hid,
-            limit=48,
-        )
-        own, sib = slot(("experts", at), own, sib)
-        part = call(
-            functools.partial(join_kernel, block=block),
-            scal,
-            (2,),
-            [tiled(own), tiled(swap(sib, "fsdp", 1))],
-            halves,
-        )
-        saved.append(
-            (stream, normed, query, kv, heads, mixed, ffn_in, gate, up, x, e_gate, e_up)
-        )
-        part = slot(("join", at), *part)
-        arrivals = tp_sum(part, functools.partial(slot, ("branch half", at)))
-        arrivals = slot(("branch sum", at), *arrivals)
-    (result,) = call(
-        functools.partial(last_kernel, block=block),
-        scal,
-        (2,),
-        [tiled(mixed)] + [whole(a) for a in arrivals],
-        [tiled(row_bf16)],
-    )
+        if at + 1 < layers:
+            part = join(own, sib, branch)
+            part = slot(("join", at), *part)
+            arrivals = tp_sum(part, functools.partial(slot, ("branch half", at)))
+            arrivals = slot(("branch sum", at), *arrivals)
+        else:
+            hidden = [ffn_in, sib_in]
+        saved.append((stream, normed, query, kv, heads, mixed, ffn_in, gate, up, hidden))
 
     outs = Outs(scal, layers, experts, block, hid)
-    packed = {}
+    packed = Packs(scal, layers, block, hid, heads_width)
+    gain_sums = []
     gain_grads = [None] * (2 * layers)
     d_next, d_branch = cot, cot
     for at in reversed(range(layers)):
-        stream, normed, query, kv, heads, mixed, ffn_in, gate, up, x, e_gate, e_up = saved[at]
+        stream, normed, query, kv, heads, mixed, ffn_in, gate, up, hidden = saved[at]
         weights = attention_ins(at)
         sib_d = swap(d_branch, "fsdp", 1)
         d_ffn, *g_shared = call(
@@ -867,40 +994,40 @@
             flops=6 * matrix * hid,
             exps=rows * hid,
         )
-        chunks = PARTS[at]
-        size = per_core // chunks
-        part_of = lambda chunk: (
+        sizes = PARTS[at]
+        fresh = len(hidden) == 2
+        part_of = lambda first, size: (
             sds((size, 3, 2 * block, hid), BF16),
             (1, 3, 2 * block, hid),
-            lambda e, s: (jnp.clip(e - chunk * size, 0, size - 1), 0, 0, 0),
+            lambda e, s: (jnp.clip(e - first, 0, size - 1), 0, 0, 0),
         )
         own, sib, *grads = call(
-            functools.partial(expert_back_kernel, block=block, chunks=chunks),
+            functools.partial(
+                expert_back_kernel, block=block, sizes=sizes, fresh=fresh,
+                sources=len(routed[at])
+            ),
             scal,
             (per_core,),
-            [whole(d_branch), whole(sib_d), whole(d_ffn)]
-            + [lead(a) for a in (*tables[:3], x, e_gate, e_up)]
+            [whole(d_branch), whole(sib_d), whole(tables[0]), whole(tables[1])]
+            + [whole(a) if fresh else lead(a) for a in hidden]
             + expert_ins(at),
             [whole(row_f32), whole(row_bf16)]
-            + [part_of(chunk) for chunk in range(chunks) for _ in range(2)],
-            scratch=pair_scratch,
+            + [part_of(sum(sizes[:n]), size) for n, size in enumerate(sizes) for _ in range(2)]
+            + [whole(row_f32), whole(row_bf16)] * fresh,
+            scratch=slot_scratch * (3 if fresh else 1),
             flops=8 * expert_flops,
             exps=per_core * capacity * hid,
             limit=56,
         )
-        for chunk in range(chunks):
+        for chunk in range(len(sizes)):
             near, far = grads[2 * chunk : 2 * chunk + 2]
-            open_flow((at, chunk), expert_flow(outs, near, far, at, chunk * size))
+            open_flow((at, chunk), expert_flow(outs, near, far, at, sum(sizes[:chunk])))
+        if fresh:
+            open_flow("result", result_flow(mixed, *grads[-2:], branch))
         if at == 0:
-            open_flow((0, "shared"), pack_flow(packed, (0, "shared"), g_shared))
+            open_flow((0, "shared"), pack_flow(functools.partial(packed.put, 0, None, True), g_shared))
         own, sib = slot((at, "experts"), own, sib)
-        part = call(
-            functools.partial(join_kernel, block=block),
-            scal,
-            (2,),
-            [tiled(own), tiled(swap(sib, "fsdp", 1))],
-            halves,
-        )
+        part = join(own, sib, d_ffn)
         part = slot((at, "join"), *part)
         arrivals = tp_sum(part, functools.partial(slot, (at, "ffn half")))
         arrivals = slot((at, "ffn sum"), *arrivals)
@@ -915,10 +1042,12 @@
         kv_shape = sds((rows, 2 * heads_width), BF16)
         kv_outs = [kv_shape] * 2 if ctx == 2 else [sds((tree_len, 2 * heads_width), BF16)]
         dq, g_out, *dkv = call(
-            attend_back_kernel,
+            functools.partial(attend_back_kernel, parts=len(kv)),
             scal,
             (2,),
-            [whole(path), tiled(query), whole(kv), tiled(d_attn), tiled(heads)] + weights,
+            [whole(path), tiled(query), tiled(d_attn), tiled(heads)]
+            + [whole(k) for k in kv]
+            + weights,
             [tiled(sds((rows, heads_width), BF16)), whole(sds((width, heads_width), BF16))]
             + [whole(k) for k in kv_outs],
             scratch=[
@@ -946,10 +1075,10 @@
         )
         g_attention = [g0, g1, g2, g3]
         if at == 0:
-            open_flow((0, "attention"), pack_flow(packed, (0, "attention"), g_attention))
+            open_flow((0, "attention"), pack_flow(functools.partial(packed.put, 0, 0, False), g_attention))
         else:
             both = [jnp.concatenate(g, axis=1) for g in zip(g_shared, g_attention)]
-            open_flow((at, "packs"), pack_flow(packed, at, both))
+            open_flow((at, "packs"), pack_flow(functools.partial(packed.put, at, 3 * hid, True), both))
         part = slot((at, "project"), *part)
         arrivals = tp_sum(part, functools.partial(slot, (at, "attention half")))
         arrivals = slot((at, "attention sum"), *arrivals)
@@ -969,27 +1098,25 @@
             (d_branch,) = rest
     gains = jnp.concatenate(gain_grads, axis=0).astype(BF16)
     cuts = [gains[:, r * block : (r + 1) * block] for r in range(4)]
-    open_flow("gains", pack_flow(packed, "gains", cuts))
+    open_flow("gains", pack_flow(lambda *v: gain_sums.extend(v), cuts))
     finish("gains")
     for step in TAIL:
         finish(*step)
-    gains = packed["gains"]
-    later = [packed[at] for at in range(1, layers)]
-    g_shared = jnp.stack([packed[0, "shared"]] + [p[:, : 3 * hid] for p in later])
-    g_attention = jnp.stack([packed[0, "attention"]] + [p[:, 3 * hid :] for p in later])
-    cut = lambda first: g_attention[:, :, first : first + heads_width]
+    gains = gain_sums[0].astype(F32) + gain_sums[1].astype(F32)
+    g_sin, g_sout, g_qkv, g_attention_out = packed.held
     g_in, g_out = outs.held
     blocks = hid // 128
     g_in = g_in.reshape(layers * experts * block, blocks, 2, 128).transpose(0, 2, 1, 3)
+    g_sin = g_sin.reshape(layers * block, blocks, 2, 128).transpose(0, 2, 1, 3)
     return (
-        result[None],
+        result[0][None],
         d_next[None],
         gains[:layers],
         gains[layers:],
-        jnp.stack([cut(QUERY), cut(KEYS), cut(KEYS + heads_width)], axis=2),
-        cut(OUT).transpose(0, 2, 1),
-        g_shared[:, :, : 2 * hid].reshape(layers, block, 2, hid),
-        g_shared[:, :, 2 * hid :].transpose(0, 2, 1),
+        g_qkv.transpose(0, 2, 1, 3),
+        g_attention_out,
+        g_sin.reshape(layers, block, 2, hid),
+        g_sout.transpose(0, 2, 1),
         g_in.reshape(layers, experts, block, 2, hid),
         g_out.transpose(0, 1, 3, 2),
     )

time: 799 us -> 703 us (0.88)
  blocking collectives: 43.3 us -> 0 us
  waiting for transfers between devices: 374 us -> 348 us
  local copies, waits for them, and re-layouts: 75 us -> 50.5 us
  starting transfers between devices: 74.1 us -> 87.1 us
  other arithmetic: 26.7 us -> 15 us
    all_gather x2 -> x0, blocking collectives: 43.3 us -> none  [shards(): kv = lax.all_gather(kv, 'ctx', axis=0, tiled=True)]
    ppermute x107 -> x117, waiting for transfers between devices: 374 us -> 348 us  [swap(): return lax.ppermute(values, axis, [(k, k ^ mask) for k in range(count)])]
    unnamed x249 -> x297, local copies, waits for them, and re-layouts: 52.3 us -> 36.7 us
    ppermute x107 -> x117, starting transfers between devices: 74.1 us -> 87.1 us  [swap(): return lax.ppermute(values, axis, [(k, k ^ mask) for k in range(count)])]
    pallas_call x36 -> x46, Pallas kernels: 197 us -> 191 us  [call(): pl.pallas_call(kernel, out_shape=[o[0] for o in outs], grid_spec=pltpu.Pr...]
    convert_element_type x45 -> x50, other arithmetic: 20.1 us -> 14.5 us  [add(): return (a.astype(F32) + b.astype(F32)).astype(BF16)]
  transfers between devices with their start and end apart: 107 -> 117, of which waited for: 54 -> 67; matrix products, arithmetic and copies ran while one was open for 7% -> 5% of each run, Pallas kernels for 21% -> 23%
where the time goes in v3:
time: 703 us; the launch traced here: 695 us
  waiting for transfers between devices  348 us (50%)
  Pallas kernels  191 us (27%)
  starting transfers between devices  87.1 us (12%)
  local copies, waits for them, and re-layouts  50.5 us (7%)
  other arithmetic  15 us (2%)
    ppermute x117, waiting for transfers between devices, swap(): return lax.ppermute(values, axis, [(k, k ^ mask) for k in range(count)])  348 us
    pallas_call x46, Pallas kernels, call(): pl.pallas_call(kernel, out_shape=[o[0] for o in outs], grid_spec=pltpu.Pr...  191 us
    ppermute x117, starting transfers between devices, swap(): return lax.ppermute(values, axis, [(k, k ^ mask) for k in range(count)])  87.1 us
    unnamed x297, local copies, waits for them, and re-layouts  36.7 us
    convert_element_type x50, other arithmetic, add(): return (a.astype(F32) + b.astype(F32)).astype(BF16)  14.5 us
  transfers between devices with their start and end apart: 117, of which 67 were waited for; matrix products, arithmetic and copies ran while one was open for 5% of the time, Pallas kernels for 23%

profile of v3, /device:TPU:0, one launch (start us, length us, event | category | flops | bytes accessed | tf_op | source)
XLA Modules:
  0.0 694.9 jit_solution(7610753443148688890)
XLA Ops:
  9.2 6.9 copy.111
  40.0 9.8 %collective-permute-done.3.refs_1_ = bf16[512,384]{1,0:T(8,128)(2,1)S(1)} collective-permute-done((bf16[512,384]{1,0:T(8,128)(2,1)S(1)}, bf16[512,384]{1,0:T(8,128)(2,1)S(1)}, u32[]{:S(2)}, u32[]{:S(2)}) %collective-permute-start.3) | collective-permute-done | bytes 393248 | tf_op jit(solution)/shard_map/ppermute | solution.py:35
  77.3 8.0 %collective-permute-done.8 = bf16[128,768]{1,0:T(8,128)(2,1)S(1)} collective-permute-done((bf16[128,768]{1,0:T(8,128)(2,1)S(1)}, bf16[128,768]{1,0:T(8,128)(2,1)S(1)}, u32[]{:S(2)}, u32[]{:S(2)}) %collective-permute-start.8) | collective-permute-done | bytes 196640 | tf_op jit(solution)/shard_map/ppermute | solution.py:35
  117.7 12.3 %shard_map.210 = (f32[512,768]{1,0:T(8,128)S(1)}, bf16[512,768]{1,0:T(8,128)(2,1)S(1)}, bf16[4,384,768]{2,1,0:T(8,128)(2,1)}, bf16[4,384,512]{2,1,0:T(8,128)(2,1)S(1)}, bf16[4,384,512]{2,1,0:T(8,128)(2,1)}) custom-call(s32[5]{0:T(128)S(1)} %stack.23.scal, bf16[512,768]{1,0:T(8,128)(2,1)S(1)} %copy-done.32, bf16[512,768]{1,0:T(8,128)(2,1)S(1)} %copy-done.88, ...), custom_call_target="tpu_custom_call" | custom-call | flops 6039797 | bytes 28344 | tf_op jit(solution)/shard_map/pallas_call | solution.py:86
  130.0 15.2 %collective-permute-done.19.refs_2_.refs_6_.refs_10_ = bf16[192,1536]{1,0:T(8,128)(2,1)S(1)} collective-permute-done((bf16[192,1536]{1,0:T(8,128)(2,1)S(1)}, bf16[192,1536]{1,0:T(8,128)(2,1)S(1)}, u32[]{:S(2)}, u32[]{:S(2)}) %collective-permute-start.19) | collective-permute-done | bytes 589856 | tf_op jit(solution)/shard_map/ppermute | solution.py:35
  169.5 9.3 %collective-permute-done.25 = bf16[128,768]{1,0:T(8,128)(2,1)S(1)} collective-permute-done((bf16[128,768]{1,0:T(8,128)(2,1)S(1)}, bf16[128,768]{1,0:T(8,128)(2,1)S(1)}, u32[]{:S(2)}, u32[]{:S(2)}) %collective-permute-start.25) | collective-permute-done | bytes 196640 | tf_op jit(solution)/shard_map/ppermute | solution.py:35
  194.1 9.0 %collective-permute-done.32.refs_1_ = bf16[512,384]{1,0:T(8,128)(2,1)S(1)} collective-permute-done((bf16[512,384]{1,0:T(8,128)(2,1)S(1)}, bf16[512,384]{1,0:T(8,128)(2,1)S(1)}, u32[]{:S(2)}, u32[]{:S(2)}) %collective-permute-start.32) | collective-permute-done | bytes 393248 | tf_op jit(solution)/shard_map/ppermute | solution.py:35
  211.2 7.7 %collective-permute-done.33 = bf16[128,768]{1,0:T(8,128)(2,1)S(1)} collective-permute-done((bf16[128,768]{1,0:T(8,128)(2,1)S(1)}, bf16[128,768]{1,0:T(8,128)(2,1)S(1)}, u32[]{:S(2)}, u32[]{:S(2)}) %collective-permute-start.33) | collective-permute-done | bytes 196640 | tf_op jit(solution)/shard_map/ppermute | solution.py:35
  223.2 10.0 %collective-permute-done.34 = bf16[128,768]{1,0:T(8,128)(2,1)S(1)} collective-permute-done((bf16[128,768]{1,0:T(8,128)(2,1)S(1)}, bf16[128,768]{1,0:T(8,128)(2,1)S(1)}, u32[]{:S(2)}, u32[]{:S(2)}) %collective-permute-start.34) | collective-permute-done | bytes 196640 | tf_op jit(solution)/shard_map/ppermute | solution.py:35
  251.9 7.8 %collective-permute-done.41.b_ref = bf16[512,768]{1,0:T(8,128)(2,1)S(1)} collective-permute-done((bf16[512,768]{1,0:T(8,128)(2,1)S(1)}, bf16[512,768]{1,0:T(8,128)(2,1)S(1)}, u32[]{:S(2)}, u32[]{:S(2)}) %collective-permute-start.41) | collective-permute-done | bytes 786464 | tf_op jit(solution)/shard_map/ppermute | solution.py:35
  265.7 32.3 %shard_map.216 = (f32[512,768]{1,0:T(8,128)}, bf16[512,768]{1,0:T(8,128)(2,1)}, bf16[2,3,384,512]{3,2,1,0:T(8,128)(2,1)}, bf16[2,3,384,512]{3,2,1,0:T(8,128)(2,1...) custom-call(s32[5]{0:T(128)} %copy-done.68, ...), custom_call_target="tpu_custom_call" | custom-call | flops 9663676 | bytes 36208 | tf_op jit(solution)/shard_map/pallas_call | solution.py:86
  323.5 10.2 %collective-permute-done.46 = bf16[128,768]{1,0:T(8,128)(2,1)S(1)} collective-permute-done((bf16[128,768]{1,0:T(8,128)(2,1)S(1)}, bf16[128,768]{1,0:T(8,128)(2,1)S(1)}, u32[]{:S(2)}, u32[]{:S(2)}) %collective-permute-start.46) | collective-permute-done | bytes 196640 | tf_op jit(solution)/shard_map/ppermute | solution.py:35
  348.8 12.9 %shard_map.221 = (bf16[512,192]{1,0:T(8,128)(2,1)}, bf16[768,192]{1,0:T(8,128)(2,1)}, bf16[512,384]{1,0:T(8,128)(2,1)}, bf16[512,384]{1,0:T(8,128)(2,1)}) custom-call(s32[5]{0:T(128)} %copy-done.68, f32[1,1024]{1,0:T(1,128)} %bitcast.94, bf16[512,192]{1,0:T(8,128)(2,1)} %copy-done.73, bf16[512,768]{1,0:T(8,128)(2,1)} %copy-done.86, ...), custom_call_target="tpu_custom_call" | custom-call | flops 1308622 | bytes 7180 | tf_op jit(solution)/shard_map/pallas_call | solution.py:86
  393.6 9.3 %collective-permute-done.57 = bf16[128,768]{1,0:T(8,128)(2,1)S(1)} collective-permute-done((bf16[128,768]{1,0:T(8,128)(2,1)S(1)}, bf16[128,768]{1,0:T(8,128)(2,1)S(1)}, u32[]{:S(2)}, u32[]{:S(2)}) %collective-permute-start.57) | collective-permute-done | bytes 196640 | tf_op jit(solution)/shard_map/ppermute | solution.py:35
  403.0 10.4 %collective-permute-done.55 = bf16[128,768]{1,0:T(8,128)(2,1)S(1)} collective-permute-done((bf16[128,768]{1,0:T(8,128)(2,1)S(1)}, bf16[128,768]{1,0:T(8,128)(2,1)S(1)}, u32[]{:S(2)}, u32[]{:S(2)}) %collective-permute-start.55) | collective-permute-done | bytes 196640 | tf_op jit(solution)/shard_map/ppermute | solution.py:35
  413.5 6.5 collective-permute-done.59.refs_3_
  434.3 25.0 %shard_map.224 = (f32[512,768]{1,0:T(8,128)}, bf16[512,768]{1,0:T(8,128)(2,1)}, bf16[1,3,384,512]{3,2,1,0:T(8,128)(2,1)}, bf16[1,3,384,512]{3,2,1,0:T(8,128)(2,1...) custom-call(s32[5]{0:T(128)} %copy-done.68, ...), custom_call_target="tpu_custom_call" | custom-call | flops 9663676 | bytes 37781 | tf_op jit(solution)/shard_map/pallas_call | solution.py:86
  480.8 10.2 %collective-permute-done.70.got_ref = bf16[1,3,384,512]{3,2,1,0:T(8,128)(2,1)S(1)} collective-permute-done((bf16[1,3,384,512]{3,2,1,0:T(8,128)(2,1)S(1)}, bf16[1,3,384,512]{3,2,1,0:T(8,128)(2,1)S(1)}, u32[]{:S(2)}, u32[]{:S(2)}) %collective-permute-start.70) | collective-permute-done | bytes 1179680 | tf_op jit(solution)/shard_map/ppermute | solution.py:35
  500.6 10.1 %collective-permute-done.74 = bf16[128,768]{1,0:T(8,128)(2,1)S(1)} collective-permute-done((bf16[128,768]{1,0:T(8,128)(2,1)S(1)}, bf16[128,768]{1,0:T(8,128)(2,1)S(1)}, u32[]{:S(2)}, u32[]{:S(2)}) %collective-permute-start.74) | collective-permute-done | bytes 196640 | tf_op jit(solution)/shard_map/ppermute | solution.py:35
  529.3 12.8 %shard_map.230 = (bf16[512,192]{1,0:T(8,128)(2,1)}, bf16[768,192]{1,0:T(8,128)(2,1)}, bf16[512,384]{1,0:T(8,128)(2,1)}, bf16[512,384]{1,0:T(8,128)(2,1)}) custom-call(s32[5]{0:T(128)} %copy-done.68, f32[1,1024]{1,0:T(1,128)} %bitcast.95, bf16[512,192]{1,0:T(8,128)(2,1)} %copy-done.74, bf16[512,768]{1,0:T(8,128)(2,1)} %copy-done.83, ...), custom_call_target="tpu_custom_call" | custom-call | flops 1308622 | bytes 4624 | tf_op jit(solution)/shard_map/pallas_call | solution.py:86
  542.1 21.3 %collective-permute-done.79.got_ref = bf16[192,2432]{1,0:T(8,128)(2,1)} collective-permute-done((bf16[192,2432]{1,0:T(8,128)(2,1)S(1)}, bf16[192,2432]{1,0:T(8,128)(2,1)}, u32[]{:S(2)}, u32[]{:S(2)}) %collective-permute-start.79) | collective-permute-done | bytes 933920 | tf_op jit(solution)/shard_map/ppermute | solution.py:35
  624.3 6.8 collective-permute-done.95.got_ref
  644.2 11.9 %collective-permute-done.111 = bf16[4,192]{1,0:T(4,128)(2,1)S(1)} collective-permute-done((bf16[4,192]{1,0:T(4,128)(2,1)S(1)}, bf16[4,192]{1,0:T(4,128)(2,1)S(1)}, u32[]{:S(2)}, u32[]{:S(2)}) %collective-permute-start.111) | collective-permute-done | bytes 1568 | tf_op jit(solution)/shard_map/ppermute | solution.py:35
  658.2 7.5 %collective-permute-done.107 = bf16[192,896]{1,0:T(8,128)(2,1)S(1)} collective-permute-done((bf16[192,896]{1,0:T(8,128)(2,1)S(1)}, bf16[192,896]{1,0:T(8,128)(2,1)S(1)}, u32[]{:S(2)}, u32[]{:S(2)}) %collective-permute-start.107) | collective-permute-done | bytes 344096 | tf_op jit(solution)/shard_map/ppermute | solution.py:35
  (651 shorter events, 408.6 us)
Async XLA Ops:
  26.6 44.4 %collective-permute-start.6 = (bf16[8,3,192,512]{3,2,1,0:T(8,128)(2,1)}, bf16[8,3,192,512]{3,2,1,0:T(8,128)(2,1)}, u32[]{:S(2)}, u32[]{:S(2)}) collective-permute-start(bf16[8,3,192,512]{3,2,1,0:T(8,128)(2,1)} %get-tuple-element.371.refs_0_.refs_1_), channel_id=1, source_target_pairs={{0,8},{8,0},{16,24},{24,16},{1,9},{9,1},{17,25},{25,17},{2,10},{10... | collective-permute-start | bytes 14155784 | tf_op jit(solution)/shard_map/ppermute | solution.py:35
  34.0 37.0 %collective-permute-start.7 = (bf16[8,3,64,512]{3,2,1,0:T(8,128)(2,1)}, bf16[8,3,64,512]{3,2,1,0:T(8,128)(2,1)}, u32[]{:S(2)}, u32[]{:S(2)}) collective-permute-start(bf16[8,3,64,512]{3,2,1,0:T(8,128)(2,1)} %copy-done.112), channel_id=1, source_target_pairs={{0,16},{8,24},{16,0},{24,8},{1,17},{9,25},{17,1},{25,9},{2,18},{10... | collective-permute-start | bytes 4718600 | tf_op jit(solution)/shard_map/ppermute | solution.py:35
  71.0 36.2 %collective-permute-start.15 = (bf16[8,3,64,512]{3,2,1,0:T(8,128)(2,1)}, bf16[8,3,64,512]{3,2,1,0:T(8,128)(2,1)}, u32[]{:S(2)}, u32[]{:S(2)}) collective-permute-start(bf16[8,3,64,512]{3,2,1,0:T(8,128)(2,1)} %get-tuple-element.364), channel_id=1, source_target_pairs={{0,16},{8,24},{16,0},{24,8},{1,17},{9,25},{17,1},{25,9},{2,18},{10... | collective-permute-start | bytes 4718600 | tf_op jit(solution)/shard_map/ppermute | solution.py:35
  71.3 35.9 %collective-permute-start.16 = (bf16[8,3,64,512]{3,2,1,0:T(8,128)(2,1)}, bf16[8,3,64,512]{3,2,1,0:T(8,128)(2,1)}, u32[]{:S(2)}, u32[]{:S(2)}) collective-permute-start(bf16[8,3,64,512]{3,2,1,0:T(8,128)(2,1)} %collective-permute-done.7.refs_2_.refs_3_), channel_id=1, source_target_pairs={{0,8},{8,0},{16,24},{24,16},{1,9},{9,1},{17,25},{25,17},{2,10},{10... | collective-permute-start | bytes 4718600 | tf_op jit(solution)/shard_map/ppermute | solution.py:35
  71.3 37.2 %collective-permute-start.14 = (bf16[8,3,64,512]{3,2,1,0:T(8,128)(2,1)}, bf16[8,3,64,512]{3,2,1,0:T(8,128)(2,1)}, u32[]{:S(2)}, u32[]{:S(2)}) collective-permute-start(bf16[8,3,64,512]{3,2,1,0:T(8,128)(2,1)} %collective-permute-done.7.refs_2_.refs_3_), channel_id=1, source_target_pairs={{0,4},{4,0},{1,5},{5,1},{2,6},{6,2},{3,7},{7,3},{8,12},{12,8},{9,1... | collective-permute-start | bytes 4718600 | tf_op jit(solution)/shard_map/ppermute | solution.py:35
  108.9 36.3 %collective-permute-start.20 = (bf16[192,2560]{1,0:T(8,128)(2,1)S(1)}, bf16[192,2560]{1,0:T(8,128)(2,1)S(1)}, u32[]{:S(2)}, u32[]{:S(2)}) collective-permute-start(bf16[192,2560]{1,0:T(8,128)(2,1)S(1)} %concatenate.39.refs_4_.refs_2_.refs_0_.refs_8_), channel_id=1, source_target_pairs={{0,16},{8,24},{16,0},{24,8},{1,17},{9,25},{17,1},{25,9},{2,18},{10... | collective-permute-start | bytes 2949128 | tf_op jit(solution)/shard_map/ppermute | solution.py:35
  110.6 34.6 %collective-permute-start.19 = (bf16[192,1536]{1,0:T(8,128)(2,1)S(1)}, bf16[192,1536]{1,0:T(8,128)(2,1)S(1)}, u32[]{:S(2)}, u32[]{:S(2)}) collective-permute-start(bf16[192,1536]{1,0:T(8,128)(2,1)S(1)} %pad_maximum_fusion.4.refs_0_.refs_4_.refs_8_), channel_id=1, source_target_pairs={{0,16},{8,24},{16,0},{24,8},{1,17},{9,25},{17,1},{25,9},{2,18},{10... | collective-permute-start | bytes 1769480 | tf_op jit(solution)/shard_map/ppermute | solution.py:35
  145.2 103.2 %collective-permute-start.39 = (bf16[8,3,192,512]{3,2,1,0:T(8,128)(2,1)}, bf16[8,3,192,512]{3,2,1,0:T(8,128)(2,1)}, u32[]{:S(2)}, u32[]{:S(2)}) collective-permute-start(bf16[8,3,192,512]{3,2,1,0:T(8,128)(2,1)} %get-tuple-element.408.refs_0_), channel_id=1, source_target_pairs={{0,16},{8,24},{16,0},{24,8},{1,17},{9,25},{17,1},{25,9},{2,18},{10... | collective-permute-start | bytes 14155784 | tf_op jit(solution)/shard_map/ppermute | solution.py:35
  298.0 63.6 %collective-permute-start.51 = (bf16[2,3,384,512]{3,2,1,0:T(8,128)(2,1)}, bf16[2,3,384,512]{3,2,1,0:T(8,128)(2,1)}, u32[]{:S(2)}, u32[]{:S(2)}) collective-permute-start(bf16[2,3,384,512]{3,2,1,0:T(8,128)(2,1)} %get-tuple-element.435), channel_id=1, source_target_pairs={{0,16},{8,24},{16,0},{24,8},{1,17},{9,25},{17,1},{25,9},{2,18},{10... | collective-permute-start | bytes 7077896 | tf_op jit(solution)/shard_map/ppermute | solution.py:35
  367.0 61.2 %collective-permute-start.60 = (bf16[2,3,384,512]{3,2,1,0:T(8,128)(2,1)S(1)}, bf16[2,3,384,512]{3,2,1,0:T(8,128)(2,1)S(1)}, u32[]{:S(2)}, u32[]{:S(2)}) collective-permute-start(bf16[2,3,384,512]{3,2,1,0:T(8,128)(2,1)S(1)} %add_convert_fusion.part_ref), channel_id=1, source_target_pairs={{0,4},{4,0},{1,5},{5,1},{2,6},{6,2},{3,7},{7,3},{8,12},{12,8},{9,1... | collective-permute-start | bytes 7077896 | tf_op jit(solution)/shard_map/ppermute | solution.py:35
  390.3 37.9 %collective-permute-start.61 = (bf16[1,3,384,512]{3,2,1,0:T(8,128)(2,1)S(1)}, bf16[1,3,384,512]{3,2,1,0:T(8,128)(2,1)S(1)}, u32[]{:S(2)}, u32[]{:S(2)}) collective-permute-start(bf16[1,3,384,512]{3,2,1,0:T(8,128)(2,1)S(1)} %copy-done.137), channel_id=1, source_target_pairs={{0,16},{8,24},{16,0},{24,8},{1,17},{9,25},{17,1},{25,9},{2,18},{10... | collective-permute-start | bytes 3538952 | tf_op jit(solution)/shard_map/ppermute | solution.py:35
  393.1 35.0 %collective-permute-start.62 = (bf16[192,2432]{1,0:T(8,128)(2,1)S(1)}, bf16[192,2432]{1,0:T(8,128)(2,1)S(1)}, u32[]{:S(2)}, u32[]{:S(2)}) collective-permute-start(bf16[192,2432]{1,0:T(8,128)(2,1)S(1)} %pad_maximum_fusion.1), channel_id=1, source_target_pairs={{0,8},{8,0},{16,24},{24,16},{1,9},{9,1},{17,25},{25,17},{2,10},{10... | collective-permute-start | bytes 2801672 | tf_op jit(solution)/shard_map/ppermute | solution.py:35
  393.1 35.0 %collective-permute-start.63 = (bf16[192,2432]{1,0:T(8,128)(2,1)S(1)}, bf16[192,2432]{1,0:T(8,128)(2,1)S(1)}, u32[]{:S(2)}, u32[]{:S(2)}) collective-permute-start(bf16[192,2432]{1,0:T(8,128)(2,1)S(1)} %pad_maximum_fusion.3), channel_id=1, source_target_pairs={{0,8},{8,0},{16,24},{24,16},{1,9},{9,1},{17,25},{25,17},{2,10},{10... | collective-permute-start | bytes 2801672 | tf_op jit(solution)/shard_map/ppermute | solution.py:35
  425.7 33.6 %collective-permute-start.65 = (bf16[1,3,384,512]{3,2,1,0:T(8,128)(2,1)S(1)}, bf16[1,3,384,512]{3,2,1,0:T(8,128)(2,1)S(1)}, u32[]{:S(2)}, u32[]{:S(2)}) collective-permute-start(bf16[1,3,384,512]{3,2,1,0:T(8,128)(2,1)S(1)} %add_convert_fusion.6.part_ref), channel_id=1, source_target_pairs={{0,4},{4,0},{1,5},{5,1},{2,6},{6,2},{3,7},{7,3},{8,12},{12,8},{9,1... | collective-permute-start | bytes 3538952 | tf_op jit(solution)/shard_map/ppermute | solution.py:35
  429.6 30.8 %collective-permute-start.66 = (bf16[192,2432]{1,0:T(8,128)(2,1)}, bf16[192,2432]{1,0:T(8,128)(2,1)}, u32[]{:S(2)}, u32[]{:S(2)}) collective-permute-start(bf16[192,2432]{1,0:T(8,128)(2,1)} %add_convert_fusion.8), channel_id=1, source_target_pairs={{0,16},{8,24},{16,0},{24,8},{1,17},{9,25},{17,1},{25,9},{2,18},{10... | collective-permute-start | bytes 2801672 | tf_op jit(solution)/shard_map/ppermute | solution.py:35
  462.7 28.3 %collective-permute-start.70 = (bf16[1,3,384,512]{3,2,1,0:T(8,128)(2,1)S(1)}, bf16[1,3,384,512]{3,2,1,0:T(8,128)(2,1)S(1)}, u32[]{:S(2)}, u32[]{:S(2)}) collective-permute-start(bf16[1,3,384,512]{3,2,1,0:T(8,128)(2,1)S(1)} %add_convert_fusion.5.part_ref), channel_id=1, source_target_pairs={{0,4},{4,0},{1,5},{5,1},{2,6},{6,2},{3,7},{7,3},{8,12},{12,8},{9,1... | collective-permute-start | bytes 3538952 | tf_op jit(solution)/shard_map/ppermute | solution.py:35
  466.7 28.3 %collective-permute-start.71 = (bf16[1,3,384,512]{3,2,1,0:T(8,128)(2,1)S(1)}, bf16[1,3,384,512]{3,2,1,0:T(8,128)(2,1)S(1)}, u32[]{:S(2)}, u32[]{:S(2)}) collective-permute-start(bf16[1,3,384,512]{3,2,1,0:T(8,128)(2,1)S(1)} %copy-done.140), channel_id=1, source_target_pairs={{0,16},{8,24},{16,0},{24,8},{1,17},{9,25},{17,1},{25,9},{2,18},{10... | collective-permute-start | bytes 3538952 | tf_op jit(solution)/shard_map/ppermute | solution.py:35
  495.0 28.2 %collective-permute-start.78 = (bf16[1,3,384,512]{3,2,1,0:T(8,128)(2,1)S(1)}, bf16[1,3,384,512]{3,2,1,0:T(8,128)(2,1)S(1)}, u32[]{:S(2)}, u32[]{:S(2)}) collective-permute-start(bf16[1,3,384,512]{3,2,1,0:T(8,128)(2,1)S(1)} %copy-done.139), channel_id=1, source_target_pairs={{0,16},{8,24},{16,0},{24,8},{1,17},{9,25},{17,1},{25,9},{2,18},{10... | collective-permute-start | bytes 3538952 | tf_op jit(solution)/shard_map/ppermute | solution.py:35
  515.4 48.0 %collective-permute-start.80 = (bf16[1,3,384,512]{3,2,1,0:T(8,128)(2,1)S(1)}, bf16[1,3,384,512]{3,2,1,0:T(8,128)(2,1)S(1)}, u32[]{:S(2)}, u32[]{:S(2)}) collective-permute-start(bf16[1,3,384,512]{3,2,1,0:T(8,128)(2,1)S(1)} %add_convert_fusion.4.part_ref), channel_id=1, source_target_pairs={{0,4},{4,0},{1,5},{5,1},{2,6},{6,2},{3,7},{7,3},{8,12},{12,8},{9,1... | collective-permute-start | bytes 3538952 | tf_op jit(solution)/shard_map/ppermute | solution.py:35
  523.2 40.2 %collective-permute-start.81 = (bf16[1,3,384,512]{3,2,1,0:T(8,128)(2,1)}, bf16[1,3,384,512]{3,2,1,0:T(8,128)(2,1)}, u32[]{:S(2)}, u32[]{:S(2)}) collective-permute-start(bf16[1,3,384,512]{3,2,1,0:T(8,128)(2,1)} %get-tuple-element.535), channel_id=1, source_target_pairs={{0,16},{8,24},{16,0},{24,8},{1,17},{9,25},{17,1},{25,9},{2,18},{10... | collective-permute-start | bytes 3538952 | tf_op jit(solution)/shard_map/ppermute | solution.py:35
  526.1 37.2 %collective-permute-start.79 = (bf16[192,2432]{1,0:T(8,128)(2,1)S(1)}, bf16[192,2432]{1,0:T(8,128)(2,1)}, u32[]{:S(2)}, u32[]{:S(2)}) collective-permute-start(bf16[192,2432]{1,0:T(8,128)(2,1)S(1)} %add_convert_fusion.7.part_ref), channel_id=1, source_target_pairs={{0,4},{4,0},{1,5},{5,1},{2,6},{6,2},{3,7},{7,3},{8,12},{12,8},{9,1... | collective-permute-start | bytes 2801672 | tf_op jit(solution)/shard_map/ppermute | solution.py:35
  602.3 28.8 %collective-permute-start.95 = (bf16[1,3,384,512]{3,2,1,0:T(8,128)(2,1)S(1)}, bf16[1,3,384,512]{3,2,1,0:T(8,128)(2,1)S(1)}, u32[]{:S(2)}, u32[]{:S(2)}) collective-permute-start(bf16[1,3,384,512]{3,2,1,0:T(8,128)(2,1)S(1)} %add_convert_fusion.2.part_ref), channel_id=1, source_target_pairs={{0,4},{4,0},{1,5},{5,1},{2,6},{6,2},{3,7},{7,3},{8,12},{12,8},{9,1... | collective-permute-start | bytes 3538952 | tf_op jit(solution)/shard_map/ppermute | solution.py:35
  619.0 48.5 %collective-permute-start.114 = (bf16[1,3,384,512]{3,2,1,0:T(8,128)(2,1)S(1)}, bf16[1,3,384,512]{3,2,1,0:T(8,128)(2,1)S(1)}, u32[]{:S(2)}, u32[]{:S(2)}) collective-permute-start(bf16[1,3,384,512]{3,2,1,0:T(8,128)(2,1)S(1)} %add_convert_fusion.1.part_ref), channel_id=1, source_target_pairs={{0,4},{4,0},{1,5},{5,1},{2,6},{6,2},{3,7},{7,3},{8,12},{12,8},{9,1... | collective-permute-start | bytes 3538952 | tf_op jit(solution)/shard_map/ppermute | solution.py:35
  624.3 33.8 %collective-permute-start.106 = (bf16[1,3,192,512]{3,2,1,0:T(8,128)(2,1)S(1)}, bf16[1,3,192,512]{3,2,1,0:T(8,128)(2,1)S(1)}, u32[]{:S(2)}, u32[]{:S(2)}) collective-permute-start(bf16[1,3,192,512]{3,2,1,0:T(8,128)(2,1)S(1)} %get-tuple-element.616), channel_id=1, source_target_pairs={{0,8},{8,0},{16,24},{24,16},{1,9},{9,1},{17,25},{25,17},{2,10},{10... | collective-permute-start | bytes 1769480 | tf_op jit(solution)/shard_map/ppermute | solution.py:35
  (238 other events, 4384.2 us)

commit v4 on v3

--- a/solution.py
+++ b/solution.py
@@ -70,7 +70,7 @@
 
 
 def call(
-    kernel, scal, grid, ins, outs, scratch=(), flops=0, exps=0, alias=None, limit=32, light=LIGHT
+    kernel, scal, grid, ins, outs, scratch=(), flops=0, exps=0, alias=None, limit=20, light=LIGHT
 ):
     def spec(item):
         shape, block, index = item[0].shape, item[1], item[2]
@@ -414,16 +414,13 @@
 
 def pack_kernel(scal, in_ref, out_ref, own_ref, first_ref, last_ref):
     third = first_ref.shape[2]
-    own_ref[0, :2] = in_ref[0, 0]
+    own_ref[0, :2] = pltpu.einshape("dkf->kdf", in_ref[0, 0])
     own_ref[0, 2] = out_ref[0, 0]
     first_ref[0] = own_ref[0, :, pl.ds(pl.multiple_of(scal[4] * third, third), third), :]
     last_ref[0] = own_ref[0, :, 2 * third :, :]
 
 
 def expert_weights(scal, refs):
-    if len(refs) == 4:
-        return [joined(refs, 0, part) for part in range(3)]
-
     def far(refs, part):
         straight, around, last = [ref[0, part] for ref in refs]
         low = jnp.where(scal[4] == 0, straight, around)
@@ -567,34 +564,38 @@
                 sin_ref[0, rows, :] = total[:, lanes : lanes + 128]
         sout_ref[0] = total[:, 2 * hid : 3 * hid]
 
-CHUNKS, PARTS = 2, ((1, 1, 1, 1), (2, 1, 1))
+CHUNKS, PARTS = 2, ((2, 2), (1, 1, 2))
 SLOTS = {
     "start": ["pack 0", ("experts", 0)],
     ("attend", 0): ["slots"],
     ("attend half", 0): [("experts", 0), "pack 1"],
     ("attend sum", 0): ["pack 2", ("experts", 1)],
-    ("mixed", 0): [("experts", 0), "pack 1", "pack 2"],
+    ("mixed", 0): [("experts", 0), "pack 1"],
     ("experts", 0): ["pack 1", "pack 2", ("experts", 1)],
-    ("attend sum", 1): [("experts", 1)],
+    ("branch sum", 0): ["pack 2", ("experts", 1)],
+    ("attend", 1): [("experts", 1)],
     ("mixed", 1): [("experts", 1)],
     (1, "experts"): [(1, 0)],
-    (1, "attention"): [(1, 0), (1, 1)],
+    (1, "ffn half"): [(1, 1)],
+    (1, "ffn sum"): [(1, 0), (1, 2)],
+    (1, "attention"): [(1, 1)],
     (1, "project"): [(1, "packs")],
-    (1, "attention half"): [(1, 1), (1, 2)],
-    (1, "input"): [(1, 0), (1, 2), (1, "packs")],
-    (0, "experts"): [(1, 1), (1, "packs"), (0, 0)],
-    (0, "ffn half"): [(1, 0), (1, 2), (0, 0), (0, 1)],
-    (0, "ffn sum"): [(1, 1), (0, 1), (0, 2), (0, "shared")],
-    (0, "attention"): [(1, "packs"), (0, 0), (0, 2), (0, 3)],
+    (1, "attention half"): [(1, 0), (1, 2)],
+    (1, "attention sum"): [(1, "packs")],
+    (1, "input"): [(1, 0), (1, 1)],
+    (0, "experts"): [(1, 2), (1, "packs"), (0, 0)],
+    (0, "ffn half"): [(1, 1), "result"],
+    (0, "ffn sum"): [(1, 2), "result", (0, 0), (0, 1), (0, "shared")],
+    (0, "attention"): [(1, "packs")],
     (0, "project"): [(0, "attention"), "result"],
-    (0, "attention half"): [(1, 2), (0, 1), (0, 3), (0, "shared")],
-    (0, "attention sum"): [(0, 0), (0, 2), (0, "shared"), (0, "attention"), "result"],
-    (0, "input"): [(0, 1), (0, "attention")],
+    (0, "attention half"): [(0, 0), (0, 1), (0, "shared")],
+    (0, "attention sum"): [(0, 0)],
+    (0, "input"): [(0, 1), (0, "shared"), (0, "attention")],
 }
 TAIL = (
-    ["gains", (0, "shared"), (0, "attention"), (0, 3), (0, 2)],
-    ["gains", "result"],
-    ["gains", (0, 3)],
+    ["gains", (0, 1), (0, "shared"), (0, "attention")],
+    ["gains", (0, "attention")],
+    ["gains"],
 )
 
 
@@ -620,7 +621,7 @@
             [whole(part), whole(got)] + [(self.held[at], "any", None) for at in before],
             [slot(self.shapes[at]) for at in used],
             alias={3 + n: used.index(at) for n, at in enumerate(before)},
-            limit=16,
+            limit=10,
         )
         for at, result in zip(used, results):
             self.held[at] = result
@@ -650,7 +651,7 @@
             [lead(i) for i in ins] + held,
             [lead(x) for x in extra] + [slot(s) for s in self.shapes],
             alias={base + at: len(extra) + at for at in range(len(held))},
-            limit=16,
+            limit=10,
         )
         self.held = (gin, gout)
         return rest
@@ -680,22 +681,16 @@
 
 def weight_flow(place, at, own, first, last):
     own, first, last = yield [own, first, last]
+    if at > 0:
+        own, first, last = yield [own, first, last]
     own, sib, straight, last = yield [own, swap(own, "fsdp", 1), swap(first, "fsdp", 2), last]
-    around, last = swap(straight, "ctx", 1), swap(last, "fsdp", 2)
-    held = yield [straight, around, last, swap(straight, "fsdp", 1)]
-    straight, around, last, cross = held
+    last = swap(last, "fsdp", 2)
+    if at > 0:
+        (straight,) = yield [straight]
+    around, cross = swap(straight, "ctx", 1), swap(straight, "fsdp", 1)
+    straight, around, last, cross = yield [straight, around, last, cross]
     place[at] = [own, sib, straight, around, last]
     place[at] += [cross, swap(around, "fsdp", 1), swap(last, "fsdp", 1)]
-    yield []
-
-
-def plain_flow(place, at, own, first, last):
-    (own,) = yield [own]
-    (own,) = yield [own]
-    own, far = yield [own, swap(own, "fsdp", 2)]
-    near = swap(own, "fsdp", 1)
-    near, far, cross = yield [near, far, swap(far, "fsdp", 1)]
-    place[at] = [own, near, far, cross]
     yield []
 
 
@@ -756,7 +751,6 @@
     def pack_shared(at):
         return [shared_in[at].reshape(block, 2 * hid), shared_out[at].T]
 
-    ein = lax.optimization_barrier(expert_in.transpose(0, 1, 3, 2, 4))
     eout = expert_out.transpose(0, 1, 3, 2)
 
     def pack_experts(at):
@@ -769,11 +763,11 @@
             scal,
             (experts,),
             [
-                (ein, (1, 1) + ein.shape[2:], lambda e, s: (at, e, 0, 0, 0)),
+                (expert_in, (1, 1) + expert_in.shape[2:], lambda e, s: (at, e, 0, 0, 0)),
                 (eout, (1, 1) + eout.shape[2:], lambda e, s: (at, e, 0, 0)),
             ],
             [lead(whole_pack), lead(part), lead(part)],
-            limit=16,
+            limit=10,
         )
 
     ancestors = ancestry(parents[0])
@@ -832,8 +826,7 @@
     small, routed = {}, {}
     open_flow("pack 0", block_flow(small, 0, pack_attention(0)))
     for at in range(layers):
-        kind = weight_flow if at == 0 else plain_flow
-        open_flow(("experts", at), kind(routed, at, *pack_experts(at)))
+        open_flow(("experts", at), weight_flow(routed, at, *pack_experts(at)))
     open_flow("pack 1", block_flow(small, 1, jnp.concatenate(pack_shared(0), axis=1)))
     rest = [pack_attention(at) for at in range(1, layers)]
     rest = [v for pack in rest for v in (pack, jnp.zeros((block, 128), BF16))]
@@ -880,7 +873,7 @@
             [whole(row_f32), whole(row_bf16)] + kept,
             scratch=slot_scratch * 2,
             flops=5 * expert_flops,
-            limit=48,
+            limit=32,
         )
 
     def join(own, sib, shared_part):
@@ -941,7 +934,7 @@
             [tiled(sds((rows, heads_width), BF16))] + halves,
             flops=4 * rows * tree_len * heads_width + matrix * heads_width,
             exps=rows * tree_len * heads_width // HEAD_DIM,
-            limit=40,
+            limit=24,
         )
         part = slot(("attend", at), *part)
         arrivals = tp_sum(part, functools.partial(slot, ("attend half", at)))
@@ -1017,7 +1010,7 @@
             scratch=slot_scratch * (3 if fresh else 1),
             flops=8 * expert_flops,
             exps=per_core * capacity * hid,
-            limit=56,
+            limit=44,
         )
         for chunk in range(len(sizes)):
             near, far = grads[2 * chunk : 2 * chunk + 2]
@@ -1056,7 +1049,7 @@
             ],
             flops=10 * rows * tree_len * heads_width + 2 * matrix * heads_width,
             exps=rows * tree_len * heads_width // HEAD_DIM,
-            limit=56,
+            limit=34,
         )
         dq, *dkv = slot((at, "attention"), dq, *dkv)
         if ctx == 2:

time: 703 us -> 686 us (0.976)
  starting transfers between devices: 87.1 us -> 107 us
  Pallas kernels: 191 us -> 172 us
  local copies, waits for them, and re-layouts: 50.5 us -> 40.4 us
    ppermute x117 -> x115, starting transfers between devices: 87.1 us -> 107 us  [swap(): return lax.ppermute(values, axis, [(k, k ^ mask) for k in range(count)])]
    pallas_call x46 -> x42, Pallas kernels: 191 us -> 172 us  [call(): pl.pallas_call(kernel, out_shape=[o[0] for o in outs], grid_spec=pltpu.Pr...]
    unnamed x297 -> x202, local copies, waits for them, and re-layouts: 36.7 us -> 24.7 us
    convert_element_type x50 -> x47, other arithmetic: 14.5 us -> 8.84 us  [add(): return (a.astype(F32) + b.astype(F32)).astype(BF16)]
    ppermute x117 -> x115, waiting for transfers between devices: 348 us -> 345 us  [swap(): return lax.ppermute(values, axis, [(k, k ^ mask) for k in range(count)])]
  transfers between devices with their start and end apart: 117 -> 115, of which waited for: 67 -> 69; matrix products, arithmetic and copies ran while one was open for 5% -> 3% of each run, Pallas kernels for 23% -> 19%
where the time goes in v4:
time: 686 us; the launch traced here: 678 us
  waiting for transfers between devices  345 us (50%)
  Pallas kernels  172 us (25%)
  starting transfers between devices  107 us (16%)
  local copies, waits for them, and re-layouts  40.4 us (6%)
  other arithmetic  9.92 us (1%)
    ppermute x115, waiting for transfers between devices, swap(): return lax.ppermute(values, axis, [(k, k ^ mask) for k in range(count)])  345 us
    pallas_call x42, Pallas kernels, call(): pl.pallas_call(kernel, out_shape=[o[0] for o in outs], grid_spec=pltpu.Pr...  172 us
    ppermute x115, starting transfers between devices, swap(): return lax.ppermute(values, axis, [(k, k ^ mask) for k in range(count)])  107 us
    unnamed x202, local copies, waits for them, and re-layouts  24.7 us
  transfers between devices with their start and end apart: 115, of which 69 were waited for; matrix products, arithmetic and copies ran while one was open for 3% of the time, Pallas kernels for 19%

profile of v4, /device:TPU:0, one launch (start us, length us, event | category | flops | bytes accessed | tf_op | source)
XLA Modules:
  0.0 678.3 jit_solution(6156569191872730458)
XLA Ops:
  34.1 9.2 %collective-permute-done.3.refs_1_ = bf16[512,384]{1,0:T(8,128)(2,1)S(1)} collective-permute-done((bf16[512,384]{1,0:T(8,128)(2,1)S(1)}, bf16[512,384]{1,0:T(8,128)(2,1)S(1)}, u32[]{:S(2)}, u32[]{:S(2)}) %collective-permute-start.3) | collective-permute-done | bytes 393248 | tf_op jit(solution)/shard_map/ppermute | solution.py:35
  70.7 8.2 %collective-permute-done.8 = bf16[128,768]{1,0:T(8,128)(2,1)S(1)} collective-permute-done((bf16[128,768]{1,0:T(8,128)(2,1)S(1)}, bf16[128,768]{1,0:T(8,128)(2,1)S(1)}, u32[]{:S(2)}, u32[]{:S(2)}) %collective-permute-start.8) | collective-permute-done | bytes 196640 | tf_op jit(solution)/shard_map/ppermute | solution.py:35
  111.8 11.0 %shard_map.210 = (f32[512,768]{1,0:T(8,128)S(1)}, bf16[512,768]{1,0:T(8,128)(2,1)S(1)}, bf16[4,384,768]{2,1,0:T(8,128)(2,1)S(1)}, bf16[4,384,512]{2,1,0:T(8,128)(2,1)S(1)}, bf16[4,384,512]{2,1,0:T(8,128)(2,1)S(1)}) custom-call(s32[5]{0:T(128)S(1)} %stack.23.scal, bf16[512,768]{1,0:T(8,128)(2,1)S(1)} %copy-done.11, bf16[512,768]{1,0:T(8,128)(2,1)S(1)} %copy-done.56, ...), custom_call_target="tpu_custom_call" | custom-call | flops 6039797 | bytes 28344 | tf_op jit(solution)/shard_map/pallas_call | solution.py:86
  151.7 9.6 %collective-permute-done.24 = bf16[128,768]{1,0:T(8,128)(2,1)S(1)} collective-permute-done((bf16[128,768]{1,0:T(8,128)(2,1)S(1)}, bf16[128,768]{1,0:T(8,128)(2,1)S(1)}, u32[]{:S(2)}, u32[]{:S(2)}) %collective-permute-start.24) | collective-permute-done | bytes 196640 | tf_op jit(solution)/shard_map/ppermute | solution.py:35
  165.3 16.2 %collective-permute-done.29.refs_6_.refs_4_.refs_2_.refs_10_ = bf16[192,2560]{1,0:T(8,128)(2,1)S(1)} collective-permute-done((bf16[192,2560]{1,0:T(8,128)(2,1)S(1)}, bf16[192,2560]{1,0:T(8,128)(2,1)S(1)}, u32[]{:S(2)}, u32[]{:S(2)}) %collective-permute-start.29) | collective-permute-done | bytes 983072 | tf_op jit(solution)/shard_map/ppermute | solution.py:35
  188.2 10.6 %collective-permute-done.34.refs_1_ = bf16[512,384]{1,0:T(8,128)(2,1)S(1)} collective-permute-done((bf16[512,384]{1,0:T(8,128)(2,1)S(1)}, bf16[512,384]{1,0:T(8,128)(2,1)S(1)}, u32[]{:S(2)}, u32[]{:S(2)}) %collective-permute-start.34) | collective-permute-done | bytes 393248 | tf_op jit(solution)/shard_map/ppermute | solution.py:35
  219.2 8.8 %collective-permute-done.36 = bf16[128,768]{1,0:T(8,128)(2,1)S(1)} collective-permute-done((bf16[128,768]{1,0:T(8,128)(2,1)S(1)}, bf16[128,768]{1,0:T(8,128)(2,1)S(1)}, u32[]{:S(2)}, u32[]{:S(2)}) %collective-permute-start.36) | collective-permute-done | bytes 196640 | tf_op jit(solution)/shard_map/ppermute | solution.py:35
  250.1 29.7 %shard_map.216 = (f32[512,768]{1,0:T(8,128)}, bf16[512,768]{1,0:T(8,128)(2,1)}, bf16[1,3,384,512]{3,2,1,0:T(8,128)(2,1)S(1)}, bf16[1,3,384,512]{3,2,1,0:T(8,128)...) custom-call(s32[5]{0:T(128)S(1)} %stack.23.scal, ...), custom_call_target="tpu_custom_call" | custom-call | flops 9663676 | bytes 36208 | tf_op jit(solution)/shard_map/pallas_call | solution.py:86
  302.3 7.2 %collective-permute-done.51 = bf16[128,768]{1,0:T(8,128)(2,1)S(1)} collective-permute-done((bf16[128,768]{1,0:T(8,128)(2,1)S(1)}, bf16[128,768]{1,0:T(8,128)(2,1)S(1)}, u32[]{:S(2)}, u32[]{:S(2)}) %collective-permute-start.51) | collective-permute-done | bytes 196640 | tf_op jit(solution)/shard_map/ppermute | solution.py:35
  328.8 9.8 %shard_map.221 = (bf16[512,192]{1,0:T(8,128)(2,1)S(1)}, bf16[768,192]{1,0:T(8,128)(2,1)S(1)}, bf16[512,384]{1,0:T(8,128)(2,1)S(1)}, bf16[512,384]{1,0:T(8,128)(2,1)S(1)}) custom-call(s32[5]{0:T(128)S(1)} %stack.23.scal, f32[1,1024]{1,0:T(1,128)S(1)} %bitcast.89, bf16[512,192]{1,0:T(8,128)(2,1)S(1)} %get-tuple-element.405.q_ref, ...), custom_call_target="tpu_custom_call" | custom-call | flops 1308622 | bytes 7180 | tf_op jit(solution)/shard_map/pallas_call | solution.py:86
  348.1 8.1 %collective-permute-done.57.got_ref = bf16[512,384]{1,0:T(8,128)(2,1)S(1)} collective-permute-done((bf16[512,384]{1,0:T(8,128)(2,1)S(1)}, bf16[512,384]{1,0:T(8,128)(2,1)S(1)}, u32[]{:S(2)}, u32[]{:S(2)}) %collective-permute-start.57) | collective-permute-done | bytes 393248 | tf_op jit(solution)/shard_map/ppermute | solution.py:35
  367.5 14.0 %collective-permute-done.59.got_ref = bf16[1,3,384,512]{3,2,1,0:T(8,128)(2,1)S(1)} collective-permute-done((bf16[1,3,384,512]{3,2,1,0:T(8,128)(2,1)S(1)}, bf16[1,3,384,512]{3,2,1,0:T(8,128)(2,1)S(1)}, u32[]{:S(2)}, u32[]{:S(2)}) %collective-permute-start.59) | collective-permute-done | bytes 1179680 | tf_op jit(solution)/shard_map/ppermute | solution.py:35
  384.7 12.0 %collective-permute-done.60 = bf16[2,3,384,512]{3,2,1,0:T(8,128)(2,1)S(1)} collective-permute-done((bf16[2,3,384,512]{3,2,1,0:T(8,128)(2,1)S(1)}, bf16[2,3,384,512]{3,2,1,0:T(8,128)(2,1)S(1)}, u32[]{:S(2)}, u32[]{:S(2)}) %collective-permute-start.60) | collective-permute-done | bytes 2359328 | tf_op jit(solution)/shard_map/ppermute | solution.py:35
  425.4 21.8 %shard_map.225 = (f32[512,768]{1,0:T(8,128)S(1)}, bf16[512,768]{1,0:T(8,128)(2,1)S(1)}, bf16[2,3,384,512]{3,2,1,0:T(8,128)(2,1)}, bf16[2,3,384,512]{3,2,1,0:T(8,...) custom-call(s32[5]{0:T(128)S(1)} %stack.23.scal, ...), custom_call_target="tpu_custom_call" | custom-call | flops 9663676 | bytes 37781 | tf_op jit(solution)/shard_map/pallas_call | solution.py:86
  447.2 8.4 %collective-permute-done.71.got_ref = bf16[2,3,384,512]{3,2,1,0:T(8,128)(2,1)} collective-permute-done((bf16[2,3,384,512]{3,2,1,0:T(8,128)(2,1)S(1)}, bf16[2,3,384,512]{3,2,1,0:T(8,128)(2,1)}, u32[]{:S(2)}, u32[]{:S(2)}) %collective-permute-start.71) | collective-permute-done | bytes 2359328 | tf_op jit(solution)/shard_map/ppermute | solution.py:35
  475.6 7.3 %collective-permute-done.77 = bf16[128,768]{1,0:T(8,128)(2,1)S(1)} collective-permute-done((bf16[128,768]{1,0:T(8,128)(2,1)S(1)}, bf16[128,768]{1,0:T(8,128)(2,1)S(1)}, u32[]{:S(2)}, u32[]{:S(2)}) %collective-permute-start.77) | collective-permute-done | bytes 196640 | tf_op jit(solution)/shard_map/ppermute | solution.py:35
  483.1 7.6 %collective-permute-start.79 = (bf16[128,768]{1,0:T(8,128)(2,1)S(1)}, bf16[128,768]{1,0:T(8,128)(2,1)S(1)}, u32[]{:S(2)}, u32[]{:S(2)}) collective-permute-start(bf16[128,768]{1,0:T(8,128)(2,1)S(1)} %add_convert_fusion.24.refs_0_), channel_id=1, source_target_pairs={{0,1},{1,0},{2,3},{3,2},{4,5},{5,4},{6,7},{7,6},{8,9},{9,8},{10,11... | collective-permute-start | bytes 589832 | tf_op jit(solution)/shard_map/ppermute | solution.py:35
  500.5 9.0 %collective-permute-done.83 = bf16[2,3,384,512]{3,2,1,0:T(8,128)(2,1)S(1)} collective-permute-done((bf16[2,3,384,512]{3,2,1,0:T(8,128)(2,1)}, bf16[2,3,384,512]{3,2,1,0:T(8,128)(2,1)S(1)}, u32[]{:S(2)}, u32[]{:S(2)}) %collective-permute-start.83) | collective-permute-done | bytes 2359328 | tf_op jit(solution)/shard_map/ppermute | solution.py:35
  515.9 9.7 %shard_map.233 = (bf16[512,192]{1,0:T(8,128)(2,1)S(1)}, bf16[768,192]{1,0:T(8,128)(2,1)S(1)}, bf16[512,384]{1,0:T(8,128)(2,1)S(1)}, bf16[512,384]{1,0:T(8,128)(2,1)S(1)}) custom-call(s32[5]{0:T(128)S(1)} %stack.23.scal, f32[1,1024]{1,0:T(1,128)S(1)} %bitcast.90, bf16[512,192]{1,0:T(8,128)(2,1)S(1)} %copy-done.44, ...), custom_call_target="tpu_custom_call" | custom-call | flops 1308622 | bytes 4624 | tf_op jit(solution)/shard_map/pallas_call | solution.py:86
  547.2 29.6 %collective-permute-done.85.got_ref = bf16[512,384]{1,0:T(8,128)(2,1)S(1)} collective-permute-done((bf16[512,384]{1,0:T(8,128)(2,1)S(1)}, bf16[512,384]{1,0:T(8,128)(2,1)S(1)}, u32[]{:S(2)}, u32[]{:S(2)}) %collective-permute-start.85) | collective-permute-done | bytes 393248 | tf_op jit(solution)/shard_map/ppermute | solution.py:35
  597.2 11.5 %collective-permute-done.99 = bf16[128,768]{1,0:T(8,128)(2,1)S(1)} collective-permute-done((bf16[128,768]{1,0:T(8,128)(2,1)S(1)}, bf16[128,768]{1,0:T(8,128)(2,1)S(1)}, u32[]{:S(2)}, u32[]{:S(2)}) %collective-permute-start.99) | collective-permute-done | bytes 196640 | tf_op jit(solution)/shard_map/ppermute | solution.py:35
  629.2 10.3 %collective-permute-done.109 = bf16[4,192]{1,0:T(4,128)(2,1)S(1)} collective-permute-done((bf16[4,192]{1,0:T(4,128)(2,1)S(1)}, bf16[4,192]{1,0:T(4,128)(2,1)S(1)}, u32[]{:S(2)}, u32[]{:S(2)}) %collective-permute-start.109) | collective-permute-done | bytes 1568 | tf_op jit(solution)/shard_map/ppermute | solution.py:35
  640.0 8.0 %collective-permute-done.103.got_ref = bf16[2,3,384,512]{3,2,1,0:T(8,128)(2,1)S(1)} collective-permute-done((bf16[2,3,384,512]{3,2,1,0:T(8,128)(2,1)S(1)}, bf16[2,3,384,512]{3,2,1,0:T(8,128)(2,1)S(1)}, u32[]{:S(2)}, u32[]{:S(2)}) %collective-permute-start.103) | collective-permute-done | bytes 2359328 | tf_op jit(solution)/shard_map/ppermute | solution.py:35
  656.7 10.7 %collective-permute-done.113.got_ref = bf16[192,1536]{1,0:T(8,128)(2,1)S(1)} collective-permute-done((bf16[192,1536]{1,0:T(8,128)(2,1)S(1)}, bf16[192,1536]{1,0:T(8,128)(2,1)S(1)}, u32[]{:S(2)}, u32[]{:S(2)}) %collective-permute-start.113) | collective-permute-done | bytes 589856 | tf_op jit(solution)/shard_map/ppermute | solution.py:35
  (545 shorter events, 387.5 us)
Async XLA Ops:
  20.2 44.2 %collective-permute-start.6 = (bf16[8,3,192,512]{3,2,1,0:T(8,128)(2,1)}, bf16[8,3,192,512]{3,2,1,0:T(8,128)(2,1)}, u32[]{:S(2)}, u32[]{:S(2)}) collective-permute-start(bf16[8,3,192,512]{3,2,1,0:T(8,128)(2,1)} %get-tuple-element.372.refs_0_.refs_1_), channel_id=1, source_target_pairs={{0,8},{8,0},{16,24},{24,16},{1,9},{9,1},{17,25},{25,17},{2,10},{10... | collective-permute-start | bytes 14155784 | tf_op jit(solution)/shard_map/ppermute | solution.py:35
  27.6 36.8 %collective-permute-start.7 = (bf16[8,3,64,512]{3,2,1,0:T(8,128)(2,1)S(1)}, bf16[8,3,64,512]{3,2,1,0:T(8,128)(2,1)}, u32[]{:S(2)}, u32[]{:S(2)}) collective-permute-start(bf16[8,3,64,512]{3,2,1,0:T(8,128)(2,1)S(1)} %copy-done.68), channel_id=1, source_target_pairs={{0,16},{8,24},{16,0},{24,8},{1,17},{9,25},{17,1},{25,9},{2,18},{10... | collective-permute-start | bytes 4718600 | tf_op jit(solution)/shard_map/ppermute | solution.py:35
  64.4 36.2 %collective-permute-start.14 = (bf16[8,3,64,512]{3,2,1,0:T(8,128)(2,1)}, bf16[8,3,64,512]{3,2,1,0:T(8,128)(2,1)}, u32[]{:S(2)}, u32[]{:S(2)}) collective-permute-start(bf16[8,3,64,512]{3,2,1,0:T(8,128)(2,1)} %collective-permute-done.7.refs_2_.refs_3_), channel_id=1, source_target_pairs={{0,4},{4,0},{1,5},{5,1},{2,6},{6,2},{3,7},{7,3},{8,12},{12,8},{9,1... | collective-permute-start | bytes 4718600 | tf_op jit(solution)/shard_map/ppermute | solution.py:35
  65.9 35.9 %collective-permute-start.15 = (bf16[8,3,64,512]{3,2,1,0:T(8,128)(2,1)}, bf16[8,3,64,512]{3,2,1,0:T(8,128)(2,1)}, u32[]{:S(2)}, u32[]{:S(2)}) collective-permute-start(bf16[8,3,64,512]{3,2,1,0:T(8,128)(2,1)} %get-tuple-element.366), channel_id=1, source_target_pairs={{0,16},{8,24},{16,0},{24,8},{1,17},{9,25},{17,1},{25,9},{2,18},{10... | collective-permute-start | bytes 4718600 | tf_op jit(solution)/shard_map/ppermute | solution.py:35
  66.4 35.4 %collective-permute-start.16 = (bf16[8,3,64,512]{3,2,1,0:T(8,128)(2,1)}, bf16[8,3,64,512]{3,2,1,0:T(8,128)(2,1)}, u32[]{:S(2)}, u32[]{:S(2)}) collective-permute-start(bf16[8,3,64,512]{3,2,1,0:T(8,128)(2,1)} %collective-permute-done.7.refs_2_.refs_3_), channel_id=1, source_target_pairs={{0,8},{8,0},{16,24},{24,16},{1,9},{9,1},{17,25},{25,17},{2,10},{10... | collective-permute-start | bytes 4718600 | tf_op jit(solution)/shard_map/ppermute | solution.py:35
  122.8 58.6 %collective-permute-start.30 = (bf16[8,3,192,512]{3,2,1,0:T(8,128)(2,1)}, bf16[8,3,192,512]{3,2,1,0:T(8,128)(2,1)S(1)}, u32[]{:S(2)}, u32[]{:S(2)}) collective-permute-start(bf16[8,3,192,512]{3,2,1,0:T(8,128)(2,1)} %get-tuple-element.423.refs_0_), channel_id=1, source_target_pairs={{0,8},{8,0},{16,24},{24,16},{1,9},{9,1},{17,25},{25,17},{2,10},{10... | collective-permute-start | bytes 14155784 | tf_op jit(solution)/shard_map/ppermute | solution.py:35
  123.9 57.5 %collective-permute-start.31 = (bf16[8,3,64,512]{3,2,1,0:T(8,128)(2,1)S(1)}, bf16[8,3,64,512]{3,2,1,0:T(8,128)(2,1)S(1)}, u32[]{:S(2)}, u32[]{:S(2)}) collective-permute-start(bf16[8,3,64,512]{3,2,1,0:T(8,128)(2,1)S(1)} %copy-done.66), channel_id=1, source_target_pairs={{0,16},{8,24},{16,0},{24,8},{1,17},{9,25},{17,1},{25,9},{2,18},{10... | collective-permute-start | bytes 4718600 | tf_op jit(solution)/shard_map/ppermute | solution.py:35
  138.8 42.6 %collective-permute-start.29 = (bf16[192,2560]{1,0:T(8,128)(2,1)S(1)}, bf16[192,2560]{1,0:T(8,128)(2,1)S(1)}, u32[]{:S(2)}, u32[]{:S(2)}) collective-permute-start(bf16[192,2560]{1,0:T(8,128)(2,1)S(1)} %concatenate.39.refs_4_.refs_2_.refs_0_.refs_8_), channel_id=1, source_target_pairs={{0,16},{8,24},{16,0},{24,8},{1,17},{9,25},{17,1},{25,9},{2,18},{10... | collective-permute-start | bytes 2949128 | tf_op jit(solution)/shard_map/ppermute | solution.py:35
  206.5 35.3 %collective-permute-start.44 = (bf16[8,3,64,512]{3,2,1,0:T(8,128)(2,1)S(1)}, bf16[8,3,64,512]{3,2,1,0:T(8,128)(2,1)S(1)}, u32[]{:S(2)}, u32[]{:S(2)}) collective-permute-start(bf16[8,3,64,512]{3,2,1,0:T(8,128)(2,1)S(1)} %copy-done.64), channel_id=1, source_target_pairs={{0,16},{8,24},{16,0},{24,8},{1,17},{9,25},{17,1},{25,9},{2,18},{10... | collective-permute-start | bytes 4718600 | tf_op jit(solution)/shard_map/ppermute | solution.py:35
  207.0 35.0 %collective-permute-start.43 = (bf16[8,3,64,512]{3,2,1,0:T(8,128)(2,1)S(1)}, bf16[8,3,64,512]{3,2,1,0:T(8,128)(2,1)S(1)}, u32[]{:S(2)}, u32[]{:S(2)}) collective-permute-start(bf16[8,3,64,512]{3,2,1,0:T(8,128)(2,1)S(1)} %collective-permute-done.31.refs_2_), channel_id=1, source_target_pairs={{0,4},{4,0},{1,5},{5,1},{2,6},{6,2},{3,7},{7,3},{8,12},{12,8},{9,1... | collective-permute-start | bytes 4718600 | tf_op jit(solution)/shard_map/ppermute | solution.py:35
  207.5 34.5 %collective-permute-start.45 = (bf16[8,3,64,512]{3,2,1,0:T(8,128)(2,1)S(1)}, bf16[8,3,64,512]{3,2,1,0:T(8,128)(2,1)S(1)}, u32[]{:S(2)}, u32[]{:S(2)}) collective-permute-start(bf16[8,3,64,512]{3,2,1,0:T(8,128)(2,1)S(1)} %collective-permute-done.31.refs_2_), channel_id=1, source_target_pairs={{0,8},{8,0},{16,24},{24,16},{1,9},{9,1},{17,25},{25,17},{2,10},{10... | collective-permute-start | bytes 4718600 | tf_op jit(solution)/shard_map/ppermute | solution.py:35
  297.7 46.5 %collective-permute-start.56 = (bf16[1,3,384,512]{3,2,1,0:T(8,128)(2,1)S(1)}, bf16[1,3,384,512]{3,2,1,0:T(8,128)(2,1)S(1)}, u32[]{:S(2)}, u32[]{:S(2)}) collective-permute-start(bf16[1,3,384,512]{3,2,1,0:T(8,128)(2,1)S(1)} %copy-done.70), channel_id=1, source_target_pairs={{0,16},{8,24},{16,0},{24,8},{1,17},{9,25},{17,1},{25,9},{2,18},{10... | collective-permute-start | bytes 3538952 | tf_op jit(solution)/shard_map/ppermute | solution.py:35
  344.6 52.1 %collective-permute-start.60 = (bf16[2,3,384,512]{3,2,1,0:T(8,128)(2,1)S(1)}, bf16[2,3,384,512]{3,2,1,0:T(8,128)(2,1)S(1)}, u32[]{:S(2)}, u32[]{:S(2)}) collective-permute-start(bf16[2,3,384,512]{3,2,1,0:T(8,128)(2,1)S(1)} %copy-done.94), channel_id=1, source_target_pairs={{0,16},{8,24},{16,0},{24,8},{1,17},{9,25},{17,1},{25,9},{2,18},{10... | collective-permute-start | bytes 7077896 | tf_op jit(solution)/shard_map/ppermute | solution.py:35
  346.5 35.0 %collective-permute-start.59 = (bf16[1,3,384,512]{3,2,1,0:T(8,128)(2,1)S(1)}, bf16[1,3,384,512]{3,2,1,0:T(8,128)(2,1)S(1)}, u32[]{:S(2)}, u32[]{:S(2)}) collective-permute-start(bf16[1,3,384,512]{3,2,1,0:T(8,128)(2,1)S(1)} %add_convert_fusion.4.part_ref), channel_id=1, source_target_pairs={{0,4},{4,0},{1,5},{5,1},{2,6},{6,2},{3,7},{7,3},{8,12},{12,8},{9,1... | collective-permute-start | bytes 3538952 | tf_op jit(solution)/shard_map/ppermute | solution.py:35
  361.2 61.6 %collective-permute-start.69 = (bf16[1,3,384,512]{3,2,1,0:T(8,128)(2,1)S(1)}, bf16[1,3,384,512]{3,2,1,0:T(8,128)(2,1)S(1)}, u32[]{:S(2)}, u32[]{:S(2)}) collective-permute-start(bf16[1,3,384,512]{3,2,1,0:T(8,128)(2,1)S(1)} %add_convert_fusion.3.part_ref), channel_id=1, source_target_pairs={{0,4},{4,0},{1,5},{5,1},{2,6},{6,2},{3,7},{7,3},{8,12},{12,8},{9,1... | collective-permute-start | bytes 3538952 | tf_op jit(solution)/shard_map/ppermute | solution.py:35
  364.9 50.8 %collective-permute-start.66 = (bf16[192,2432]{1,0:T(8,128)(2,1)S(1)}, bf16[192,2432]{1,0:T(8,128)(2,1)S(1)}, u32[]{:S(2)}, u32[]{:S(2)}) collective-permute-start(bf16[192,2432]{1,0:T(8,128)(2,1)S(1)} %pad_maximum_fusion.1), channel_id=1, source_target_pairs={{0,8},{8,0},{16,24},{24,16},{1,9},{9,1},{17,25},{25,17},{2,10},{10... | collective-permute-start | bytes 2801672 | tf_op jit(solution)/shard_map/ppermute | solution.py:35
  367.4 48.3 %collective-permute-start.67 = (bf16[192,2432]{1,0:T(8,128)(2,1)S(1)}, bf16[192,2432]{1,0:T(8,128)(2,1)S(1)}, u32[]{:S(2)}, u32[]{:S(2)}) collective-permute-start(bf16[192,2432]{1,0:T(8,128)(2,1)S(1)} %pad_maximum_fusion.3), channel_id=1, source_target_pairs={{0,8},{8,0},{16,24},{24,16},{1,9},{9,1},{17,25},{25,17},{2,10},{10... | collective-permute-start | bytes 2801672 | tf_op jit(solution)/shard_map/ppermute | solution.py:35
  400.5 55.2 %collective-permute-start.71 = (bf16[2,3,384,512]{3,2,1,0:T(8,128)(2,1)S(1)}, bf16[2,3,384,512]{3,2,1,0:T(8,128)(2,1)}, u32[]{:S(2)}, u32[]{:S(2)}) collective-permute-start(bf16[2,3,384,512]{3,2,1,0:T(8,128)(2,1)S(1)} %add_convert_fusion.2.part_ref), channel_id=1, source_target_pairs={{0,4},{4,0},{1,5},{5,1},{2,6},{6,2},{3,7},{7,3},{8,12},{12,8},{9,1... | collective-permute-start | bytes 7077896 | tf_op jit(solution)/shard_map/ppermute | solution.py:35
  455.6 53.9 %collective-permute-start.83 = (bf16[2,3,384,512]{3,2,1,0:T(8,128)(2,1)}, bf16[2,3,384,512]{3,2,1,0:T(8,128)(2,1)S(1)}, u32[]{:S(2)}, u32[]{:S(2)}) collective-permute-start(bf16[2,3,384,512]{3,2,1,0:T(8,128)(2,1)} %get-tuple-element.550), channel_id=1, source_target_pairs={{0,16},{8,24},{16,0},{24,8},{1,17},{9,25},{17,1},{25,9},{2,18},{10... | collective-permute-start | bytes 7077896 | tf_op jit(solution)/shard_map/ppermute | solution.py:35
  510.3 78.4 %collective-permute-start.93 = (bf16[2,3,384,512]{3,2,1,0:T(8,128)(2,1)S(1)}, bf16[2,3,384,512]{3,2,1,0:T(8,128)(2,1)S(1)}, u32[]{:S(2)}, u32[]{:S(2)}) collective-permute-start(bf16[2,3,384,512]{3,2,1,0:T(8,128)(2,1)S(1)} %add_convert_fusion.1.part_ref), channel_id=1, source_target_pairs={{0,4},{4,0},{1,5},{5,1},{2,6},{6,2},{3,7},{7,3},{8,12},{12,8},{9,1... | collective-permute-start | bytes 7077896 | tf_op jit(solution)/shard_map/ppermute | solution.py:35
  511.2 77.5 %collective-permute-start.94 = (bf16[2,3,384,512]{3,2,1,0:T(8,128)(2,1)S(1)}, bf16[2,3,384,512]{3,2,1,0:T(8,128)(2,1)S(1)}, u32[]{:S(2)}, u32[]{:S(2)}) collective-permute-start(bf16[2,3,384,512]{3,2,1,0:T(8,128)(2,1)S(1)} %copy-done.93), channel_id=1, source_target_pairs={{0,16},{8,24},{16,0},{24,8},{1,17},{9,25},{17,1},{25,9},{2,18},{10... | collective-permute-start | bytes 7077896 | tf_op jit(solution)/shard_map/ppermute | solution.py:35
  525.6 51.2 %collective-permute-start.85 = (bf16[512,384]{1,0:T(8,128)(2,1)S(1)}, bf16[512,384]{1,0:T(8,128)(2,1)S(1)}, u32[]{:S(2)}, u32[]{:S(2)}) collective-permute-start(bf16[512,384]{1,0:T(8,128)(2,1)S(1)} %get-tuple-element.570), channel_id=1, source_target_pairs={{0,4},{4,0},{1,5},{5,1},{2,6},{6,2},{3,7},{7,3},{8,12},{12,8},{9,1... | collective-permute-start | bytes 1179656 | tf_op jit(solution)/shard_map/ppermute | solution.py:35
  537.3 39.5 %collective-permute-start.90 = (bf16[128,768]{1,0:T(8,128)(2,1)S(1)}, bf16[128,768]{1,0:T(8,128)(2,1)S(1)}, u32[]{:S(2)}, u32[]{:S(2)}) collective-permute-start(bf16[128,768]{1,0:T(8,128)(2,1)S(1)} %add_convert_fusion.20.refs_0_), channel_id=1, source_target_pairs={{0,1},{1,0},{2,3},{3,2},{4,5},{5,4},{6,7},{7,6},{8,9},{9,8},{10,11... | collective-permute-start | bytes 589832 | tf_op jit(solution)/shard_map/ppermute | solution.py:35
  596.6 51.4 %collective-permute-start.103 = (bf16[2,3,384,512]{3,2,1,0:T(8,128)(2,1)S(1)}, bf16[2,3,384,512]{3,2,1,0:T(8,128)(2,1)S(1)}, u32[]{:S(2)}, u32[]{:S(2)}) collective-permute-start(bf16[2,3,384,512]{3,2,1,0:T(8,128)(2,1)S(1)} %add_convert_fusion.part_ref), channel_id=1, source_target_pairs={{0,4},{4,0},{1,5},{5,1},{2,6},{6,2},{3,7},{7,3},{8,12},{12,8},{9,1... | collective-permute-start | bytes 7077896 | tf_op jit(solution)/shard_map/ppermute | solution.py:35
  (189 other events, 2153.2 us)

commit v5 on v4

--- a/solution.py
+++ b/solution.py
@@ -564,7 +564,7 @@
                 sin_ref[0, rows, :] = total[:, lanes : lanes + 128]
         sout_ref[0] = total[:, 2 * hid : 3 * hid]
 
-CHUNKS, PARTS = 2, ((2, 2), (1, 1, 2))
+CHUNKS, PARTS = 2, ((1, 1, 2), (1, 1, 2))
 SLOTS = {
     "start": ["pack 0", ("experts", 0)],
     ("attend", 0): ["slots"],
@@ -584,16 +584,15 @@
     (1, "attention sum"): [(1, "packs")],
     (1, "input"): [(1, 0), (1, 1)],
     (0, "experts"): [(1, 2), (1, "packs"), (0, 0)],
-    (0, "ffn half"): [(1, 1), "result"],
-    (0, "ffn sum"): [(1, 2), "result", (0, 0), (0, 1), (0, "shared")],
-    (0, "attention"): [(1, "packs")],
-    (0, "project"): [(0, "attention"), "result"],
-    (0, "attention half"): [(0, 0), (0, 1), (0, "shared")],
-    (0, "attention sum"): [(0, 0)],
-    (0, "input"): [(0, 1), (0, "shared"), (0, "attention")],
+    (0, "ffn half"): [(1, 1), "result", (0, 0), (0, 1)],
+    (0, "ffn sum"): [(1, 2), (1, "packs"), "result", (0, 0), (0, 2), (0, "shared")],
+    (0, "project"): [(0, 0), (0, 1), (0, "attention"), "result"],
+    (0, "attention half"): [(0, 2), (0, "shared")],
+    (0, "attention sum"): [(0, 1)],
+    (0, "input"): [(0, 1), (0, 2), (0, "shared"), (0, "attention")],
 }
 TAIL = (
-    ["gains", (0, 1), (0, "shared"), (0, "attention")],
+    ["gains", (0, 2), (0, "shared"), (0, "attention")],
     ["gains", (0, "attention")],
     ["gains"],
 )

time: 686 us -> 739 us (1.077)
  waiting for transfers between devices: 345 us -> 404 us
    ppermute x115 -> x118, waiting for transfers between devices: 345 us -> 404 us  [swap(): return lax.ppermute(values, axis, [(k, k ^ mask) for k in range(count)])]
    ppermute x115 -> x118, starting transfers between devices: 107 us -> 101 us  [swap(): return lax.ppermute(values, axis, [(k, k ^ mask) for k in range(count)])]
    pallas_call x42 -> x44, Pallas kernels: 172 us -> 174 us  [call(): pl.pallas_call(kernel, out_shape=[o[0] for o in outs], grid_spec=pltpu.Pr...]
    unnamed x202 -> x198, local copies, waits for them, and re-layouts: 24.7 us -> 24.7 us
  transfers between devices with their start and end apart: 115 -> 118, of which waited for: 69 -> 67; matrix products, arithmetic and copies ran while one was open for 3% -> 3% of each run, Pallas kernels for 19% -> 18%
where the time goes in v5:
time: 739 us; the launch traced here: 732 us
  waiting for transfers between devices  404 us (55%)
  Pallas kernels  174 us (24%)
  starting transfers between devices  101 us (14%)
  local copies, waits for them, and re-layouts  40.3 us (5%)
  other arithmetic  8.02 us (1%)
    ppermute x118, waiting for transfers between devices, swap(): return lax.ppermute(values, axis, [(k, k ^ mask) for k in range(count)])  404 us
    pallas_call x44, Pallas kernels, call(): pl.pallas_call(kernel, out_shape=[o[0] for o in outs], grid_spec=pltpu.Pr...  174 us
    ppermute x118, starting transfers between devices, swap(): return lax.ppermute(values, axis, [(k, k ^ mask) for k in range(count)])  101 us
    unnamed x198, local copies, waits for them, and re-layouts  24.7 us
  transfers between devices with their start and end apart: 118, of which 67 were waited for; matrix products, arithmetic and copies ran while one was open for 3% of the time, Pallas kernels for 18%

profile of v5, /device:TPU:0, one launch (start us, length us, event | category | flops | bytes accessed | tf_op | source)
XLA Modules:
  0.0 731.6 jit_solution(1683124182336748378)
XLA Ops:
  34.1 9.2 %collective-permute-done.3.refs_1_ = bf16[512,384]{1,0:T(8,128)(2,1)S(1)} collective-permute-done((bf16[512,384]{1,0:T(8,128)(2,1)S(1)}, bf16[512,384]{1,0:T(8,128)(2,1)S(1)}, u32[]{:S(2)}, u32[]{:S(2)}) %collective-permute-start.3) | collective-permute-done | bytes 393248 | tf_op jit(solution)/shard_map/ppermute | solution.py:35
  111.8 11.0 %shard_map.210 = (f32[512,768]{1,0:T(8,128)S(1)}, bf16[512,768]{1,0:T(8,128)(2,1)S(1)}, bf16[4,384,768]{2,1,0:T(8,128)(2,1)S(1)}, bf16[4,384,512]{2,1,0:T(8,128)(2,1)S(1)}, bf16[4,384,512]{2,1,0:T(8,128)(2,1)S(1)}) custom-call(s32[5]{0:T(128)S(1)} %stack.23.scal, bf16[512,768]{1,0:T(8,128)(2,1)S(1)} %copy-done.11, bf16[512,768]{1,0:T(8,128)(2,1)S(1)} %copy-done.52, ...), custom_call_target="tpu_custom_call" | custom-call | flops 6039797 | bytes 28344 | tf_op jit(solution)/shard_map/pallas_call | solution.py:86
  151.8 9.3 %collective-permute-done.24 = bf16[128,768]{1,0:T(8,128)(2,1)S(1)} collective-permute-done((bf16[128,768]{1,0:T(8,128)(2,1)S(1)}, bf16[128,768]{1,0:T(8,128)(2,1)S(1)}, u32[]{:S(2)}, u32[]{:S(2)}) %collective-permute-start.24) | collective-permute-done | bytes 196640 | tf_op jit(solution)/shard_map/ppermute | solution.py:35
  165.3 16.1 %collective-permute-done.29.refs_6_.refs_4_.refs_2_.refs_10_ = bf16[192,2560]{1,0:T(8,128)(2,1)S(1)} collective-permute-done((bf16[192,2560]{1,0:T(8,128)(2,1)S(1)}, bf16[192,2560]{1,0:T(8,128)(2,1)S(1)}, u32[]{:S(2)}, u32[]{:S(2)}) %collective-permute-start.29) | collective-permute-done | bytes 983072 | tf_op jit(solution)/shard_map/ppermute | solution.py:35
  188.2 10.7 %collective-permute-done.34.refs_1_ = bf16[512,384]{1,0:T(8,128)(2,1)S(1)} collective-permute-done((bf16[512,384]{1,0:T(8,128)(2,1)S(1)}, bf16[512,384]{1,0:T(8,128)(2,1)S(1)}, u32[]{:S(2)}, u32[]{:S(2)}) %collective-permute-start.34) | collective-permute-done | bytes 393248 | tf_op jit(solution)/shard_map/ppermute | solution.py:35
  219.1 8.8 %collective-permute-done.36 = bf16[128,768]{1,0:T(8,128)(2,1)S(1)} collective-permute-done((bf16[128,768]{1,0:T(8,128)(2,1)S(1)}, bf16[128,768]{1,0:T(8,128)(2,1)S(1)}, u32[]{:S(2)}, u32[]{:S(2)}) %collective-permute-start.36) | collective-permute-done | bytes 196640 | tf_op jit(solution)/shard_map/ppermute | solution.py:35
  250.1 29.6 %shard_map.216 = (f32[512,768]{1,0:T(8,128)}, bf16[512,768]{1,0:T(8,128)(2,1)}, bf16[1,3,384,512]{3,2,1,0:T(8,128)(2,1)S(1)}, bf16[1,3,384,512]{3,2,1,0:T(8,128)...) custom-call(s32[5]{0:T(128)S(1)} %stack.23.scal, ...), custom_call_target="tpu_custom_call" | custom-call | flops 9663676 | bytes 36208 | tf_op jit(solution)/shard_map/pallas_call | solution.py:86
  328.7 9.8 %shard_map.221 = (bf16[512,192]{1,0:T(8,128)(2,1)S(1)}, bf16[768,192]{1,0:T(8,128)(2,1)S(1)}, bf16[512,384]{1,0:T(8,128)(2,1)S(1)}, bf16[512,384]{1,0:T(8,128)(2,1)S(1)}) custom-call(s32[5]{0:T(128)S(1)} %stack.23.scal, f32[1,1024]{1,0:T(1,128)S(1)} %bitcast.89, bf16[512,192]{1,0:T(8,128)(2,1)S(1)} %get-tuple-element.416.q_ref, ...), custom_call_target="tpu_custom_call" | custom-call | flops 1308622 | bytes 7180 | tf_op jit(solution)/shard_map/pallas_call | solution.py:86
  367.5 14.0 %collective-permute-done.59.got_ref = bf16[1,3,384,512]{3,2,1,0:T(8,128)(2,1)S(1)} collective-permute-done((bf16[1,3,384,512]{3,2,1,0:T(8,128)(2,1)S(1)}, bf16[1,3,384,512]{3,2,1,0:T(8,128)(2,1)S(1)}, u32[]{:S(2)}, u32[]{:S(2)}) %collective-permute-start.59) | collective-permute-done | bytes 1179680 | tf_op jit(solution)/shard_map/ppermute | solution.py:35
  384.2 12.4 %collective-permute-done.60 = bf16[2,3,384,512]{3,2,1,0:T(8,128)(2,1)S(1)} collective-permute-done((bf16[2,3,384,512]{3,2,1,0:T(8,128)(2,1)S(1)}, bf16[2,3,384,512]{3,2,1,0:T(8,128)(2,1)S(1)}, u32[]{:S(2)}, u32[]{:S(2)}) %collective-permute-start.60) | collective-permute-done | bytes 2359328 | tf_op jit(solution)/shard_map/ppermute | solution.py:35
  424.2 21.4 %shard_map.225 = (f32[512,768]{1,0:T(8,128)S(1)}, bf16[512,768]{1,0:T(8,128)(2,1)}, bf16[1,3,384,512]{3,2,1,0:T(8,128)(2,1)S(1)}, bf16[1,3,384,512]{3,2,1,0:T(8,...) custom-call(s32[5]{0:T(128)S(1)} %stack.23.scal, ...), custom_call_target="tpu_custom_call" | custom-call | flops 9663676 | bytes 37781 | tf_op jit(solution)/shard_map/pallas_call | solution.py:86
  445.7 9.9 %collective-permute-done.71.got_ref = bf16[2,3,384,512]{3,2,1,0:T(8,128)(2,1)} collective-permute-done((bf16[2,3,384,512]{3,2,1,0:T(8,128)(2,1)S(1)}, bf16[2,3,384,512]{3,2,1,0:T(8,128)(2,1)}, u32[]{:S(2)}, u32[]{:S(2)}) %collective-permute-start.71) | collective-permute-done | bytes 2359328 | tf_op jit(solution)/shard_map/ppermute | solution.py:35
  472.9 11.1 %collective-permute-done.76 = bf16[1,3,384,512]{3,2,1,0:T(8,128)(2,1)S(1)} collective-permute-done((bf16[1,3,384,512]{3,2,1,0:T(8,128)(2,1)S(1)}, bf16[1,3,384,512]{3,2,1,0:T(8,128)(2,1)S(1)}, u32[]{:S(2)}, u32[]{:S(2)}) %collective-permute-start.76) | collective-permute-done | bytes 1179680 | tf_op jit(solution)/shard_map/ppermute | solution.py:35
  489.7 9.8 %collective-permute-done.79 = bf16[128,768]{1,0:T(8,128)(2,1)S(1)} collective-permute-done((bf16[128,768]{1,0:T(8,128)(2,1)S(1)}, bf16[128,768]{1,0:T(8,128)(2,1)S(1)}, u32[]{:S(2)}, u32[]{:S(2)}) %collective-permute-start.79) | collective-permute-done | bytes 196640 | tf_op jit(solution)/shard_map/ppermute | solution.py:35
  499.5 11.7 %collective-permute-done.77 = bf16[128,768]{1,0:T(8,128)(2,1)S(1)} collective-permute-done((bf16[128,768]{1,0:T(8,128)(2,1)S(1)}, bf16[128,768]{1,0:T(8,128)(2,1)S(1)}, u32[]{:S(2)}, u32[]{:S(2)}) %collective-permute-start.77) | collective-permute-done | bytes 196640 | tf_op jit(solution)/shard_map/ppermute | solution.py:35
  514.5 17.5 %collective-permute-done.83.got_ref = bf16[192,2432]{1,0:T(8,128)(2,1)S(1)} collective-permute-done((bf16[192,2432]{1,0:T(8,128)(2,1)S(1)}, bf16[192,2432]{1,0:T(8,128)(2,1)S(1)}, u32[]{:S(2)}, u32[]{:S(2)}) %collective-permute-start.83) | collective-permute-done | bytes 933920 | tf_op jit(solution)/shard_map/ppermute | solution.py:35
  539.7 9.7 %shard_map.233 = (bf16[512,192]{1,0:T(8,128)(2,1)S(1)}, bf16[768,192]{1,0:T(8,128)(2,1)S(1)}, bf16[512,384]{1,0:T(8,128)(2,1)S(1)}, bf16[512,384]{1,0:T(8,128)(2,1)S(1)}) custom-call(s32[5]{0:T(128)S(1)} %stack.23.scal, f32[1,1024]{1,0:T(1,128)S(1)} %bitcast.90, bf16[512,192]{1,0:T(8,128)(2,1)S(1)} %copy-done.40, ...), custom_call_target="tpu_custom_call" | custom-call | flops 1308622 | bytes 4624 | tf_op jit(solution)/shard_map/pallas_call | solution.py:86
  564.0 8.9 %collective-permute-done.90 = bf16[128,768]{1,0:T(8,128)(2,1)S(1)} collective-permute-done((bf16[128,768]{1,0:T(8,128)(2,1)S(1)}, bf16[128,768]{1,0:T(8,128)(2,1)S(1)}, u32[]{:S(2)}, u32[]{:S(2)}) %collective-permute-start.90) | collective-permute-done | bytes 196640 | tf_op jit(solution)/shard_map/ppermute | solution.py:35
  573.0 11.0 %collective-permute-done.92 = bf16[128,768]{1,0:T(8,128)(2,1)S(1)} collective-permute-done((bf16[128,768]{1,0:T(8,128)(2,1)S(1)}, bf16[128,768]{1,0:T(8,128)(2,1)S(1)}, u32[]{:S(2)}, u32[]{:S(2)}) %collective-permute-start.92) | collective-permute-done | bytes 196640 | tf_op jit(solution)/shard_map/ppermute | solution.py:35
  589.0 20.4 %collective-permute-done.88 = bf16[1,3,384,512]{3,2,1,0:T(8,128)(2,1)S(1)} collective-permute-done((bf16[1,3,384,512]{3,2,1,0:T(8,128)(2,1)S(1)}, bf16[1,3,384,512]{3,2,1,0:T(8,128)(2,1)S(1)}, u32[]{:S(2)}, u32[]{:S(2)}) %collective-permute-start.88) | collective-permute-done | bytes 1179680 | tf_op jit(solution)/shard_map/ppermute | solution.py:35
  627.1 10.8 %collective-permute-done.101 = bf16[128,768]{1,0:T(8,128)(2,1)S(1)} collective-permute-done((bf16[128,768]{1,0:T(8,128)(2,1)S(1)}, bf16[128,768]{1,0:T(8,128)(2,1)S(1)}, u32[]{:S(2)}, u32[]{:S(2)}) %collective-permute-start.101) | collective-permute-done | bytes 196640 | tf_op jit(solution)/shard_map/ppermute | solution.py:35
  665.0 13.2 %collective-permute-done.107 = bf16[192,1536]{1,0:T(8,128)(2,1)S(1)} collective-permute-done((bf16[192,1536]{1,0:T(8,128)(2,1)S(1)}, bf16[192,1536]{1,0:T(8,128)(2,1)S(1)}, u32[]{:S(2)}, u32[]{:S(2)}) %collective-permute-start.107) | collective-permute-done | bytes 589856 | tf_op jit(solution)/shard_map/ppermute | solution.py:35
  678.2 20.5 %collective-permute-done.106.got_ref = bf16[2,3,384,512]{3,2,1,0:T(8,128)(2,1)S(1)} collective-permute-done((bf16[2,3,384,512]{3,2,1,0:T(8,128)(2,1)S(1)}, bf16[2,3,384,512]{3,2,1,0:T(8,128)(2,1)S(1)}, u32[]{:S(2)}, u32[]{:S(2)}) %collective-permute-start.106) | collective-permute-done | bytes 2359328 | tf_op jit(solution)/shard_map/ppermute | solution.py:35
  708.2 12.5 %collective-permute-done.116.got_ref = bf16[192,1536]{1,0:T(8,128)(2,1)S(1)} collective-permute-done((bf16[192,1536]{1,0:T(8,128)(2,1)S(1)}, bf16[192,1536]{1,0:T(8,128)(2,1)S(1)}, u32[]{:S(2)}, u32[]{:S(2)}) %collective-permute-start.116) | collective-permute-done | bytes 589856 | tf_op jit(solution)/shard_map/ppermute | solution.py:35
  (550 shorter events, 410.1 us)
Async XLA Ops:
  20.1 44.2 %collective-permute-start.6 = (bf16[8,3,192,512]{3,2,1,0:T(8,128)(2,1)}, bf16[8,3,192,512]{3,2,1,0:T(8,128)(2,1)}, u32[]{:S(2)}, u32[]{:S(2)}) collective-permute-start(bf16[8,3,192,512]{3,2,1,0:T(8,128)(2,1)} %get-tuple-element.383.refs_0_.refs_1_), channel_id=1, source_target_pairs={{0,8},{8,0},{16,24},{24,16},{1,9},{9,1},{17,25},{25,17},{2,10},{10... | collective-permute-start | bytes 14155784 | tf_op jit(solution)/shard_map/ppermute | solution.py:35
  27.6 36.8 %collective-permute-start.7 = (bf16[8,3,64,512]{3,2,1,0:T(8,128)(2,1)S(1)}, bf16[8,3,64,512]{3,2,1,0:T(8,128)(2,1)}, u32[]{:S(2)}, u32[]{:S(2)}) collective-permute-start(bf16[8,3,64,512]{3,2,1,0:T(8,128)(2,1)S(1)} %copy-done.65), channel_id=1, source_target_pairs={{0,16},{8,24},{16,0},{24,8},{1,17},{9,25},{17,1},{25,9},{2,18},{10... | collective-permute-start | bytes 4718600 | tf_op jit(solution)/shard_map/ppermute | solution.py:35
  64.3 36.2 %collective-permute-start.14 = (bf16[8,3,64,512]{3,2,1,0:T(8,128)(2,1)}, bf16[8,3,64,512]{3,2,1,0:T(8,128)(2,1)}, u32[]{:S(2)}, u32[]{:S(2)}) collective-permute-start(bf16[8,3,64,512]{3,2,1,0:T(8,128)(2,1)} %collective-permute-done.7.refs_2_.refs_3_), channel_id=1, source_target_pairs={{0,4},{4,0},{1,5},{5,1},{2,6},{6,2},{3,7},{7,3},{8,12},{12,8},{9,1... | collective-permute-start | bytes 4718600 | tf_op jit(solution)/shard_map/ppermute | solution.py:35
  65.9 35.9 %collective-permute-start.15 = (bf16[8,3,64,512]{3,2,1,0:T(8,128)(2,1)}, bf16[8,3,64,512]{3,2,1,0:T(8,128)(2,1)}, u32[]{:S(2)}, u32[]{:S(2)}) collective-permute-start(bf16[8,3,64,512]{3,2,1,0:T(8,128)(2,1)} %get-tuple-element.377), channel_id=1, source_target_pairs={{0,16},{8,24},{16,0},{24,8},{1,17},{9,25},{17,1},{25,9},{2,18},{10... | collective-permute-start | bytes 4718600 | tf_op jit(solution)/shard_map/ppermute | solution.py:35
  66.4 35.4 %collective-permute-start.16 = (bf16[8,3,64,512]{3,2,1,0:T(8,128)(2,1)}, bf16[8,3,64,512]{3,2,1,0:T(8,128)(2,1)}, u32[]{:S(2)}, u32[]{:S(2)}) collective-permute-start(bf16[8,3,64,512]{3,2,1,0:T(8,128)(2,1)} %collective-permute-done.7.refs_2_.refs_3_), channel_id=1, source_target_pairs={{0,8},{8,0},{16,24},{24,16},{1,9},{9,1},{17,25},{25,17},{2,10},{10... | collective-permute-start | bytes 4718600 | tf_op jit(solution)/shard_map/ppermute | solution.py:35
  122.8 58.6 %collective-permute-start.30 = (bf16[8,3,192,512]{3,2,1,0:T(8,128)(2,1)}, bf16[8,3,192,512]{3,2,1,0:T(8,128)(2,1)S(1)}, u32[]{:S(2)}, u32[]{:S(2)}) collective-permute-start(bf16[8,3,192,512]{3,2,1,0:T(8,128)(2,1)} %get-tuple-element.434.refs_0_), channel_id=1, source_target_pairs={{0,8},{8,0},{16,24},{24,16},{1,9},{9,1},{17,25},{25,17},{2,10},{10... | collective-permute-start | bytes 14155784 | tf_op jit(solution)/shard_map/ppermute | solution.py:35
  123.9 57.5 %collective-permute-start.31 = (bf16[8,3,64,512]{3,2,1,0:T(8,128)(2,1)S(1)}, bf16[8,3,64,512]{3,2,1,0:T(8,128)(2,1)S(1)}, u32[]{:S(2)}, u32[]{:S(2)}) collective-permute-start(bf16[8,3,64,512]{3,2,1,0:T(8,128)(2,1)S(1)} %copy-done.63), channel_id=1, source_target_pairs={{0,16},{8,24},{16,0},{24,8},{1,17},{9,25},{17,1},{25,9},{2,18},{10... | collective-permute-start | bytes 4718600 | tf_op jit(solution)/shard_map/ppermute | solution.py:35
  138.7 42.8 %collective-permute-start.29 = (bf16[192,2560]{1,0:T(8,128)(2,1)S(1)}, bf16[192,2560]{1,0:T(8,128)(2,1)S(1)}, u32[]{:S(2)}, u32[]{:S(2)}) collective-permute-start(bf16[192,2560]{1,0:T(8,128)(2,1)S(1)} %concatenate.39.refs_4_.refs_2_.refs_0_.refs_8_), channel_id=1, source_target_pairs={{0,16},{8,24},{16,0},{24,8},{1,17},{9,25},{17,1},{25,9},{2,18},{10... | collective-permute-start | bytes 2949128 | tf_op jit(solution)/shard_map/ppermute | solution.py:35
  206.5 35.3 %collective-permute-start.44 = (bf16[8,3,64,512]{3,2,1,0:T(8,128)(2,1)S(1)}, bf16[8,3,64,512]{3,2,1,0:T(8,128)(2,1)S(1)}, u32[]{:S(2)}, u32[]{:S(2)}) collective-permute-start(bf16[8,3,64,512]{3,2,1,0:T(8,128)(2,1)S(1)} %copy-done.61), channel_id=1, source_target_pairs={{0,16},{8,24},{16,0},{24,8},{1,17},{9,25},{17,1},{25,9},{2,18},{10... | collective-permute-start | bytes 4718600 | tf_op jit(solution)/shard_map/ppermute | solution.py:35
  207.0 35.0 %collective-permute-start.43 = (bf16[8,3,64,512]{3,2,1,0:T(8,128)(2,1)S(1)}, bf16[8,3,64,512]{3,2,1,0:T(8,128)(2,1)S(1)}, u32[]{:S(2)}, u32[]{:S(2)}) collective-permute-start(bf16[8,3,64,512]{3,2,1,0:T(8,128)(2,1)S(1)} %collective-permute-done.31.refs_2_), channel_id=1, source_target_pairs={{0,4},{4,0},{1,5},{5,1},{2,6},{6,2},{3,7},{7,3},{8,12},{12,8},{9,1... | collective-permute-start | bytes 4718600 | tf_op jit(solution)/shard_map/ppermute | solution.py:35
  297.6 46.5 %collective-permute-start.56 = (bf16[1,3,384,512]{3,2,1,0:T(8,128)(2,1)S(1)}, bf16[1,3,384,512]{3,2,1,0:T(8,128)(2,1)S(1)}, u32[]{:S(2)}, u32[]{:S(2)}) collective-permute-start(bf16[1,3,384,512]{3,2,1,0:T(8,128)(2,1)S(1)} %copy-done.67), channel_id=1, source_target_pairs={{0,16},{8,24},{16,0},{24,8},{1,17},{9,25},{17,1},{25,9},{2,18},{10... | collective-permute-start | bytes 3538952 | tf_op jit(solution)/shard_map/ppermute | solution.py:35
  344.5 52.1 %collective-permute-start.60 = (bf16[2,3,384,512]{3,2,1,0:T(8,128)(2,1)S(1)}, bf16[2,3,384,512]{3,2,1,0:T(8,128)(2,1)S(1)}, u32[]{:S(2)}, u32[]{:S(2)}) collective-permute-start(bf16[2,3,384,512]{3,2,1,0:T(8,128)(2,1)S(1)} %copy-done.92), channel_id=1, source_target_pairs={{0,16},{8,24},{16,0},{24,8},{1,17},{9,25},{17,1},{25,9},{2,18},{10... | collective-permute-start | bytes 7077896 | tf_op jit(solution)/shard_map/ppermute | solution.py:35
  361.1 60.7 %collective-permute-start.69 = (bf16[1,3,384,512]{3,2,1,0:T(8,128)(2,1)S(1)}, bf16[1,3,384,512]{3,2,1,0:T(8,128)(2,1)S(1)}, u32[]{:S(2)}, u32[]{:S(2)}) collective-permute-start(bf16[1,3,384,512]{3,2,1,0:T(8,128)(2,1)S(1)} %add_convert_fusion.4.part_ref), channel_id=1, source_target_pairs={{0,4},{4,0},{1,5},{5,1},{2,6},{6,2},{3,7},{7,3},{8,12},{12,8},{9,1... | collective-permute-start | bytes 3538952 | tf_op jit(solution)/shard_map/ppermute | solution.py:35
  364.9 50.5 %collective-permute-start.66 = (bf16[192,2432]{1,0:T(8,128)(2,1)S(1)}, bf16[192,2432]{1,0:T(8,128)(2,1)S(1)}, u32[]{:S(2)}, u32[]{:S(2)}) collective-permute-start(bf16[192,2432]{1,0:T(8,128)(2,1)S(1)} %pad_maximum_fusion.1), channel_id=1, source_target_pairs={{0,8},{8,0},{16,24},{24,16},{1,9},{9,1},{17,25},{25,17},{2,10},{10... | collective-permute-start | bytes 2801672 | tf_op jit(solution)/shard_map/ppermute | solution.py:35
  367.4 48.0 %collective-permute-start.67 = (bf16[192,2432]{1,0:T(8,128)(2,1)S(1)}, bf16[192,2432]{1,0:T(8,128)(2,1)S(1)}, u32[]{:S(2)}, u32[]{:S(2)}) collective-permute-start(bf16[192,2432]{1,0:T(8,128)(2,1)S(1)} %pad_maximum_fusion.3), channel_id=1, source_target_pairs={{0,8},{8,0},{16,24},{24,16},{1,9},{9,1},{17,25},{25,17},{2,10},{10... | collective-permute-start | bytes 2801672 | tf_op jit(solution)/shard_map/ppermute | solution.py:35
  400.3 55.3 %collective-permute-start.71 = (bf16[2,3,384,512]{3,2,1,0:T(8,128)(2,1)S(1)}, bf16[2,3,384,512]{3,2,1,0:T(8,128)(2,1)}, u32[]{:S(2)}, u32[]{:S(2)}) collective-permute-start(bf16[2,3,384,512]{3,2,1,0:T(8,128)(2,1)S(1)} %add_convert_fusion.1.part_ref), channel_id=1, source_target_pairs={{0,4},{4,0},{1,5},{5,1},{2,6},{6,2},{3,7},{7,3},{8,12},{12,8},{9,1... | collective-permute-start | bytes 7077896 | tf_op jit(solution)/shard_map/ppermute | solution.py:35
  471.2 60.8 %collective-permute-start.82 = (bf16[2,3,192,512]{3,2,1,0:T(8,128)(2,1)S(1)}, bf16[2,3,192,512]{3,2,1,0:T(8,128)(2,1)S(1)}, u32[]{:S(2)}, u32[]{:S(2)}) collective-permute-start(bf16[2,3,192,512]{3,2,1,0:T(8,128)(2,1)S(1)} %get-tuple-element.556), channel_id=1, source_target_pairs={{0,8},{8,0},{16,24},{24,16},{1,9},{9,1},{17,25},{25,17},{2,10},{10... | collective-permute-start | bytes 3538952 | tf_op jit(solution)/shard_map/ppermute | solution.py:35
  484.4 47.7 %collective-permute-start.85 = (bf16[1,3,384,512]{3,2,1,0:T(8,128)(2,1)S(1)}, bf16[1,3,384,512]{3,2,1,0:T(8,128)(2,1)S(1)}, u32[]{:S(2)}, u32[]{:S(2)}) collective-permute-start(bf16[1,3,384,512]{3,2,1,0:T(8,128)(2,1)S(1)} %add_convert_fusion.3.part_ref), channel_id=1, source_target_pairs={{0,4},{4,0},{1,5},{5,1},{2,6},{6,2},{3,7},{7,3},{8,12},{12,8},{9,1... | collective-permute-start | bytes 3538952 | tf_op jit(solution)/shard_map/ppermute | solution.py:35
  485.1 46.9 %collective-permute-start.83 = (bf16[192,2432]{1,0:T(8,128)(2,1)S(1)}, bf16[192,2432]{1,0:T(8,128)(2,1)S(1)}, u32[]{:S(2)}, u32[]{:S(2)}) collective-permute-start(bf16[192,2432]{1,0:T(8,128)(2,1)S(1)} %add_convert_fusion.6.part_ref), channel_id=1, source_target_pairs={{0,4},{4,0},{1,5},{5,1},{2,6},{6,2},{3,7},{7,3},{8,12},{12,8},{9,1... | collective-permute-start | bytes 2801672 | tf_op jit(solution)/shard_map/ppermute | solution.py:35
  532.1 92.5 %collective-permute-start.96 = (bf16[2,3,384,512]{3,2,1,0:T(8,128)(2,1)S(1)}, bf16[2,3,384,512]{3,2,1,0:T(8,128)(2,1)S(1)}, u32[]{:S(2)}, u32[]{:S(2)}) collective-permute-start(bf16[2,3,384,512]{3,2,1,0:T(8,128)(2,1)S(1)} %copy-done.91), channel_id=1, source_target_pairs={{0,16},{8,24},{16,0},{24,8},{1,17},{9,25},{17,1},{25,9},{2,18},{10... | collective-permute-start | bytes 7077896 | tf_op jit(solution)/shard_map/ppermute | solution.py:35
  535.2 74.2 %collective-permute-start.88 = (bf16[1,3,384,512]{3,2,1,0:T(8,128)(2,1)S(1)}, bf16[1,3,384,512]{3,2,1,0:T(8,128)(2,1)S(1)}, u32[]{:S(2)}, u32[]{:S(2)}) collective-permute-start(bf16[1,3,384,512]{3,2,1,0:T(8,128)(2,1)S(1)} %get-tuple-element.601), channel_id=1, source_target_pairs={{0,16},{8,24},{16,0},{24,8},{1,17},{9,25},{17,1},{25,9},{2,18},{10... | collective-permute-start | bytes 3538952 | tf_op jit(solution)/shard_map/ppermute | solution.py:35
  554.0 55.4 %collective-permute-start.87 = (bf16[1,3,192,512]{3,2,1,0:T(8,128)(2,1)S(1)}, bf16[1,3,192,512]{3,2,1,0:T(8,128)(2,1)S(1)}, u32[]{:S(2)}, u32[]{:S(2)}) collective-permute-start(bf16[1,3,192,512]{3,2,1,0:T(8,128)(2,1)S(1)} %get-tuple-element.599), channel_id=1, source_target_pairs={{0,8},{8,0},{16,24},{24,16},{1,9},{9,1},{17,25},{25,17},{2,10},{10... | collective-permute-start | bytes 1769480 | tf_op jit(solution)/shard_map/ppermute | solution.py:35
  625.5 73.2 %collective-permute-start.106 = (bf16[2,3,384,512]{3,2,1,0:T(8,128)(2,1)S(1)}, bf16[2,3,384,512]{3,2,1,0:T(8,128)(2,1)S(1)}, u32[]{:S(2)}, u32[]{:S(2)}) collective-permute-start(bf16[2,3,384,512]{3,2,1,0:T(8,128)(2,1)S(1)} %add_convert_fusion.part_ref), channel_id=1, source_target_pairs={{0,4},{4,0},{1,5},{5,1},{2,6},{6,2},{3,7},{7,3},{8,12},{12,8},{9,1... | collective-permute-start | bytes 7077896 | tf_op jit(solution)/shard_map/ppermute | solution.py:35
  663.9 43.8 %collective-permute-start.113 = (bf16[4,192]{1,0:T(4,128)(2,1)S(1)}, bf16[4,192]{1,0:T(4,128)(2,1)S(1)}, u32[]{:S(2)}, u32[]{:S(2)}) collective-permute-start(bf16[4,192]{1,0:T(4,128)(2,1)S(1)} %add_convert_fusion.47), channel_id=1, source_target_pairs={{0,4},{4,0},{1,5},{5,1},{2,6},{6,2},{3,7},{7,3},{8,12},{12,8},{9,1... | collective-permute-start | bytes 4616 | tf_op jit(solution)/shard_map/ppermute | solution.py:35
  (190 other events, 2273.2 us)
